TPU v7x, 32 devices: a whole 2x2x4 slice. The times are simulated.
32 devices in a mesh: region: 8 (over z, y), strip: 4 (over x, core).
Axes of the slice: x: 2, y: 2, z: 4, core: 2. Of those that a mesh axis runs over, the one named last changes fastest.
Arguments:
- features: bfloat16 [32, 64, 32, 128], P(None, 'region', 'strip'), may hold values from -28 to 28
- brick_mask: int32 [8, 4, 16], P('region', 'strip'), may hold values from 0 to 1, as said below
- conv_first: bfloat16 [3, 3, 3, 32, 32], replicated, may hold values from -0.21875 to 0.21875
- conv_second: bfloat16 [3, 3, 3, 32, 32], replicated, may hold values from -0.21875 to 0.21875
- gain_first: float32 [32], replicated, may hold values from 0.5 to 1.5
- shift_first: float32 [32], replicated, may hold values from -2 to 2
- gain_second: float32 [32], replicated, may hold values from 0.5 to 1.5
- shift_second: float32 [32], replicated, may hold values from -2 to 2
Outputs:
- block_out: bfloat16 [32, 64, 32, 128], P(None, 'region', 'strip')
Inputs may be any that keep to these rules, and one draw needn't show every extreme that they name: `brick_mask`: every device's block of 1 x 1 x 16 bricks holds at least one active brick.
All inputs are finite; a program needn't handle non-finite values.
Results may differ from a plain program's by a relative error of at most 0.0085.
Values may be sent and summed in bfloat16 or wider, within the bound.
No kernel may reach another device: no remote copies, remote signals or barrier semaphores. Data moves between devices by JAX's collectives and lax.ppermute only.
A program may use at most 64 MiB of HBM per device.

v0:
```python
import jax
import jax.numpy as jnp
from jax import lax
from jax.sharding import PartitionSpec as P

BRICK = 8


EPSILON = 1e-05


def with_halo(block, sides, width):
    for axis, dim in sides:
        count = lax.axis_size(axis)
        forward = [(i, i + 1) for i in range(count - 1)]
        backward = [(target, source) for source, target in forward]
        low = lax.ppermute(
            lax.slice_in_dim(block, block.shape[dim] - width, None, axis=dim), axis, forward
        )
        high = lax.ppermute(lax.slice_in_dim(block, 0, width, axis=dim), axis, backward)
        block = jnp.concatenate([low, block, high], axis=dim)
    return block


def expand(bricks):
    count_x, count_y, count_z = bricks.shape
    values = bricks.astype(jnp.float32)
    grown = jnp.broadcast_to(
        values[:, None, :, None, :, None], (count_x, BRICK, count_y, BRICK, count_z, BRICK)
    )
    return grown.reshape(count_x * BRICK, count_y * BRICK, count_z * BRICK)


def convolve(padded, weight, extent_x, extent_y):
    depth = padded.shape[3]
    channels = padded.shape[0]
    framed = jnp.pad(padded, ((0, 0), (0, 0), (0, 0), (1, 1)))
    flat_kernel = weight.reshape(27 * channels, weight.shape[4])
    pieces = []
    for start in range(0, extent_x, 2):
        width = min(2, extent_x - start)
        windows = []
        for step_x in range(3):
            for step_y in range(3):
                for step_z in range(3):
                    windows.append(
                        framed[
                            :,
                            start + step_x : start + step_x + width,
                            step_y : step_y + extent_y,
                            step_z : step_z + depth,
                        ]
                    )
        stacked = jnp.concatenate(windows, axis=0)
        pieces.append(
            jnp.einsum("ko,kxyz->oxyz", flat_kernel, stacked, preferred_element_type=jnp.float32)
        )
    return jnp.concatenate(pieces, axis=1)


def moments(values, voxel_mask):
    active_total, channel_sums, channel_squares = lax.psum(
        (
            jnp.sum(voxel_mask),
            jnp.sum(values * voxel_mask, axis=(1, 2, 3)),
            jnp.sum(values * values * voxel_mask, axis=(1, 2, 3)),
        ),
        ("region", "strip"),
    )
    average = channel_sums / active_total
    variance = channel_squares / active_total - average * average
    return (average, variance)


def normalize(values, average, variance, gain, shift):
    scale = lax.rsqrt(variance + EPSILON) * gain
    return (values - average[:, None, None, None]) * scale[:, None, None, None] + shift[
        :, None, None, None
    ]


def per_device(
    features,
    brick_mask,
    conv_first,
    conv_second,
    gain_first,
    shift_first,
    gain_second,
    shift_second,
):
    voxel_mask = expand(brick_mask)
    masked_input = features * voxel_mask.astype(jnp.bfloat16)
    channels, extent_x, extent_y, depth = features.shape
    padded = with_halo(masked_input, (("region", 1), ("strip", 2)), 1)
    first_out = (convolve(padded, conv_first, extent_x, extent_y) * voxel_mask).astype(jnp.bfloat16)
    first_values = first_out.astype(jnp.float32)
    average, variance = moments(first_values, voxel_mask)
    activation = (
        jax.nn.relu(normalize(first_values, average, variance, gain_first, shift_first))
        * voxel_mask
    ).astype(jnp.bfloat16)
    second_in = with_halo(activation, (("region", 1), ("strip", 2)), 1)
    second_out = (convolve(second_in, conv_second, extent_x, extent_y) * voxel_mask).astype(
        jnp.bfloat16
    )
    second_values = second_out.astype(jnp.float32)
    average, variance = moments(second_values, voxel_mask)
    result = (
        jax.nn.relu(
            normalize(second_values, average, variance, gain_second, shift_second)
            + masked_input.astype(jnp.float32)
        )
        * voxel_mask
    )
    return result.astype(jnp.bfloat16)


def solution(mesh):
    in_specs = (
        P(None, "region", "strip", None),
        P("region", "strip", None),
        P(),
        P(),
        P(),
        P(),
        P(),
        P(),
    )
    out_specs = P(None, "region", "strip", None)
    return jax.shard_map(
        per_device, mesh=mesh, in_specs=in_specs, out_specs=out_specs, check_vma=False
    )
```

profile of v0, /device:TPU:0, one launch (start us, length us, event | category | flops | bytes accessed | tf_op | source)
XLA Modules:
  0.0 147.9 jit_solution(14460607415461236595)
XLA Ops:
  0.9 1.3 copy_multiply_fusion
  2.2 4.9 %collective-permute-start = (bf16[32,1,8,128]{3,0,2,1:T(8,128)(2,1)S(1)}, bf16[32,1,8,128]{3,0,2,1:T(8,128)(2,1)S(1)}, u32[]{:S(2)}, u32[]{:S(2)}) collective-permute-start(bf16[32,1,8,128]{3,0,2,1:T(8,128)(2,1)S(1)} %get-tuple-element.54), channel_id=1, source_target_pairs={{0,4},{4,8},{8,12},{12,16},{16,20},{20,24},{24,28},{1,5},{5,9},{9,... | collective-permute-start | bytes 196616 | tf_op jit(solution)/shard_map/ppermute | solution.py:17
  7.1 1.3 collective-permute-start.1
  9.0 4.3 %collective-permute-done.1 = bf16[32,1,8,128]{3,0,2,1:T(8,128)(2,1)S(1)} collective-permute-done((bf16[32,1,8,128]{3,0,2,1:T(8,128)(2,1)S(1)}, bf16[32,1,8,128]{3,0,2,1:T(8,128)(2,1)S(1)}, u32[]{:S(2)}, u32[]{:S(2)}) %collective-permute-start.1) | collective-permute-done | bytes 65568 | tf_op jit(solution)/shard_map/ppermute | solution.py:20
  13.3 1.3 collective-permute-start.2
  14.6 1.3 collective-permute-start.3
  16.5 3.0 %collective-permute-done.3 = bf16[32,10,1,128]{3,0,2,1:T(8,128)(2,1)S(1)} collective-permute-done((bf16[32,10,1,128]{3,0,2,1:T(8,128)(2,1)S(1)}, bf16[32,10,1,128]{3,0,2,1:T(8,128)(2,1)S(1)}, u32[]{:S(2)}, u32[]{:S(2)}) %collective-permute-start.3) | collective-permute-done | bytes 81952 | tf_op jit(solution)/shard_map/ppermute | solution.py:20
  19.5 1.5 %fusion.10 = bf16[32,10,10,130]{3,0,2,1:T(8,128)(2,1)S(1)} fusion(bf16[32,10,1,128]{3,0,2,1:T(8,128)(2,1)S(1)} %collective-permute-done.3, bf16[32,10,1,128]{3,0,2,1:T(8,128)(2,1)S(1)} %collective-permute-done.2, bf16[32,1,8,128]{3,0,2,1:T(8,128)(2,1)S(1)} %collective-permute-done.1, bf16[32,8,8,128]{3,0,2,1:T(8,128)(2,1)S(1)} %copy_multiply_fusion, ...), kind=kLoop, calls=%fused_computation.14 | loop fusion | flops 7488000 | bytes 1651200 | tf_op jit(solution)/shard_map/concatenate | solution.py:21
  24.7 0.7 convolution_bitcast_fusion.7
  25.6 0.7 convolution_bitcast_fusion.6
  30.3 0.7 convolution_bitcast_fusion.4
  31.4 43.2 %all-reduce.3 = (f32[32]{0:T(128)S(1)}, f32[]{:T(128)}, f32[32]{0:T(128)S(1)}) all-reduce(f32[32]{0:T(128)S(1)} %get-tuple-element.8, f32[]{:T(128)} %broadcast_reduce_fusion, f32[32]{0:T(128)S(1)} %get-tuple-element.7), channel_id=1, replica_groups=mesh['region'=8,'strip'=4] {'region','strip'}, use_global_device_ids=true, to_apply=%region_1.2 | all-reduce | flops 65 | bytes 520 | tf_op jit(solution)/shard_map/psum | solution.py:62
  75.6 4.4 %collective-permute-start.4 = (bf16[32,1,8,128]{3,0,2,1:T(8,128)(2,1)S(1)}, bf16[32,1,8,128]{3,0,2,1:T(8,128)(2,1)S(1)}, u32[]{:S(2)}, u32[]{:S(2)}) collective-permute-start(bf16[32,1,8,128]{3,0,2,1:T(8,128)(2,1)S(1)} %get-tuple-element.52), channel_id=1, source_target_pairs={{0,4},{4,8},{8,12},{12,16},{16,20},{20,24},{24,28},{1,5},{5,9},{9,... | collective-permute-start | bytes 196616 | tf_op jit(solution)/shard_map/ppermute | solution.py:17
  80.0 1.3 collective-permute-start.5
  81.3 1.2 collective-permute-done.4
  82.5 3.7 %collective-permute-done.5 = bf16[32,1,8,128]{3,0,2,1:T(8,128)(2,1)S(1)} collective-permute-done((bf16[32,1,8,128]{3,0,2,1:T(8,128)(2,1)S(1)}, bf16[32,1,8,128]{3,0,2,1:T(8,128)(2,1)S(1)}, u32[]{:S(2)}, u32[]{:S(2)}) %collective-permute-start.5) | collective-permute-done | bytes 65568 | tf_op jit(solution)/shard_map/ppermute | solution.py:20
  86.2 1.3 collective-permute-start.6
  87.5 1.5 collective-permute-start.7
  89.0 1.9 %collective-permute-done.7 = bf16[32,10,1,128]{3,0,2,1:T(8,128)(2,1)S(1)} collective-permute-done((bf16[32,10,1,128]{3,0,2,1:T(8,128)(2,1)S(1)}, bf16[32,10,1,128]{3,0,2,1:T(8,128)(2,1)S(1)}, u32[]{:S(2)}, u32[]{:S(2)}) %collective-permute-start.7) | collective-permute-done | bytes 81952 | tf_op jit(solution)/shard_map/ppermute | solution.py:20
  90.9 1.5 %select_maximum_fusion = bf16[32,10,10,130]{3,0,2,1:T(8,128)(2,1)S(1)} fusion(bf16[32,10,1,128]{3,0,2,1:T(8,128)(2,1)S(1)} %collective-permute-done.7, bf16[32,10,1,128]{3,0,2,1:T(8,128)(2,1)S(1)} %collective-permute-done.6, bf16[32,1,8,128]{3,0,2,1:T(8,128)(2,1)S(1)} %collective-permute-done.5, bf16[32,8,8,128]{3,0,2,1:T(8,128)(2,1)S(1)} %fusion.20, ...), kind=kLoop, calls=%fused_computation.3 | loop fusion | flops 7488000 | bytes 1651200 | tf_op jit(solution)/shard_map/concatenate | solution.py:21
  97.0 0.7 convolution_bitcast_fusion.2
  101.7 0.7 convolution_bitcast_fusion
  102.8 42.9 %all-reduce.2 = (f32[32]{0:T(128)S(1)}, f32[32]{0:T(128)S(1)}) all-reduce(f32[32]{0:T(128)S(1)} %get-tuple-element.6, f32[32]{0:T(128)S(1)} %get-tuple-element.5), channel_id=1, replica_groups=mesh['region'=8,'strip'=4] {'region','strip'}, use_global_device_ids=true, to_apply=%region_7.8 | all-reduce | flops 64 | bytes 512 | tf_op jit(solution)/shard_map/psum | solution.py:62
  146.9 1.0 copy.38
  (237 shorter events, 20.2 us)
Async XLA Ops:
  0.0 24.7 %copy-start = (bf16[3,3,3,32,32]{4,3,2,1,0:T(8,128)(2,1)S(1)}, bf16[3,3,3,32,32]{4,3,2,1,0:T(8,128)(2,1)}, u32[]{:S(2)}) copy-start(bf16[3,3,3,32,32]{4,3,2,1,0:T(8,128)(2,1)} %param.10) | copy-start | bytes 165892
  2.2 6.8 %collective-permute-start = (bf16[32,1,8,128]{3,0,2,1:T(8,128)(2,1)S(1)}, bf16[32,1,8,128]{3,0,2,1:T(8,128)(2,1)S(1)}, u32[]{:S(2)}, u32[]{:S(2)}) collective-permute-start(bf16[32,1,8,128]{3,0,2,1:T(8,128)(2,1)S(1)} %get-tuple-element.54), channel_id=1, source_target_pairs={{0,4},{4,8},{8,12},{12,16},{16,20},{20,24},{24,28},{1,5},{5,9},{9,... | collective-permute-start | bytes 196616 | tf_op jit(solution)/shard_map/ppermute | solution.py:17
  7.1 6.2 %collective-permute-start.1 = (bf16[32,1,8,128]{3,0,2,1:T(8,128)(2,1)S(1)}, bf16[32,1,8,128]{3,0,2,1:T(8,128)(2,1)S(1)}, u32[]{:S(2)}, u32[]{:S(2)}) collective-permute-start(bf16[32,1,8,128]{3,0,2,1:T(8,128)(2,1)S(1)} %get-tuple-element.55), channel_id=1, source_target_pairs={{4,0},{8,4},{12,8},{16,12},{20,16},{24,20},{28,24},{5,1},{9,5},{13... | collective-permute-start | bytes 196616 | tf_op jit(solution)/shard_map/ppermute | solution.py:20
  13.3 3.2 %collective-permute-start.2 = (bf16[32,10,1,128]{3,0,2,1:T(8,128)(2,1)S(1)}, bf16[32,10,1,128]{3,0,2,1:T(8,128)(2,1)S(1)}, u32[]{:S(2)}, u32[]{:S(2)}) collective-permute-start(bf16[32,10,1,128]{3,0,2,1:T(8,128)(2,1)S(1)} %get-tuple-element.50), channel_id=1, source_target_pairs={{0,1},{1,2},{2,3},{4,5},{5,6},{6,7},{8,9},{9,10},{10,11},{12,13},{... | collective-permute-start | bytes 245768 | tf_op jit(solution)/shard_map/ppermute | solution.py:17
  14.6 4.9 %collective-permute-start.3 = (bf16[32,10,1,128]{3,0,2,1:T(8,128)(2,1)S(1)}, bf16[32,10,1,128]{3,0,2,1:T(8,128)(2,1)S(1)}, u32[]{:S(2)}, u32[]{:S(2)}) collective-permute-start(bf16[32,10,1,128]{3,0,2,1:T(8,128)(2,1)S(1)} %get-tuple-element.51), channel_id=1, source_target_pairs={{1,0},{2,1},{3,2},{5,4},{6,5},{7,6},{9,8},{10,9},{11,10},{13,12},{... | collective-permute-start | bytes 245768 | tf_op jit(solution)/shard_map/ppermute | solution.py:20
  29.9 44.7 %copy-start.5 = (f32[32]{0:T(128)S(1)}, f32[32]{0:T(128)}, u32[]{:S(2)}) copy-start(f32[32]{0:T(128)} %param.12) | copy-start | bytes 388
  29.9 45.4 %copy-start.3 = (f32[32]{0:T(128)S(1)}, f32[32]{0:T(128)}, u32[]{:S(2)}) copy-start(f32[32]{0:T(128)} %param.13) | copy-start | bytes 388
  75.6 6.9 %collective-permute-start.4 = (bf16[32,1,8,128]{3,0,2,1:T(8,128)(2,1)S(1)}, bf16[32,1,8,128]{3,0,2,1:T(8,128)(2,1)S(1)}, u32[]{:S(2)}, u32[]{:S(2)}) collective-permute-start(bf16[32,1,8,128]{3,0,2,1:T(8,128)(2,1)S(1)} %get-tuple-element.52), channel_id=1, source_target_pairs={{0,4},{4,8},{8,12},{12,16},{16,20},{20,24},{24,28},{1,5},{5,9},{9,... | collective-permute-start | bytes 196616 | tf_op jit(solution)/shard_map/ppermute | solution.py:17
  80.0 6.2 %collective-permute-start.5 = (bf16[32,1,8,128]{3,0,2,1:T(8,128)(2,1)S(1)}, bf16[32,1,8,128]{3,0,2,1:T(8,128)(2,1)S(1)}, u32[]{:S(2)}, u32[]{:S(2)}) collective-permute-start(bf16[32,1,8,128]{3,0,2,1:T(8,128)(2,1)S(1)} %get-tuple-element.53), channel_id=1, source_target_pairs={{4,0},{8,4},{12,8},{16,12},{20,16},{24,20},{28,24},{5,1},{9,5},{13... | collective-permute-start | bytes 196616 | tf_op jit(solution)/shard_map/ppermute | solution.py:20
  86.2 2.8 %collective-permute-start.6 = (bf16[32,10,1,128]{3,0,2,1:T(8,128)(2,1)S(1)}, bf16[32,10,1,128]{3,0,2,1:T(8,128)(2,1)S(1)}, u32[]{:S(2)}, u32[]{:S(2)}) collective-permute-start(bf16[32,10,1,128]{3,0,2,1:T(8,128)(2,1)S(1)} %get-tuple-element.46), channel_id=1, source_target_pairs={{0,1},{1,2},{2,3},{4,5},{5,6},{6,7},{8,9},{9,10},{10,11},{12,13},{... | collective-permute-start | bytes 245768 | tf_op jit(solution)/shard_map/ppermute | solution.py:17
  87.5 3.4 %collective-permute-start.7 = (bf16[32,10,1,128]{3,0,2,1:T(8,128)(2,1)S(1)}, bf16[32,10,1,128]{3,0,2,1:T(8,128)(2,1)S(1)}, u32[]{:S(2)}, u32[]{:S(2)}) collective-permute-start(bf16[32,10,1,128]{3,0,2,1:T(8,128)(2,1)S(1)} %get-tuple-element.47), channel_id=1, source_target_pairs={{1,0},{2,1},{3,2},{5,4},{6,5},{7,6},{9,8},{10,9},{11,10},{13,12},{... | collective-permute-start | bytes 245768 | tf_op jit(solution)/shard_map/ppermute | solution.py:20
  94.4 1.7 %copy-start.1 = (bf16[3,3,3,32,32]{4,3,2,1,0:T(8,128)(2,1)S(1)}, bf16[3,3,3,32,32]{4,3,2,1,0:T(8,128)(2,1)}, u32[]{:S(2)}) copy-start(bf16[3,3,3,32,32]{4,3,2,1,0:T(8,128)(2,1)} %param.11) | copy-start | bytes 165892
  101.3 44.4 %copy-start.6 = (f32[32]{0:T(128)S(1)}, f32[32]{0:T(128)}, u32[]{:S(2)}) copy-start(f32[32]{0:T(128)} %param.14) | copy-start | bytes 388
  101.3 45.1 %copy-start.2 = (bf16[32,8,8,128]{3,2,1,0:T(8,128)(2,1)S(1)}, bf16[32,8,8,128]{3,2,1,0:T(8,128)(2,1)}, u32[]{:S(2)}) copy-start(bf16[32,8,8,128]{3,2,1,0:T(8,128)(2,1)} %param.8) | copy-start | bytes 1572868
  101.3 45.1 %copy-start.4 = (f32[32]{0:T(128)S(1)}, f32[32]{0:T(128)}, u32[]{:S(2)}) copy-start(f32[32]{0:T(128)} %param.15) | copy-start | bytes 388
where the time goes:
time: 148 us
  blocking collectives  86.1 us (58%)
  starting transfers between devices  17.2 us (12%)
  waiting for transfers between devices  14.7 us (10%)
  local copies, waits for them, and re-layouts  13.8 us (9%)
  other arithmetic  9.02 us (6%)
  matrix products  5.88 us (4%)
    psum x2, blocking collectives, moments(): lax.psum((jnp.sum(voxel_mask), jnp.sum(values * voxel_mask, axis=(1, 2, 3...  86.1 us
    ppermute x4, waiting for transfers between devices, with_halo(): lax.ppermute(lax.slice_in_dim(block, 0, width, axis=dim), axis, backward)  12.9 us
    ppermute x4, starting transfers between devices, with_halo(): lax.ppermute(lax.slice_in_dim(block, block.shape[dim] - width, None, axis...  11.9 us
    unnamed x202, local copies, waits for them, and re-layouts  11.4 us
    dot_general x8, matrix products, convolve(): jnp.einsum('ko,kxyz->oxyz', flat_kernel, stacked, preferred_element_type=...  5.88 us
    ppermute x4, starting transfers between devices, with_halo(): lax.ppermute(lax.slice_in_dim(block, 0, width, axis=dim), axis, backward)  5.35 us
    concatenate x4, other arithmetic, with_halo(): block = jnp.concatenate([low, block, high], axis=dim)  3.33 us
  transfers between devices with their start and end apart: 8, of which 6 were waited for; matrix products, arithmetic and copies ran while one was open for 0% of the time, Pallas kernels for 0%

commit v1 on v0

--- a/solution.py
+++ b/solution.py
@@ -58,17 +58,27 @@
     return jnp.concatenate(pieces, axis=1)
 
 
+def exchange_sums(part):
+    axes = ("region", "strip")
+    count = lax.axis_size(axes)
+    copies = jnp.broadcast_to(part[None, :], (count, part.shape[0]))
+    return jnp.sum(lax.all_to_all(copies, axes, 0, 0, tiled=True), axis=0)
+
+
 def moments(values, voxel_mask):
-    active_total, channel_sums, channel_squares = lax.psum(
-        (
-            jnp.sum(voxel_mask),
+    channels = values.shape[0]
+    part = jnp.concatenate(
+        [
             jnp.sum(values * voxel_mask, axis=(1, 2, 3)),
             jnp.sum(values * values * voxel_mask, axis=(1, 2, 3)),
-        ),
-        ("region", "strip"),
+            jnp.sum(voxel_mask)[None],
+            jnp.zeros((127 - 2 * channels % 128,), jnp.float32),
+        ]
     )
-    average = channel_sums / active_total
-    variance = channel_squares / active_total - average * average
+    total = exchange_sums(part)
+    active_total = total[2 * channels]
+    average = total[:channels] / active_total
+    variance = total[channels : 2 * channels] / active_total - average * average
     return (average, variance)
 
 

time: 148 us -> 90.5 us (0.61)
  blocking collectives: 86.1 us -> 26.8 us
  starting transfers between devices: 17.2 us -> 15.3 us
  other arithmetic: 9.02 us -> 10.6 us
    psum x2 -> x0, blocking collectives: 86.1 us -> none  [moments(): lax.psum((jnp.sum(voxel_mask), jnp.sum(values * voxel_mask, axis=(1, 2, 3...]
    all_to_all x0 -> x2, blocking collectives: none -> 26.8 us  [exchange_sums(): return jnp.sum(lax.all_to_all(copies, axes, 0, 0, tiled=True), axis=0)]
    ppermute x4, starting transfers between devices: 11.9 us -> 9.94 us  [with_halo(): lax.ppermute(lax.slice_in_dim(block, block.shape[dim] - width, None, axis...]
  transfers between devices with their start and end apart: 8 -> 8, of which waited for: 6 -> 6; matrix products, arithmetic and copies ran while one was open for 0% -> 1% of each run, Pallas kernels for 0% -> 0%
where the time goes in v1:
time: 90.5 us; the launch traced here: 90.1 us
  blocking collectives  26.8 us (30%)
  starting transfers between devices  15.3 us (17%)
  waiting for transfers between devices  15.2 us (17%)
  local copies, waits for them, and re-layouts  15 us (17%)
  other arithmetic  10.6 us (12%)
  matrix products  5.88 us (6%)
  between operations  1.18 us (1%)
    all_to_all x2, blocking collectives, exchange_sums(): return jnp.sum(lax.all_to_all(copies, axes, 0, 0, tiled=True), axis=0)  26.8 us
    ppermute x4, waiting for transfers between devices, with_halo(): lax.ppermute(lax.slice_in_dim(block, 0, width, axis=dim), axis, backward)  14.1 us
    unnamed x202, local copies, waits for them, and re-layouts  11.4 us
    ppermute x4, starting transfers between devices, with_halo(): lax.ppermute(lax.slice_in_dim(block, block.shape[dim] - width, None, axis...  9.94 us
    dot_general x8, matrix products, convolve(): jnp.einsum('ko,kxyz->oxyz', flat_kernel, stacked, preferred_element_type=...  5.88 us
    ppermute x4, starting transfers between devices, with_halo(): lax.ppermute(lax.slice_in_dim(block, 0, width, axis=dim), axis, backward)  5.35 us
    concatenate x4, other arithmetic, with_halo(): block = jnp.concatenate([low, block, high], axis=dim)  3.33 us
  transfers between devices with their start and end apart: 8, of which 6 were waited for; matrix products, arithmetic and copies ran while one was open for 1% of the time, Pallas kernels for 0%

profile of v1, /device:TPU:0, one launch (start us, length us, event | category | flops | bytes accessed | tf_op | source)
XLA Modules:
  0.0 90.1 jit_solution(17314830056297904978)
XLA Ops:
  0.9 1.3 %copy_multiply_fusion = bf16[32,8,8,128]{3,0,2,1:T(8,128)(2,1)S(1)} fusion(bf16[32,8,8,128]{3,2,1,0:T(8,128)(2,1)} %param.8, bf16[128]{0:T(256)(128)(2,1)S(1)} %convert_element_type.33), kind=kLoop, calls=%fused_computation.58 | loop fusion | flops 262144 | bytes 1048832 | tf_op jit(solution)/shard_map/mul | solution.py:103
  2.2 4.9 %collective-permute-start = (bf16[32,1,8,128]{3,0,2,1:T(8,128)(2,1)S(1)}, bf16[32,1,8,128]{3,0,2,1:T(8,128)(2,1)S(1)}, u32[]{:S(2)}, u32[]{:S(2)}) collective-permute-start(bf16[32,1,8,128]{3,0,2,1:T(8,128)(2,1)S(1)} %get-tuple-element.49), channel_id=1, source_target_pairs={{0,4},{4,8},{8,12},{12,16},{16,20},{20,24},{24,28},{1,5},{5,9},{9,... | collective-permute-start | bytes 196616 | tf_op jit(solution)/shard_map/ppermute | solution.py:17
  7.1 1.3 %collective-permute-start.1 = (bf16[32,1,8,128]{3,0,2,1:T(8,128)(2,1)S(1)}, bf16[32,1,8,128]{3,0,2,1:T(8,128)(2,1)S(1)}, u32[]{:S(2)}, u32[]{:S(2)}) collective-permute-start(bf16[32,1,8,128]{3,0,2,1:T(8,128)(2,1)S(1)} %get-tuple-element.50), channel_id=1, source_target_pairs={{4,0},{8,4},{12,8},{16,12},{20,16},{24,20},{28,24},{5,1},{9,5},{13... | collective-permute-start | bytes 196616 | tf_op jit(solution)/shard_map/ppermute | solution.py:20
  9.0 4.3 %collective-permute-done.1 = bf16[32,1,8,128]{3,0,2,1:T(8,128)(2,1)S(1)} collective-permute-done((bf16[32,1,8,128]{3,0,2,1:T(8,128)(2,1)S(1)}, bf16[32,1,8,128]{3,0,2,1:T(8,128)(2,1)S(1)}, u32[]{:S(2)}, u32[]{:S(2)}) %collective-permute-start.1) | collective-permute-done | bytes 65568 | tf_op jit(solution)/shard_map/ppermute | solution.py:20
  13.3 1.3 %collective-permute-start.2 = (bf16[32,10,1,128]{3,0,2,1:T(8,128)(2,1)S(1)}, bf16[32,10,1,128]{3,0,2,1:T(8,128)(2,1)S(1)}, u32[]{:S(2)}, u32[]{:S(2)}) collective-permute-start(bf16[32,10,1,128]{3,0,2,1:T(8,128)(2,1)S(1)} %get-tuple-element.45), channel_id=1, source_target_pairs={{0,1},{1,2},{2,3},{4,5},{5,6},{6,7},{8,9},{9,10},{10,11},{12,13},{... | collective-permute-start | bytes 245768 | tf_op jit(solution)/shard_map/ppermute | solution.py:17
  14.6 1.3 %collective-permute-start.3 = (bf16[32,10,1,128]{3,0,2,1:T(8,128)(2,1)S(1)}, bf16[32,10,1,128]{3,0,2,1:T(8,128)(2,1)S(1)}, u32[]{:S(2)}, u32[]{:S(2)}) collective-permute-start(bf16[32,10,1,128]{3,0,2,1:T(8,128)(2,1)S(1)} %get-tuple-element.46), channel_id=1, source_target_pairs={{1,0},{2,1},{3,2},{5,4},{6,5},{7,6},{9,8},{10,9},{11,10},{13,12},{... | collective-permute-start | bytes 245768 | tf_op jit(solution)/shard_map/ppermute | solution.py:20
  16.5 3.0 %collective-permute-done.3 = bf16[32,10,1,128]{3,0,2,1:T(8,128)(2,1)S(1)} collective-permute-done((bf16[32,10,1,128]{3,0,2,1:T(8,128)(2,1)S(1)}, bf16[32,10,1,128]{3,0,2,1:T(8,128)(2,1)S(1)}, u32[]{:S(2)}, u32[]{:S(2)}) %collective-permute-start.3) | collective-permute-done | bytes 81952 | tf_op jit(solution)/shard_map/ppermute | solution.py:20
  19.5 1.5 %fusion.10 = bf16[32,10,10,130]{3,0,2,1:T(8,128)(2,1)S(1)} fusion(bf16[32,10,1,128]{3,0,2,1:T(8,128)(2,1)S(1)} %collective-permute-done.3, bf16[32,10,1,128]{3,0,2,1:T(8,128)(2,1)S(1)} %collective-permute-done.2, bf16[32,1,8,128]{3,0,2,1:T(8,128)(2,1)S(1)} %collective-permute-done.1, bf16[32,8,8,128]{3,0,2,1:T(8,128)(2,1)S(1)} %copy_multiply_fusion, ...), kind=kLoop, calls=%fused_computation.14 | loop fusion | flops 7488000 | bytes 1651200 | tf_op jit(solution)/shard_map/concatenate | solution.py:21
  24.7 0.7 convolution_bitcast_fusion.7
  25.6 0.7 convolution_bitcast_fusion.6
  28.0 0.7 convolution_bitcast_fusion.5
  30.3 0.7 convolution_bitcast_fusion.4
  32.1 14.5 %all_to_all.12 = f32[32,1,128]{2,1,0:T(1,128)S(1)} all-to-all(f32[32,1,128]{2,1,0:T(1,128)S(1)} %broadcast_in_dim.19), channel_id=1, replica_groups=mesh['region'=8,'strip'=4] {'region','strip'}, dimensions={0} | all-to-all | bytes 32768 | tf_op jit(solution)/shard_map/all_to_all | solution.py:65
  48.3 2.5 %collective-permute-start.4 = (bf16[32,1,8,128]{3,0,2,1:T(8,128)(2,1)S(1)}, bf16[32,1,8,128]{3,0,2,1:T(8,128)(2,1)S(1)}, u32[]{:S(2)}, u32[]{:S(2)}) collective-permute-start(bf16[32,1,8,128]{3,0,2,1:T(8,128)(2,1)S(1)} %get-tuple-element.47), channel_id=1, source_target_pairs={{0,4},{4,8},{8,12},{12,16},{16,20},{20,24},{24,28},{1,5},{5,9},{9,... | collective-permute-start | bytes 196616 | tf_op jit(solution)/shard_map/ppermute | solution.py:17
  50.8 1.3 %collective-permute-start.5 = (bf16[32,1,8,128]{3,0,2,1:T(8,128)(2,1)S(1)}, bf16[32,1,8,128]{3,0,2,1:T(8,128)(2,1)S(1)}, u32[]{:S(2)}, u32[]{:S(2)}) collective-permute-start(bf16[32,1,8,128]{3,0,2,1:T(8,128)(2,1)S(1)} %get-tuple-element.48), channel_id=1, source_target_pairs={{4,0},{8,4},{12,8},{16,12},{20,16},{24,20},{28,24},{5,1},{9,5},{13... | collective-permute-start | bytes 196616 | tf_op jit(solution)/shard_map/ppermute | solution.py:20
  52.7 4.3 %collective-permute-done.5 = bf16[32,1,8,128]{3,0,2,1:T(8,128)(2,1)S(1)} collective-permute-done((bf16[32,1,8,128]{3,0,2,1:T(8,128)(2,1)S(1)}, bf16[32,1,8,128]{3,0,2,1:T(8,128)(2,1)S(1)}, u32[]{:S(2)}, u32[]{:S(2)}) %collective-permute-start.5) | collective-permute-done | bytes 65568 | tf_op jit(solution)/shard_map/ppermute | solution.py:20
  57.0 1.3 %collective-permute-start.6 = (bf16[32,10,1,128]{3,0,2,1:T(8,128)(2,1)S(1)}, bf16[32,10,1,128]{3,0,2,1:T(8,128)(2,1)S(1)}, u32[]{:S(2)}, u32[]{:S(2)}) collective-permute-start(bf16[32,10,1,128]{3,0,2,1:T(8,128)(2,1)S(1)} %get-tuple-element.41), channel_id=1, source_target_pairs={{0,1},{1,2},{2,3},{4,5},{5,6},{6,7},{8,9},{9,10},{10,11},{12,13},{... | collective-permute-start | bytes 245768 | tf_op jit(solution)/shard_map/ppermute | solution.py:17
  58.3 1.5 %collective-permute-start.7 = (bf16[32,10,1,128]{3,0,2,1:T(8,128)(2,1)S(1)}, bf16[32,10,1,128]{3,0,2,1:T(8,128)(2,1)S(1)}, u32[]{:S(2)}, u32[]{:S(2)}) collective-permute-start(bf16[32,10,1,128]{3,0,2,1:T(8,128)(2,1)S(1)} %get-tuple-element.42), channel_id=1, source_target_pairs={{1,0},{2,1},{3,2},{5,4},{6,5},{7,6},{9,8},{10,9},{11,10},{13,12},{... | collective-permute-start | bytes 245768 | tf_op jit(solution)/shard_map/ppermute | solution.py:20
  59.8 2.5 %collective-permute-done.7 = bf16[32,10,1,128]{3,0,2,1:T(8,128)(2,1)S(1)} collective-permute-done((bf16[32,10,1,128]{3,0,2,1:T(8,128)(2,1)S(1)}, bf16[32,10,1,128]{3,0,2,1:T(8,128)(2,1)S(1)}, u32[]{:S(2)}, u32[]{:S(2)}) %collective-permute-start.7) | collective-permute-done | bytes 81952 | tf_op jit(solution)/shard_map/ppermute | solution.py:20
  62.3 1.5 %select_maximum_fusion = bf16[32,10,10,130]{3,0,2,1:T(8,128)(2,1)S(1)} fusion(bf16[32,10,1,128]{3,0,2,1:T(8,128)(2,1)S(1)} %collective-permute-done.7, bf16[32,10,1,128]{3,0,2,1:T(8,128)(2,1)S(1)} %collective-permute-done.6, bf16[32,1,8,128]{3,0,2,1:T(8,128)(2,1)S(1)} %collective-permute-done.5, bf16[32,8,8,128]{3,0,2,1:T(8,128)(2,1)S(1)} %fusion.22, ...), kind=kLoop, calls=%fused_computation.3 | loop fusion | flops 7488000 | bytes 1651200 | tf_op jit(solution)/shard_map/concatenate | solution.py:21
  68.4 0.7 convolution_bitcast_fusion.2
  73.0 0.7 convolution_bitcast_fusion
  74.9 12.4 %all_to_all.13 = f32[32,1,128]{2,1,0:T(1,128)S(1)} all-to-all(f32[32,1,128]{2,1,0:T(1,128)S(1)} %broadcast_in_dim.20), channel_id=1, replica_groups=mesh['region'=8,'strip'=4] {'region','strip'}, dimensions={0} | all-to-all | bytes 32768 | tf_op jit(solution)/shard_map/all_to_all | solution.py:65
  89.1 1.0 %copy.50 = bf16[32,8,8,128]{3,2,1,0:T(8,128)(2,1)} copy(bf16[32,8,8,128]{3,0,2,1:T(8,128)(2,1)S(1)} %fusion.31) | data formatting | bytes 1048576 | tf_op jit(solution)/shard_map/convert_element_type | solution.py:126
  (246 shorter events, 22.9 us)
Async XLA Ops:
  0.0 24.7 %copy-start = (bf16[3,3,3,32,32]{4,3,2,1,0:T(8,128)(2,1)S(1)}, bf16[3,3,3,32,32]{4,3,2,1,0:T(8,128)(2,1)}, u32[]{:S(2)}) copy-start(bf16[3,3,3,32,32]{4,3,2,1,0:T(8,128)(2,1)} %param.10) | copy-start | bytes 165892
  2.2 6.8 %collective-permute-start = (bf16[32,1,8,128]{3,0,2,1:T(8,128)(2,1)S(1)}, bf16[32,1,8,128]{3,0,2,1:T(8,128)(2,1)S(1)}, u32[]{:S(2)}, u32[]{:S(2)}) collective-permute-start(bf16[32,1,8,128]{3,0,2,1:T(8,128)(2,1)S(1)} %get-tuple-element.49), channel_id=1, source_target_pairs={{0,4},{4,8},{8,12},{12,16},{16,20},{20,24},{24,28},{1,5},{5,9},{9,... | collective-permute-start | bytes 196616 | tf_op jit(solution)/shard_map/ppermute | solution.py:17
  7.1 6.2 %collective-permute-start.1 = (bf16[32,1,8,128]{3,0,2,1:T(8,128)(2,1)S(1)}, bf16[32,1,8,128]{3,0,2,1:T(8,128)(2,1)S(1)}, u32[]{:S(2)}, u32[]{:S(2)}) collective-permute-start(bf16[32,1,8,128]{3,0,2,1:T(8,128)(2,1)S(1)} %get-tuple-element.50), channel_id=1, source_target_pairs={{4,0},{8,4},{12,8},{16,12},{20,16},{24,20},{28,24},{5,1},{9,5},{13... | collective-permute-start | bytes 196616 | tf_op jit(solution)/shard_map/ppermute | solution.py:20
  13.3 3.2 %collective-permute-start.2 = (bf16[32,10,1,128]{3,0,2,1:T(8,128)(2,1)S(1)}, bf16[32,10,1,128]{3,0,2,1:T(8,128)(2,1)S(1)}, u32[]{:S(2)}, u32[]{:S(2)}) collective-permute-start(bf16[32,10,1,128]{3,0,2,1:T(8,128)(2,1)S(1)} %get-tuple-element.45), channel_id=1, source_target_pairs={{0,1},{1,2},{2,3},{4,5},{5,6},{6,7},{8,9},{9,10},{10,11},{12,13},{... | collective-permute-start | bytes 245768 | tf_op jit(solution)/shard_map/ppermute | solution.py:17
  14.6 4.9 %collective-permute-start.3 = (bf16[32,10,1,128]{3,0,2,1:T(8,128)(2,1)S(1)}, bf16[32,10,1,128]{3,0,2,1:T(8,128)(2,1)S(1)}, u32[]{:S(2)}, u32[]{:S(2)}) collective-permute-start(bf16[32,10,1,128]{3,0,2,1:T(8,128)(2,1)S(1)} %get-tuple-element.46), channel_id=1, source_target_pairs={{1,0},{2,1},{3,2},{5,4},{6,5},{7,6},{9,8},{10,9},{11,10},{13,12},{... | collective-permute-start | bytes 245768 | tf_op jit(solution)/shard_map/ppermute | solution.py:20
  29.9 17.3 %copy-start.5 = (f32[32]{0:T(128)S(1)}, f32[32]{0:T(128)}, u32[]{:S(2)}) copy-start(f32[32]{0:T(128)} %param.12) | copy-start | bytes 388
  29.9 18.0 %copy-start.3 = (f32[32]{0:T(128)S(1)}, f32[32]{0:T(128)}, u32[]{:S(2)}) copy-start(f32[32]{0:T(128)} %param.13) | copy-start | bytes 388
  48.3 4.3 %collective-permute-start.4 = (bf16[32,1,8,128]{3,0,2,1:T(8,128)(2,1)S(1)}, bf16[32,1,8,128]{3,0,2,1:T(8,128)(2,1)S(1)}, u32[]{:S(2)}, u32[]{:S(2)}) collective-permute-start(bf16[32,1,8,128]{3,0,2,1:T(8,128)(2,1)S(1)} %get-tuple-element.47), channel_id=1, source_target_pairs={{0,4},{4,8},{8,12},{12,16},{16,20},{20,24},{24,28},{1,5},{5,9},{9,... | collective-permute-start | bytes 196616 | tf_op jit(solution)/shard_map/ppermute | solution.py:17
  50.8 6.2 %collective-permute-start.5 = (bf16[32,1,8,128]{3,0,2,1:T(8,128)(2,1)S(1)}, bf16[32,1,8,128]{3,0,2,1:T(8,128)(2,1)S(1)}, u32[]{:S(2)}, u32[]{:S(2)}) collective-permute-start(bf16[32,1,8,128]{3,0,2,1:T(8,128)(2,1)S(1)} %get-tuple-element.48), channel_id=1, source_target_pairs={{4,0},{8,4},{12,8},{16,12},{20,16},{24,20},{28,24},{5,1},{9,5},{13... | collective-permute-start | bytes 196616 | tf_op jit(solution)/shard_map/ppermute | solution.py:20
  57.0 2.8 %collective-permute-start.6 = (bf16[32,10,1,128]{3,0,2,1:T(8,128)(2,1)S(1)}, bf16[32,10,1,128]{3,0,2,1:T(8,128)(2,1)S(1)}, u32[]{:S(2)}, u32[]{:S(2)}) collective-permute-start(bf16[32,10,1,128]{3,0,2,1:T(8,128)(2,1)S(1)} %get-tuple-element.41), channel_id=1, source_target_pairs={{0,1},{1,2},{2,3},{4,5},{5,6},{6,7},{8,9},{9,10},{10,11},{12,13},{... | collective-permute-start | bytes 245768 | tf_op jit(solution)/shard_map/ppermute | solution.py:17
  58.3 4.0 %collective-permute-start.7 = (bf16[32,10,1,128]{3,0,2,1:T(8,128)(2,1)S(1)}, bf16[32,10,1,128]{3,0,2,1:T(8,128)(2,1)S(1)}, u32[]{:S(2)}, u32[]{:S(2)}) collective-permute-start(bf16[32,10,1,128]{3,0,2,1:T(8,128)(2,1)S(1)} %get-tuple-element.42), channel_id=1, source_target_pairs={{1,0},{2,1},{3,2},{5,4},{6,5},{7,6},{9,8},{10,9},{11,10},{13,12},{... | collective-permute-start | bytes 245768 | tf_op jit(solution)/shard_map/ppermute | solution.py:20
  65.8 1.7 %copy-start.1 = (bf16[3,3,3,32,32]{4,3,2,1,0:T(8,128)(2,1)S(1)}, bf16[3,3,3,32,32]{4,3,2,1,0:T(8,128)(2,1)}, u32[]{:S(2)}) copy-start(bf16[3,3,3,32,32]{4,3,2,1,0:T(8,128)(2,1)} %param.11) | copy-start | bytes 165892
  72.7 15.2 %copy-start.6 = (f32[32]{0:T(128)S(1)}, f32[32]{0:T(128)}, u32[]{:S(2)}) copy-start(f32[32]{0:T(128)} %param.14) | copy-start | bytes 388
  72.7 15.9 %copy-start.2 = (bf16[32,8,8,128]{3,2,1,0:T(8,128)(2,1)S(1)}, bf16[32,8,8,128]{3,2,1,0:T(8,128)(2,1)}, u32[]{:S(2)}) copy-start(bf16[32,8,8,128]{3,2,1,0:T(8,128)(2,1)} %param.8) | copy-start | bytes 1572868
  72.7 15.9 %copy-start.4 = (f32[32]{0:T(128)S(1)}, f32[32]{0:T(128)}, u32[]{:S(2)}) copy-start(f32[32]{0:T(128)} %param.15) | copy-start | bytes 388

commit v2 on v0

v2 whole, which is shorter than its diff:
```python
import functools

import jax
import jax.numpy as jnp
from jax import lax
from jax.experimental import pallas as pl
from jax.experimental.pallas import tpu as pltpu
from jax.sharding import PartitionSpec as P

BRICK = 8
EPSILON = 1e-05
HALO = 2
AXES = ("region", "strip")
F32 = jnp.float32
BF16 = jnp.bfloat16


def even_pairs(count):
    return [(i, i ^ 1) for i in range(count) if (i ^ 1) < count]


def odd_pairs(count):
    pairs = [(i, i + 1) for i in range(1, count - 1, 2)]
    return pairs + [(b, a) for a, b in pairs]


def swap(even, odd, axis):
    count = lax.axis_size(axis)
    return lax.ppermute(even, axis, even_pairs(count)), lax.ppermute(odd, axis, odd_pairs(count))


def whole(*_):
    return pl.BlockSpec(memory_space=pltpu.VMEM)


def call(body, outs, ins, scratch=(), flops=0, smem=0):
    in_specs = [pl.BlockSpec(memory_space=pltpu.SMEM)] * smem + [whole()] * (len(ins) - smem)
    return pl.pallas_call(
        body,
        out_shape=outs,
        in_specs=in_specs,
        out_specs=jax.tree.map(whole, outs),
        scratch_shapes=list(scratch),
        cost_estimate=pl.CostEstimate(
            flops=flops,
            transcendentals=0,
            bytes_accessed=sum(a.size * a.dtype.itemsize for a in ins),
        ),
    )(*ins)


def brick_rows(bricks, depth):
    count = bricks.shape[1]
    at = lax.broadcasted_iota(jnp.int32, (count, depth), 0)
    voxel = lax.broadcasted_iota(jnp.int32, (count, depth), 1)
    spread = (voxel // BRICK == at).astype(F32)
    return jnp.dot(bricks, spread, preferred_element_type=F32, precision=lax.Precision.HIGHEST)


def gather_kernel(dims, place, features, bricks, own, masks, even, odd, turned):
    channels, extent_x, extent_y, depth, bx, by = dims
    rows = brick_rows(bricks[...].astype(F32), depth)
    for i in range(bx * by):
        masks[i] = jnp.broadcast_to(rows[i : i + 1], (16, depth))
    for x in range(extent_x):
        for j in range(by):
            part = features[:, x, j * BRICK : (j + 1) * BRICK, :].astype(F32)
            part = part * masks[x // BRICK * by + j][None, :BRICK, :]
            turned[...] = part.reshape(channels * BRICK, depth)
            for y in range(BRICK):
                own[x, j * BRICK + y] = turned[pl.ds(y, channels, stride=BRICK), :].astype(BF16)
    first = place[0] == 0
    for out, low in ((even, jnp.where(first, 0, 1)), (odd, jnp.where(first, 1, 0))):
        start = jnp.where(low == 1, 0, extent_x - HALO)
        for i in range(HALO):
            for y in range(extent_y):
                at = (i * extent_y + y) * channels
                out[at : at + channels, :] = own[start + i, y]
        base = HALO * extent_y * channels
        for j in range(by):
            tile = masks[jnp.where(low == 1, 0, bx - 1) * by + j]
            out[base + 16 * j : base + 16 * (j + 1), :] = tile.astype(BF16)


def corner_kernel(dims, place, own, masks, from_even, from_odd, even, odd):
    channels, extent_x, extent_y, depth, bx, by = dims
    first_x = place[0] == 0
    first_y = place[1] == 0
    wide = extent_x + 2 * HALO
    base = HALO * extent_y * channels
    for out, low in ((even, jnp.where(first_y, 0, 1)), (odd, jnp.where(first_y, 1, 0))):
        start = jnp.where(low == 1, 0, extent_y - HALO)
        brick = jnp.where(low == 1, 0, by - 1)

        def put(x, j, value):
            at = (x * HALO + j) * channels
            out[at : at + channels, :] = value

        def put_mask(x, value):
            at = wide * HALO * channels + 16 * x
            out[at : at + 16, :] = value

        for x in range(extent_x):
            for j in range(HALO):
                put(HALO + x, j, own[x, start + j])
        for x in range(bx):
            put_mask(1 + x, masks[x * by + brick].astype(BF16))
        for i in range(HALO):
            for j in range(HALO):
                at = pl.multiple_of((i * extent_y + start + j) * channels, channels)
                a = from_even[pl.ds(at, channels), :]
                b = from_odd[pl.ds(at, channels), :]
                put(i, j, jnp.where(first_x, b, a))
                put(HALO + extent_x + i, j, jnp.where(first_x, a, b))
        at = pl.multiple_of(base + brick * 16, 16)
        a = from_even[pl.ds(at, 16), :]
        b = from_odd[pl.ds(at, 16), :]
        put_mask(0, jnp.where(first_x, b, a))
        put_mask(1 + bx, jnp.where(first_x, a, b))


def put_shifted(field, x, y, value):
    channels, depth = value.shape
    lane = lax.broadcasted_iota(jnp.int32, value.shape, 1)
    before = jnp.where(lane == 0, 0.0, pltpu.roll(value, 1, 1))
    after = jnp.where(lane == depth - 1, 0.0, pltpu.roll(value, depth - 1, 1))
    for k, part in enumerate((before, value, after)):
        at = (3 * y + k) * channels
        field[at : at + channels, x * depth : (x + 1) * depth] = part.astype(BF16)


def send_stats(out, channels, sums, squares, counts):
    depth = sums.shape[1]
    rest = jnp.zeros((128 - 2 * channels - counts.shape[0], depth), F32)
    table = jnp.concatenate([sums, squares, counts, rest], axis=0)
    row = jnp.sum(jnp.transpose(table), axis=0, keepdims=True)
    out[...] = jnp.broadcast_to(row, out.shape)


def affine(stats, gain, channels, depth):
    row = jnp.sum(stats[...], axis=0, keepdims=True)
    table = jnp.transpose(jnp.broadcast_to(row, (128, 128)))
    total = jnp.sum(table[2 * channels : 2 * channels + BRICK], axis=0, keepdims=True)
    average = table[:channels] / total
    variance = table[channels : 2 * channels] / total - average * average
    return average, lax.rsqrt(variance + EPSILON) * gain


def first_kernel(
    dims, place, own, masks, x_even, x_odd, y_even, y_odd, band, first_out, wide_masks, stats, field
):
    channels, extent_x, extent_y, depth, bx, by = dims
    first_x = place[0] == 0
    first_y = place[1] == 0
    wide_x = extent_x + 2 * HALO
    for x in range(extent_x):
        for y in range(extent_y):
            put_shifted(field, HALO + x, HALO + y, own[x, y].astype(F32))
    for i in range(HALO):
        for y in range(extent_y):
            at = (i * extent_y + y) * channels
            a = x_even[at : at + channels, :].astype(F32)
            b = x_odd[at : at + channels, :].astype(F32)
            put_shifted(field, i, HALO + y, jnp.where(first_x, b, a))
            put_shifted(field, HALO + extent_x + i, HALO + y, jnp.where(first_x, a, b))
    for x in range(wide_x):
        for j in range(HALO):
            at = (x * HALO + j) * channels
            a = y_even[at : at + channels, :].astype(F32)
            b = y_odd[at : at + channels, :].astype(F32)
            put_shifted(field, x, j, jnp.where(first_y, b, a))
            put_shifted(field, x, HALO + extent_y + j, jnp.where(first_y, a, b))
    for i in range(bx):
        for j in range(by):
            wide_masks[1 + i, 1 + j] = masks[i * by + j][:BRICK]
    base = HALO * extent_y * channels
    for j in range(by):
        a = x_even[base + 16 * j : base + 16 * (j + 1), :].astype(F32)[:BRICK]
        b = x_odd[base + 16 * j : base + 16 * (j + 1), :].astype(F32)[:BRICK]
        wide_masks[0, 1 + j] = jnp.where(first_x, b, a)
        wide_masks[1 + bx, 1 + j] = jnp.where(first_x, a, b)
    base = wide_x * HALO * channels
    for i in range(bx + 2):
        a = y_even[base + 16 * i : base + 16 * (i + 1), :].astype(F32)[:BRICK]
        b = y_odd[base + 16 * i : base + 16 * (i + 1), :].astype(F32)[:BRICK]
        wide_masks[i, 0] = jnp.where(first_y, b, a)
        wide_masks[i, 1 + by] = jnp.where(first_y, a, b)

    sums = jnp.zeros((channels, depth), F32)
    squares = jnp.zeros((channels, depth), F32)
    ring = 1
    block = band.shape[1] // channels
    reach = band.shape[2]
    for x in range(0, extent_x + 2 * ring, 2):
        for start in range(0, extent_y + 2 * ring, block):
            total = jnp.zeros((block * channels, 2 * depth), F32)
            for step in range(3):
                window = field[
                    start * 3 * channels : start * 3 * channels + reach,
                    (x + step) * depth : (x + step + 2) * depth,
                ]
                total = total + jnp.dot(band[step], window, preferred_element_type=F32)
            for i in range(2):
                for j in range(block):
                    at_x, at_y = x + i - ring, start + j - ring
                    mask = wide_masks[at_x // BRICK + 1, at_y // BRICK + 1][:1]
                    part = total[j * channels : (j + 1) * channels, i * depth : (i + 1) * depth]
                    value = (part * mask).astype(BF16)
                    first_out[
                        (start + j) * channels : (start + j + 1) * channels,
                        (x + i) * depth : (x + i + 1) * depth,
                    ] = value
                    if 0 <= at_x < extent_x and 0 <= at_y < extent_y:
                        value = value.astype(F32)
                        sums = sums + value
                        squares = squares + value * value
    count_mask(stats, channels, sums, squares, wide_masks, dims)


def count_mask(stats, channels, sums, squares, wide_masks, dims):
    bx, by = dims[4:]
    counts = jnp.zeros(wide_masks.shape[2:], F32)
    for i in range(bx):
        for j in range(by):
            counts = counts + wide_masks[1 + i, 1 + j] * float(BRICK)
    send_stats(stats, channels, sums, squares, counts)


def second_kernel(dims, first_out, wide_masks, received, params, band, second_out, stats, field):
    channels, extent_x, extent_y, depth, bx, by = dims
    average, scale = affine(received, params[0], channels, depth)
    shift = params[1]
    for x in range(extent_x + 2):
        for y in range(extent_y + 2):
            part = first_out[
                y * channels : (y + 1) * channels, x * depth : (x + 1) * depth
            ].astype(F32)
            mask = wide_masks[(x - 1) // BRICK + 1, (y - 1) // BRICK + 1][:1]
            part = jnp.maximum((part - average) * scale + shift, 0.0) * mask
            put_shifted(field, x, y, part)
    sums = jnp.zeros((channels, depth), F32)
    squares = jnp.zeros((channels, depth), F32)
    block = band.shape[1] // channels
    reach = band.shape[2]
    for x in range(0, extent_x, 2):
        for start in range(0, extent_y, block):
            total = jnp.zeros((block * channels, 2 * depth), F32)
            for step in range(3):
                window = field[
                    start * 3 * channels : start * 3 * channels + reach,
                    (x + step) * depth : (x + step + 2) * depth,
                ]
                total = total + jnp.dot(band[step], window, preferred_element_type=F32)
            for i in range(2):
                for j in range(block):
                    mask = wide_masks[(x + i) // BRICK + 1, (start + j) // BRICK + 1][:1]
                    part = total[j * channels : (j + 1) * channels, i * depth : (i + 1) * depth]
                    value = (part * mask).astype(BF16)
                    second_out[
                        (start + j) * channels : (start + j + 1) * channels,
                        (x + i) * depth : (x + i + 1) * depth,
                    ] = value
                    value = value.astype(F32)
                    sums = sums + value
                    squares = squares + value * value
    count_mask(stats, channels, sums, squares, wide_masks, dims)


def last_kernel(dims, second_out, wide_masks, received, params, own, result, turned):
    channels, extent_x, extent_y, depth, bx, by = dims
    average, scale = affine(received, params[2], channels, depth)
    shift = params[3]
    for x in range(extent_x):
        for j in range(by):
            mask = wide_masks[x // BRICK + 1, j + 1][:1]
            for y in range(BRICK):
                at = j * BRICK + y
                part = second_out[
                    at * channels : (at + 1) * channels, x * depth : (x + 1) * depth
                ].astype(F32)
                part = (part - average) * scale + shift + own[x, at].astype(F32)
                turned[pl.ds(y, channels, stride=BRICK), :] = jnp.maximum(part, 0.0) * mask
            result[:, x, j * BRICK : (j + 1) * BRICK, :] = (
                turned[...].reshape(channels, BRICK, depth).astype(BF16)
            )


def band_of(weight, block):
    fan_in, fan_out = weight.shape[3:]
    tall = weight.reshape(3, 9 * fan_in, fan_out).transpose(0, 2, 1)
    step = 3 * fan_in
    parts = [
        jnp.pad(tall, ((0, 0), (0, 0), (y * step, (block - 1 - y) * step))) for y in range(block)
    ]
    return jnp.concatenate(parts, axis=1)


def per_device(
    features,
    brick_mask,
    conv_first,
    conv_second,
    gain_first,
    shift_first,
    gain_second,
    shift_second,
):
    channels, extent_x, extent_y, depth = features.shape
    bx, by, bz = brick_mask.shape
    dims = (channels, extent_x, extent_y, depth, bx, by)
    devices = lax.axis_size(AXES)
    place = jnp.stack([lax.axis_index("region") % 2, lax.axis_index("strip") % 2]).astype(jnp.int32)
    wide_x = extent_x + 2 * HALO
    shape = jax.ShapeDtypeStruct

    x_rows = HALO * extent_y * channels + 16 * by
    own, masks, even, odd = call(
        functools.partial(gather_kernel, dims),
        (
            shape((extent_x, extent_y, channels, depth), BF16),
            shape((bx * by, 16, depth), F32),
            shape((x_rows, depth), BF16),
            shape((x_rows, depth), BF16),
        ),
        (place, features, brick_mask.reshape(bx * by, bz)),
        scratch=[pltpu.VMEM((channels * BRICK, depth), F32)],
        smem=1,
    )
    x_even, x_odd = swap(even, odd, "region")
    y_rows = wide_x * HALO * channels + 16 * (bx + 2)
    even, odd = call(
        functools.partial(corner_kernel, dims),
        (shape((y_rows, depth), BF16), shape((y_rows, depth), BF16)),
        (place, own, masks, x_even, x_odd),
        smem=1,
    )
    y_even, y_odd = swap(even, odd, "strip")

    first_band = band_of(conv_first, (extent_y + 2) // 2)
    second_band = band_of(conv_second, extent_y // 2)
    params = jnp.broadcast_to(
        jnp.stack([gain_first, shift_first, gain_second, shift_second])[:, :, None],
        (4, channels, depth),
    )
    first_out, wide_masks, sent = call(
        functools.partial(first_kernel, dims),
        (
            shape(((extent_y + 2) * channels, (extent_x + 2) * depth), BF16),
            shape((bx + 2, by + 2, BRICK, depth), F32),
            shape((devices, 128), F32),
        ),
        (place, own, masks, x_even, x_odd, y_even, y_odd, first_band),
        scratch=[pltpu.VMEM(((extent_y + 4) * 3 * channels, wide_x * depth), BF16)],
        smem=1,
    )
    received = lax.all_to_all(sent, AXES, 0, 0, tiled=True)
    second_out, sent = call(
        functools.partial(second_kernel, dims),
        (
            shape((extent_y * channels, extent_x * depth), BF16),
            shape((devices, 128), F32),
        ),
        (first_out, wide_masks, received, params, second_band),
        scratch=[pltpu.VMEM(((extent_y + 2) * 3 * channels, (extent_x + 2) * depth), BF16)],
    )
    received = lax.all_to_all(sent, AXES, 0, 0, tiled=True)
    return call(
        functools.partial(last_kernel, dims),
        shape(features.shape, BF16),
        (second_out, wide_masks, received, params, own),
        scratch=[pltpu.VMEM((channels * BRICK, depth), F32)],
    )


def solution(mesh):
    in_specs = (
        P(None, "region", "strip", None),
        P("region", "strip", None),
        P(),
        P(),
        P(),
        P(),
        P(),
        P(),
    )
    out_specs = P(None, "region", "strip", None)
    return jax.shard_map(
        per_device, mesh=mesh, in_specs=in_specs, out_specs=out_specs, check_vma=False
    )
```

time: 148 us -> 59.5 us (0.40)
  blocking collectives: 86.1 us -> 10.3 us
  Pallas kernels: 0 us -> 15.7 us
  local copies, waits for them, and re-layouts: 13.8 us -> 4.77 us
  other arithmetic: 9.02 us -> 1.68 us
  waiting for transfers between devices: 14.7 us -> 8.19 us
  matrix products: 5.88 us -> 0 us
    psum x2 -> x0, blocking collectives: 86.1 us -> none  [moments(): lax.psum((jnp.sum(voxel_mask), jnp.sum(values * voxel_mask, axis=(1, 2, 3...]
    pallas_call x0 -> x5, Pallas kernels: none -> 15.7 us  [call(): pl.pallas_call(body, out_shape=outs, in_specs=in_specs, out_specs=jax.tre...]
    all_to_all x0 -> x1, starting transfers between devices: none -> 14 us  [per_device(): received = lax.all_to_all(sent, AXES, 0, 0, tiled=True)]
    ppermute x8 -> x4, waiting for transfers between devices: 14.7 us -> 1.73 us  [the longest x2 1.72 us: swap(): lax.ppermute(even, axis, even_pairs(count))]
    ppermute x8 -> x4, starting transfers between devices: 17.2 us -> 4.32 us  [the longest x2 3 us: swap(): lax.ppermute(even, axis, even_pairs(count))]
    all_to_all x0 -> x1, blocking collectives: none -> 10.3 us  [per_device(): received = lax.all_to_all(sent, AXES, 0, 0, tiled=True)]
    unnamed x202 -> x28, local copies, waits for them, and re-layouts: 11.4 us -> 3.74 us
    all_to_all x0 -> x1, waiting for transfers between devices: none -> 6.46 us  [per_device(): received = lax.all_to_all(sent, AXES, 0, 0, tiled=True)]
  transfers between devices with their start and end apart: 8 -> 5, of which waited for: 6 -> 2; matrix products, arithmetic and copies ran while one was open for 0% -> 3% of each run, Pallas kernels for 0% -> 0%
where the time goes in v2:
time: 59.5 us; the launch traced here: 59.1 us
  starting transfers between devices  18.3 us (31%)
  Pallas kernels  15.7 us (26%)
  blocking collectives  10.3 us (17%)
  waiting for transfers between devices  8.19 us (14%)
  local copies, waits for them, and re-layouts  4.77 us (8%)
  other arithmetic  1.68 us (3%)
    pallas_call x5, Pallas kernels, call(): pl.pallas_call(body, out_shape=outs, in_specs=in_specs, out_specs=jax.tre...  15.7 us
    all_to_all x1, starting transfers between devices, per_device(): received = lax.all_to_all(sent, AXES, 0, 0, tiled=True)  14 us
    all_to_all x1, blocking collectives, per_device(): received = lax.all_to_all(sent, AXES, 0, 0, tiled=True)  10.3 us
    all_to_all x1, waiting for transfers between devices, per_device(): received = lax.all_to_all(sent, AXES, 0, 0, tiled=True)  6.46 us
    unnamed x28, local copies, waits for them, and re-layouts  3.74 us
    ppermute x2, starting transfers between devices, swap(): lax.ppermute(even, axis, even_pairs(count))  3 us
    ppermute x2, waiting for transfers between devices, swap(): lax.ppermute(even, axis, even_pairs(count))  1.72 us
    ppermute x2, starting transfers between devices, swap(): lax.ppermute(odd, axis, odd_pairs(count))  1.32 us
  transfers between devices with their start and end apart: 5, of which 2 were waited for; matrix products, arithmetic and copies ran while one was open for 3% of the time, Pallas kernels for 0%

profile of v2, /device:TPU:0, one launch (start us, length us, event | category | flops | bytes accessed | tf_op | source)
XLA Modules:
  0.0 59.1 jit_solution(14607319526527211679)
XLA Ops:
  0.0 0.7 %pad_add_fusion.place = s32[2]{0:T(128)} fusion(s32[1]{0:T(128)} %bitcast.1, s32[1]{0:T(128)} %bitcast), kind=kLoop, calls=%fused_computation.21 | loop fusion | flops 2 | bytes 16 | tf_op jit(solution)/shard_map/stack | solution.py:312
  0.7 2.4 %shard_map.82 = (bf16[8,8,32,128]{3,2,1,0:T(8,128)(2,1)}, f32[1,16,128]{2,1,0:T(8,128)}, bf16[528,128]{1,0:T(8,128)(2,1)}, bf16[528,128]{1,0:T(8,128)(2,1)}) custom-call(s32[2]{0:T(128)} %pad_add_fusion.place, bf16[32,8,8,128]{3,2,1,0:T(8,128)(2,1)} %features.1, s32[1,16]{1,0:T(1,128)} %bitcast.35), custom_call_target="tpu_custom_call" | custom-call | bytes 524360 | tf_op jit(solution)/shard_map/pallas_call | solution.py:38
  3.1 3.0 %collective-permute-start = (bf16[528,128]{1,0:T(8,128)(2,1)}, bf16[528,128]{1,0:T(8,128)(2,1)S(1)}, u32[]{:S(2)}, u32[]{:S(2)}) collective-permute-start(bf16[528,128]{1,0:T(8,128)(2,1)} %get-tuple-element.18), channel_id=1, source_target_pairs={{0,4},{4,0},{8,12},{12,8},{16,20},{20,16},{24,28},{28,24},{1,5},{5... | collective-permute-start | bytes 405512 | tf_op jit(solution)/shard_map/ppermute | solution.py:29
  6.1 0.7 %collective-permute-start.1 = (bf16[528,128]{1,0:T(8,128)(2,1)}, bf16[528,128]{1,0:T(8,128)(2,1)S(1)}, u32[]{:S(2)}, u32[]{:S(2)}) collective-permute-start(bf16[528,128]{1,0:T(8,128)(2,1)} %get-tuple-element.19), channel_id=1, source_target_pairs={{4,8},{12,16},{20,24},{8,4},{16,12},{24,20},{5,9},{13,17},{21,25},... | collective-permute-start | bytes 405512 | tf_op jit(solution)/shard_map/ppermute | solution.py:29
  6.7 0.2 copy.17
  6.9 0.1 pad_dynamic-update-slice_fusion.3
  7.1 0.7 %copy-done.4 = bf16[3,3,3,32,32]{4,3,2,1,0:T(8,128)(2,1)S(1)} copy-done((bf16[3,3,3,32,32]{4,3,2,1,0:T(8,128)(2,1)S(1)}, bf16[3,3,3,32,32]{4,3,2,1,0:T(8,128)(2,1)}, u32[]{:S(2)}) %copy-start.4) | copy-done | bytes 55320
  7.9 0.2 copy.18
  8.0 0.1 pad_dynamic-update-slice_fusion.1
  8.1 1.7 %collective-permute-done.from_even.x_even = bf16[528,128]{1,0:T(8,128)(2,1)S(1)} collective-permute-done((bf16[528,128]{1,0:T(8,128)(2,1)}, bf16[528,128]{1,0:T(8,128)(2,1)S(1)}, u32[]{:S(2)}, u32[]{:S(2)}) %collective-permute-start) | collective-permute-done | bytes 135200 | tf_op jit(solution)/shard_map/ppermute | solution.py:29
  9.9 0.6 %copy-done.1 = bf16[528,128]{1,0:T(8,128)(2,1)} copy-done((bf16[528,128]{1,0:T(8,128)(2,1)}, bf16[528,128]{1,0:T(8,128)(2,1)S(1)}, u32[]{:S(2)}) %copy-start.1) | copy-done | bytes 135192
  10.5 1.9 %shard_map.83 = (bf16[816,128]{1,0:T(8,128)(2,1)}, bf16[816,128]{1,0:T(8,128)(2,1)}) custom-call(s32[2]{0:T(128)} %pad_add_fusion.place, bf16[8,8,32,128]{3,2,1,0:T(8,128)(2,1)} %get-tuple-element.16.own, f32[1,16,128]{2,1,0:T(8,128)} %get-tuple-element.17.masks, bf16[528,128]{1,0:T(8,128)(2,1)} %copy-done.1, bf16[528,128]{1,0:T(8,128)(2,1)} %copy-done.2), custom_call_target="tpu_custom_call" | custom-call | bytes 802824 | tf_op jit(solution)/shard_map/pallas_call | solution.py:38
  12.5 0.7 %collective-permute-start.3 = (bf16[816,128]{1,0:T(8,128)(2,1)}, bf16[816,128]{1,0:T(8,128)(2,1)S(1)}, u32[]{:S(2)}, u32[]{:S(2)}) collective-permute-start(bf16[816,128]{1,0:T(8,128)(2,1)} %get-tuple-element.21), channel_id=1, source_target_pairs={{1,2},{2,1},{5,6},{6,5},{9,10},{10,9},{13,14},{14,13},{17,18},{18,... | collective-permute-start | bytes 626696 | tf_op jit(solution)/shard_map/ppermute | solution.py:29
  13.2 1.0 %fusion.7.band = bf16[3,128,576]{2,1,0:T(8,128)(2,1)} fusion(bf16[3,32,288]{2,1,0:T(8,128)(2,1)S(1)} %bitcast.24), kind=kLoop, calls=%fused_computation.13 | loop fusion | flops 4423680 | bytes 497664 | tf_op jit(solution)/shard_map/concatenate | solution.py:295
  14.2 0.7 %copy-done.5 = bf16[816,128]{1,0:T(8,128)(2,1)} copy-done((bf16[816,128]{1,0:T(8,128)(2,1)}, bf16[816,128]{1,0:T(8,128)(2,1)S(1)}, u32[]{:S(2)}) %copy-start.5) | copy-done | bytes 208920
  14.9 0.7 %copy-done.6 = bf16[816,128]{1,0:T(8,128)(2,1)} copy-done((bf16[816,128]{1,0:T(8,128)(2,1)}, bf16[816,128]{1,0:T(8,128)(2,1)S(1)}, u32[]{:S(2)}) %copy-start.6) | copy-done | bytes 208920
  15.6 4.7 %shard_map.84 = (bf16[320,1280]{1,0:T(8,128)(2,1)}, f32[3,3,8,128]{3,2,1,0:T(8,128)}, f32[32,128]{1,0:T(8,128)}) custom-call(s32[2]{0:T(128)} %pad_add_fusion.place, bf16[8,8,32,128]{3,2,1,0:T(8,128)(2,1)} %get-tuple-element.16.own, f32[1,16,128]{2,1,0:T(8,128)} %get-tuple-element.17.masks, bf16[528,128]{1,0:T(8,128)(2,1)} %copy-done.1, ...), custom_call_target="tpu_custom_call" | custom-call | bytes 1865736 | tf_op jit(solution)/shard_map/pallas_call | solution.py:38
  20.3 14.0 %all-to-all-start = ((f32[32,1,128]{2,1,0:T(1,128)}), f32[32,1,128]{2,1,0:T(1,128)S(1)}, u32[]{:S(2)}, u32[]{:S(2)}) async-start(f32[32,1,128]{2,1,0:T(1,128)} %bitcast.29), calls=%async_computation | async-start | bytes 32768 | tf_op jit(solution)/shard_map/all_to_all | solution.py:356
  34.3 0.6 %copy-done.8 = f32[32]{0:T(128)S(1)} copy-done((f32[32]{0:T(128)S(1)}, f32[32]{0:T(128)}, u32[]{:S(2)}) %copy-start.8) | copy-done | bytes 152
  35.0 6.5 %all-to-all-done = f32[32,1,128]{2,1,0:T(1,128)S(1)} async-done(((f32[32,1,128]{2,1,0:T(1,128)}), f32[32,1,128]{2,1,0:T(1,128)S(1)}, u32[]{:S(2)}, u32[]{:S(2)}) %all-to-all-start) | async-done | bytes 16416 | tf_op jit(solution)/shard_map/all_to_all | solution.py:356
  41.4 0.7 %broadcast_in_dim.2.params = f32[4,32,128]{2,1,0:T(8,128)} broadcast(f32[4,32]{1,0:T(4,128)S(1)} %pad_maximum_fusion), dimensions={0,1} | broadcast | bytes 66048 | tf_op jit(solution)/shard_map/broadcast_in_dim | solution.py:341
  42.1 4.0 %shard_map.85 = (bf16[256,1024]{1,0:T(8,128)(2,1)}, f32[32,128]{1,0:T(8,128)}) custom-call(bf16[320,1280]{1,0:T(8,128)(2,1)} %get-tuple-element.22.first_out, f32[3,3,8,128]{3,2,1,0:T(8,128)} %get-tuple-element.23.wide_masks, f32[32,128]{1,0:T(8,128)} %bitcast.27, f32[4,32,128]{2,1,0:T(8,128)} %broadcast_in_dim.2.params, bf16[3,128,576]{2,1,0:T(8,128)(2,1)} %fusion.7.band), custom_call_target="tpu_custom_call" | custom-call | bytes 1380352 | tf_op jit(solution)/shard_map/pallas_call | solution.py:38
  46.2 10.3 %all_to_all.22 = f32[32,1,128]{2,1,0:T(1,128)} all-to-all(f32[32,1,128]{2,1,0:T(1,128)} %bitcast.30), channel_id=1, replica_groups=mesh['region'=8,'strip'=4] {'region','strip'}, dimensions={0} | all-to-all | bytes 32768 | tf_op jit(solution)/shard_map/all_to_all | solution.py:366
  56.5 2.6 %shard_map.86 = bf16[32,8,8,128]{3,2,1,0:T(8,128)(2,1)} custom-call(bf16[256,1024]{1,0:T(8,128)(2,1)} %get-tuple-element.25.second_out, f32[3,3,8,128]{3,2,1,0:T(8,128)} %get-tuple-element.23.wide_masks, f32[32,128]{1,0:T(8,128)} %bitcast.28, f32[4,32,128]{2,1,0:T(8,128)} %broadcast_in_dim.2.params, bf16[8,8,32,128]{3,2,1,0:T(8,128)(2,1)} %get-tuple-element.16.own), custom_call_target="tpu_custom_call" | custom-call | bytes 1167360 | tf_op jit(solution)/shard_map/pallas_call | solution.py:38
  (27 shorter events, 0.3 us)
Async XLA Ops:
  0.7 6.1 %copy-start.3 = (bf16[3,3,3,32,32]{4,3,2,1,0:T(8,128)(2,1)S(1)}, bf16[3,3,3,32,32]{4,3,2,1,0:T(8,128)(2,1)}, u32[]{:S(2)}) copy-start(bf16[3,3,3,32,32]{4,3,2,1,0:T(8,128)(2,1)} %param.10) | copy-start | bytes 165892
  3.1 6.8 %collective-permute-start = (bf16[528,128]{1,0:T(8,128)(2,1)}, bf16[528,128]{1,0:T(8,128)(2,1)S(1)}, u32[]{:S(2)}, u32[]{:S(2)}) collective-permute-start(bf16[528,128]{1,0:T(8,128)(2,1)} %get-tuple-element.18), channel_id=1, source_target_pairs={{0,4},{4,0},{8,12},{12,8},{16,20},{20,16},{24,28},{28,24},{1,5},{5... | collective-permute-start | bytes 405512 | tf_op jit(solution)/shard_map/ppermute | solution.py:29
  6.1 3.8 %collective-permute-start.1 = (bf16[528,128]{1,0:T(8,128)(2,1)}, bf16[528,128]{1,0:T(8,128)(2,1)S(1)}, u32[]{:S(2)}, u32[]{:S(2)}) collective-permute-start(bf16[528,128]{1,0:T(8,128)(2,1)} %get-tuple-element.19), channel_id=1, source_target_pairs={{4,8},{12,16},{20,24},{8,4},{16,12},{24,20},{5,9},{13,17},{21,25},... | collective-permute-start | bytes 405512 | tf_op jit(solution)/shard_map/ppermute | solution.py:29
  6.9 0.9 %copy-start.4 = (bf16[3,3,3,32,32]{4,3,2,1,0:T(8,128)(2,1)S(1)}, bf16[3,3,3,32,32]{4,3,2,1,0:T(8,128)(2,1)}, u32[]{:S(2)}) copy-start(bf16[3,3,3,32,32]{4,3,2,1,0:T(8,128)(2,1)} %param.11) | copy-start | bytes 165892
  9.8 0.6 %copy-start.1 = (bf16[528,128]{1,0:T(8,128)(2,1)}, bf16[528,128]{1,0:T(8,128)(2,1)S(1)}, u32[]{:S(2)}) copy-start(bf16[528,128]{1,0:T(8,128)(2,1)S(1)} %collective-permute-done.from_even.x_even) | copy-start | bytes 405508
  9.9 0.7 %copy-start.2 = (bf16[528,128]{1,0:T(8,128)(2,1)}, bf16[528,128]{1,0:T(8,128)(2,1)S(1)}, u32[]{:S(2)}) copy-start(bf16[528,128]{1,0:T(8,128)(2,1)S(1)} %collective-permute-done.1.from_odd.x_odd) | copy-start | bytes 405508
  12.5 1.7 %collective-permute-start.2 = (bf16[816,128]{1,0:T(8,128)(2,1)}, bf16[816,128]{1,0:T(8,128)(2,1)S(1)}, u32[]{:S(2)}, u32[]{:S(2)}) collective-permute-start(bf16[816,128]{1,0:T(8,128)(2,1)} %get-tuple-element.20), channel_id=1, source_target_pairs={{0,1},{1,0},{2,3},{3,2},{4,5},{5,4},{6,7},{7,6},{8,9},{9,8},{10,11... | collective-permute-start | bytes 626696 | tf_op jit(solution)/shard_map/ppermute | solution.py:29
  12.5 1.7 %collective-permute-start.3 = (bf16[816,128]{1,0:T(8,128)(2,1)}, bf16[816,128]{1,0:T(8,128)(2,1)S(1)}, u32[]{:S(2)}, u32[]{:S(2)}) collective-permute-start(bf16[816,128]{1,0:T(8,128)(2,1)} %get-tuple-element.21), channel_id=1, source_target_pairs={{1,2},{2,1},{5,6},{6,5},{9,10},{10,9},{13,14},{14,13},{17,18},{18,... | collective-permute-start | bytes 626696 | tf_op jit(solution)/shard_map/ppermute | solution.py:29
  13.2 1.0 %copy-start = (bf16[3,160,672]{2,1,0:T(8,128)(2,1)}, bf16[3,160,672]{2,1,0:T(8,128)(2,1)S(1)}, u32[]{:S(2)}) copy-start(bf16[3,160,672]{2,1,0:T(8,128)(2,1)S(1)} %pad_dynamic-update-slice_fusion.band) | copy-start | bytes 1935364
  14.2 0.7 %copy-start.5 = (bf16[816,128]{1,0:T(8,128)(2,1)}, bf16[816,128]{1,0:T(8,128)(2,1)S(1)}, u32[]{:S(2)}) copy-start(bf16[816,128]{1,0:T(8,128)(2,1)S(1)} %collective-permute-done.2.y_even) | copy-start | bytes 626692
  14.9 0.7 %copy-start.6 = (bf16[816,128]{1,0:T(8,128)(2,1)}, bf16[816,128]{1,0:T(8,128)(2,1)S(1)}, u32[]{:S(2)}) copy-start(bf16[816,128]{1,0:T(8,128)(2,1)S(1)} %collective-permute-done.3.y_odd) | copy-start | bytes 626692
  15.6 18.7 %copy-start.11 = (f32[32]{0:T(128)S(1)}, f32[32]{0:T(128)}, u32[]{:S(2)}) copy-start(f32[32]{0:T(128)} %param.12) | copy-start | bytes 388
  20.3 21.2 %all-to-all-start = ((f32[32,1,128]{2,1,0:T(1,128)}), f32[32,1,128]{2,1,0:T(1,128)S(1)}, u32[]{:S(2)}, u32[]{:S(2)}) async-start(f32[32,1,128]{2,1,0:T(1,128)} %bitcast.29), calls=%async_computation | async-start | bytes 32768 | tf_op jit(solution)/shard_map/all_to_all | solution.py:356
  34.3 0.7 %copy-start.8 = (f32[32]{0:T(128)S(1)}, f32[32]{0:T(128)}, u32[]{:S(2)}) copy-start(f32[32]{0:T(128)} %param.15) | copy-start | bytes 388
  34.3 0.7 %copy-start.9 = (f32[32]{0:T(128)S(1)}, f32[32]{0:T(128)}, u32[]{:S(2)}) copy-start(f32[32]{0:T(128)} %param.14) | copy-start | bytes 388
  34.3 0.7 %copy-start.10 = (f32[32]{0:T(128)S(1)}, f32[32]{0:T(128)}, u32[]{:S(2)}) copy-start(f32[32]{0:T(128)} %param.13) | copy-start | bytes 388
  41.4 0.7 %copy-start.7 = (f32[32,1,128]{2,1,0:T(1,128)}, f32[32,1,128]{2,1,0:T(1,128)S(1)}, u32[]{:S(2)}) copy-start(f32[32,1,128]{2,1,0:T(1,128)S(1)} %all-to-all-done) | copy-start | bytes 49156

commit v3 on v2

--- a/solution.py
+++ b/solution.py
@@ -41,6 +41,7 @@
         in_specs=in_specs,
         out_specs=jax.tree.map(whole, outs),
         scratch_shapes=list(scratch),
+        compiler_params=pltpu.CompilerParams(vmem_limit_bytes=16 << 20),
         cost_estimate=pl.CostEstimate(
             flops=flops,
             transcendentals=0,

time: 59.5 us -> 49.5 us (0.83)
  Pallas kernels: 15.7 us -> 8.36 us
  other arithmetic: 1.68 us -> 0.23 us
  blocking collectives: 10.3 us -> 8.87 us
  starting transfers between devices: 18.3 us -> 19.3 us
  local copies, waits for them, and re-layouts: 4.77 us -> 3.79 us
    pallas_call x5, Pallas kernels: 15.7 us -> 8.36 us  [call(): pl.pallas_call(body, out_shape=outs, in_specs=in_specs, out_specs=jax.tre...]
    all_to_all x1, blocking collectives: 10.3 us -> 8.87 us  [per_device(): received = lax.all_to_all(sent, AXES, 0, 0, tiled=True)]
    concatenate x1, other arithmetic: 1.01 us -> 0.14 us  [band_of(): return jnp.concatenate(parts, axis=1)]
    all_to_all x1, starting transfers between devices: 14 us -> 14.8 us  [per_device(): received = lax.all_to_all(sent, AXES, 0, 0, tiled=True)]
    broadcast_in_dim x1, local copies, waits for them, and re-layouts: 0.7 us -> 0.07 us  [per_device(): jnp.broadcast_to(jnp.stack([gain_first, shift_first, gain_second, shift_s...]
    unnamed x28 -> x20, local copies, waits for them, and re-layouts: 3.74 us -> 3.38 us
  transfers between devices with their start and end apart: 5 -> 5, of which waited for: 2 -> 3; matrix products, arithmetic and copies ran while one was open for 3% -> 2% of each run, Pallas kernels for 0% -> 0%
where the time goes in v3:
time: 49.5 us; the launch traced here: 49.2 us
  starting transfers between devices  19.3 us (39%)
  blocking collectives  8.87 us (18%)
  waiting for transfers between devices  8.51 us (17%)
  Pallas kernels  8.36 us (17%)
  local copies, waits for them, and re-layouts  3.79 us (8%)
    all_to_all x1, starting transfers between devices, per_device(): received = lax.all_to_all(sent, AXES, 0, 0, tiled=True)  14.8 us
    all_to_all x1, blocking collectives, per_device(): received = lax.all_to_all(sent, AXES, 0, 0, tiled=True)  8.87 us
    pallas_call x5, Pallas kernels, call(): pl.pallas_call(body, out_shape=outs, in_specs=in_specs, out_specs=jax.tre...  8.36 us
    all_to_all x1, waiting for transfers between devices, per_device(): received = lax.all_to_all(sent, AXES, 0, 0, tiled=True)  6.4 us
    unnamed x20, local copies, waits for them, and re-layouts  3.38 us
    ppermute x2, starting transfers between devices, swap(): lax.ppermute(even, axis, even_pairs(count))  3.13 us
    ppermute x2, waiting for transfers between devices, swap(): lax.ppermute(even, axis, even_pairs(count))  2.11 us
    ppermute x2, starting transfers between devices, swap(): lax.ppermute(odd, axis, odd_pairs(count))  1.33 us
  transfers between devices with their start and end apart: 5, of which 3 were waited for; matrix products, arithmetic and copies ran while one was open for 2% of the time, Pallas kernels for 0%

profile of v3, /device:TPU:0, one launch (start us, length us, event | category | flops | bytes accessed | tf_op | source)
XLA Modules:
  0.0 49.2 jit_solution(4028683685378721947)
XLA Ops:
  0.0 0.1 pad_add_fusion.place
  0.1 0.7 %copy-done.1 = s32[1,1,16]{2,1,0:T(1,128)S(1)} copy-done((s32[1,1,16]{2,1,0:T(1,128)S(1)}, s32[1,1,16]{2,1,0:T(1,128)}, u32[]{:S(2)}) %copy-start.1) | copy-done | bytes 88
  0.7 1.0 %copy-done = bf16[32,8,8,128]{3,2,1,0:T(8,128)(2,1)S(1)} copy-done((bf16[32,8,8,128]{3,2,1,0:T(8,128)(2,1)S(1)}, bf16[32,8,8,128]{3,2,1,0:T(8,128)(2,1)}, u32[]{:S(2)}) %copy-start) | copy-done | bytes 524312
  1.8 1.0 %shard_map.82 = (bf16[8,8,32,128]{3,2,1,0:T(8,128)(2,1)S(1)}, f32[1,16,128]{2,1,0:T(8,128)S(1)}, bf16[528,128]{1,0:T(8,128)(2,1)S(1)}, bf16[528,128]{1,0:T(8,128)(2,1)S(1)}) custom-call(s32[2]{0:T(128)S(1)} %pad_add_fusion.place, bf16[32,8,8,128]{3,2,1,0:T(8,128)(2,1)S(1)} %copy-done, s32[1,16]{1,0:T(1,128)S(1)} %bitcast.22), custom_call_target="tpu_custom_call" | custom-call | bytes 524360 | tf_op jit(solution)/shard_map/pallas_call | solution.py:38
  2.8 3.1 %collective-permute-start = (bf16[528,128]{1,0:T(8,128)(2,1)S(1)}, bf16[528,128]{1,0:T(8,128)(2,1)S(1)}, u32[]{:S(2)}, u32[]{:S(2)}) collective-permute-start(bf16[528,128]{1,0:T(8,128)(2,1)S(1)} %get-tuple-element.18), channel_id=1, source_target_pairs={{0,4},{4,0},{8,12},{12,8},{16,20},{20,16},{24,28},{28,24},{1,5},{5... | collective-permute-start | bytes 405512 | tf_op jit(solution)/shard_map/ppermute | solution.py:29
  5.8 0.7 %collective-permute-start.1 = (bf16[528,128]{1,0:T(8,128)(2,1)S(1)}, bf16[528,128]{1,0:T(8,128)(2,1)S(1)}, u32[]{:S(2)}, u32[]{:S(2)}) collective-permute-start(bf16[528,128]{1,0:T(8,128)(2,1)S(1)} %get-tuple-element.19), channel_id=1, source_target_pairs={{4,8},{12,16},{20,24},{8,4},{16,12},{24,20},{5,9},{13,17},{21,25},... | collective-permute-start | bytes 405512 | tf_op jit(solution)/shard_map/ppermute | solution.py:29
  6.5 0.2 copy.17
  6.7 0.1 pad_dynamic-update-slice_fusion.3
  6.8 0.1 pad_dynamic-update-slice_fusion.2
  6.9 0.7 %copy-done.3 = bf16[3,3,3,32,32]{4,3,2,1,0:T(8,128)(2,1)S(1)} copy-done((bf16[3,3,3,32,32]{4,3,2,1,0:T(8,128)(2,1)S(1)}, bf16[3,3,3,32,32]{4,3,2,1,0:T(8,128)(2,1)}, u32[]{:S(2)}) %copy-start.3) | copy-done | bytes 55320
  7.6 0.2 copy.18
  7.8 0.1 pad_dynamic-update-slice_fusion.1
  7.9 1.5 %collective-permute-done.from_even.x_even = bf16[528,128]{1,0:T(8,128)(2,1)S(1)} collective-permute-done((bf16[528,128]{1,0:T(8,128)(2,1)S(1)}, bf16[528,128]{1,0:T(8,128)(2,1)S(1)}, u32[]{:S(2)}, u32[]{:S(2)}) %collective-permute-start) | collective-permute-done | bytes 135200 | tf_op jit(solution)/shard_map/ppermute | solution.py:29
  9.4 0.6 %shard_map.83 = (bf16[816,128]{1,0:T(8,128)(2,1)S(1)}, bf16[816,128]{1,0:T(8,128)(2,1)S(1)}) custom-call(s32[2]{0:T(128)S(1)} %pad_add_fusion.place, bf16[8,8,32,128]{3,2,1,0:T(8,128)(2,1)S(1)} %get-tuple-element.16.own, f32[1,16,128]{2,1,0:T(8,128)S(1)} %get-tuple-element.17.masks, bf16[528,128]{1,0:T(8,128)(2,1)S(1)} %collective-permute-done.from_even.x_even, ...), custom_call_target="tpu_custom_call" | custom-call | bytes 802824 | tf_op jit(solution)/shard_map/pallas_call | solution.py:38
  10.1 0.7 %collective-permute-start.3 = (bf16[816,128]{1,0:T(8,128)(2,1)S(1)}, bf16[816,128]{1,0:T(8,128)(2,1)S(1)}, u32[]{:S(2)}, u32[]{:S(2)}) collective-permute-start(bf16[816,128]{1,0:T(8,128)(2,1)S(1)} %get-tuple-element.21), channel_id=1, source_target_pairs={{1,2},{2,1},{5,6},{6,5},{9,10},{10,9},{13,14},{14,13},{17,18},{18,... | collective-permute-start | bytes 626696 | tf_op jit(solution)/shard_map/ppermute | solution.py:29
  10.8 0.1 fusion.7.band
  10.9 0.6 %collective-permute-done.2.y_even = bf16[816,128]{1,0:T(8,128)(2,1)S(1)} collective-permute-done((bf16[816,128]{1,0:T(8,128)(2,1)S(1)}, bf16[816,128]{1,0:T(8,128)(2,1)S(1)}, u32[]{:S(2)}, u32[]{:S(2)}) %collective-permute-start.2) | collective-permute-done | bytes 208928 | tf_op jit(solution)/shard_map/ppermute | solution.py:29
  11.5 3.5 %shard_map.84 = (bf16[320,1280]{1,0:T(8,128)(2,1)S(1)}, f32[3,3,8,128]{3,2,1,0:T(8,128)S(1)}, f32[32,128]{1,0:T(8,128)}) custom-call(s32[2]{0:T(128)S(1)} %pad_add_fusion.place, bf16[8,8,32,128]{3,2,1,0:T(8,128)(2,1)S(1)} %get-tuple-element.16.own, f32[1,16,128]{2,1,0:T(8,128)S(1)} %get-tuple-element.17.masks, ...), custom_call_target="tpu_custom_call" | custom-call | bytes 1865736 | tf_op jit(solution)/shard_map/pallas_call | solution.py:38
  15.0 14.8 %all-to-all-start = ((f32[32,1,128]{2,1,0:T(1,128)}), f32[32,1,128]{2,1,0:T(1,128)S(1)}, u32[]{:S(2)}, u32[]{:S(2)}) async-start(f32[32,1,128]{2,1,0:T(1,128)} %bitcast.6), calls=%async_computation | async-start | bytes 32768 | tf_op jit(solution)/shard_map/all_to_all | solution.py:357
  29.9 0.6 %copy-done.4 = f32[32]{0:T(128)S(1)} copy-done((f32[32]{0:T(128)S(1)}, f32[32]{0:T(128)}, u32[]{:S(2)}) %copy-start.4) | copy-done | bytes 152
  30.5 6.4 %all-to-all-done = f32[32,1,128]{2,1,0:T(1,128)S(1)} async-done(((f32[32,1,128]{2,1,0:T(1,128)}), f32[32,1,128]{2,1,0:T(1,128)S(1)}, u32[]{:S(2)}, u32[]{:S(2)}) %all-to-all-start) | async-done | bytes 16416 | tf_op jit(solution)/shard_map/all_to_all | solution.py:357
  37.0 2.0 %shard_map.85 = (bf16[256,1024]{1,0:T(8,128)(2,1)S(1)}, f32[32,128]{1,0:T(8,128)S(1)}) custom-call(bf16[320,1280]{1,0:T(8,128)(2,1)S(1)} %get-tuple-element.22.first_out, f32[3,3,8,128]{3,2,1,0:T(8,128)S(1)} %get-tuple-element.23.wide_masks, f32[32,128]{1,0:T(8,128)S(1)} %bitcast.19, f32[4,32,128]{2,1,0:T(8,128)S(1)} %broadcast_in_dim.2.params, ...), custom_call_target="tpu_custom_call" | custom-call | bytes 1380352 | tf_op jit(solution)/shard_map/pallas_call | solution.py:38
  39.0 8.9 %all_to_all.22 = f32[32,1,128]{2,1,0:T(1,128)S(1)} all-to-all(f32[32,1,128]{2,1,0:T(1,128)S(1)} %bitcast.21), channel_id=1, replica_groups=mesh['region'=8,'strip'=4] {'region','strip'}, dimensions={0} | all-to-all | bytes 32768 | tf_op jit(solution)/shard_map/all_to_all | solution.py:367
  47.9 1.3 %shard_map.86 = bf16[32,8,8,128]{3,2,1,0:T(8,128)(2,1)} custom-call(bf16[256,1024]{1,0:T(8,128)(2,1)S(1)} %get-tuple-element.25.second_out, f32[3,3,8,128]{3,2,1,0:T(8,128)S(1)} %get-tuple-element.23.wide_masks, f32[32,128]{1,0:T(8,128)S(1)} %bitcast.20, f32[4,32,128]{2,1,0:T(8,128)S(1)} %broadcast_in_dim.2.params, ...), custom_call_target="tpu_custom_call" | custom-call | bytes 1167360 | tf_op jit(solution)/shard_map/pallas_call | solution.py:38
  (19 shorter events, 0.2 us)
Async XLA Ops:
  0.1 0.7 %copy-start.1 = (s32[1,1,16]{2,1,0:T(1,128)S(1)}, s32[1,1,16]{2,1,0:T(1,128)}, u32[]{:S(2)}) copy-start(s32[1,1,16]{2,1,0:T(1,128)} %param.9) | copy-start | bytes 196
  0.7 1.0 %copy-start = (bf16[32,8,8,128]{3,2,1,0:T(8,128)(2,1)S(1)}, bf16[32,8,8,128]{3,2,1,0:T(8,128)(2,1)}, u32[]{:S(2)}) copy-start(bf16[32,8,8,128]{3,2,1,0:T(8,128)(2,1)} %features.1) | copy-start | bytes 1572868
  1.8 4.7 %copy-start.2 = (bf16[3,3,3,32,32]{4,3,2,1,0:T(8,128)(2,1)S(1)}, bf16[3,3,3,32,32]{4,3,2,1,0:T(8,128)(2,1)}, u32[]{:S(2)}) copy-start(bf16[3,3,3,32,32]{4,3,2,1,0:T(8,128)(2,1)} %param.10) | copy-start | bytes 165892
  2.8 6.6 %collective-permute-start = (bf16[528,128]{1,0:T(8,128)(2,1)S(1)}, bf16[528,128]{1,0:T(8,128)(2,1)S(1)}, u32[]{:S(2)}, u32[]{:S(2)}) collective-permute-start(bf16[528,128]{1,0:T(8,128)(2,1)S(1)} %get-tuple-element.18), channel_id=1, source_target_pairs={{0,4},{4,0},{8,12},{12,8},{16,20},{20,16},{24,28},{28,24},{1,5},{5... | collective-permute-start | bytes 405512 | tf_op jit(solution)/shard_map/ppermute | solution.py:29
  5.8 3.6 %collective-permute-start.1 = (bf16[528,128]{1,0:T(8,128)(2,1)S(1)}, bf16[528,128]{1,0:T(8,128)(2,1)S(1)}, u32[]{:S(2)}, u32[]{:S(2)}) collective-permute-start(bf16[528,128]{1,0:T(8,128)(2,1)S(1)} %get-tuple-element.19), channel_id=1, source_target_pairs={{4,8},{12,16},{20,24},{8,4},{16,12},{24,20},{5,9},{13,17},{21,25},... | collective-permute-start | bytes 405512 | tf_op jit(solution)/shard_map/ppermute | solution.py:29
  6.7 0.9 %copy-start.3 = (bf16[3,3,3,32,32]{4,3,2,1,0:T(8,128)(2,1)S(1)}, bf16[3,3,3,32,32]{4,3,2,1,0:T(8,128)(2,1)}, u32[]{:S(2)}) copy-start(bf16[3,3,3,32,32]{4,3,2,1,0:T(8,128)(2,1)} %param.11) | copy-start | bytes 165892
  10.0 1.5 %collective-permute-start.2 = (bf16[816,128]{1,0:T(8,128)(2,1)S(1)}, bf16[816,128]{1,0:T(8,128)(2,1)S(1)}, u32[]{:S(2)}, u32[]{:S(2)}) collective-permute-start(bf16[816,128]{1,0:T(8,128)(2,1)S(1)} %get-tuple-element.20), channel_id=1, source_target_pairs={{0,1},{1,0},{2,3},{3,2},{4,5},{5,4},{6,7},{7,6},{8,9},{9,8},{10,11... | collective-permute-start | bytes 626696 | tf_op jit(solution)/shard_map/ppermute | solution.py:29
  10.1 1.4 %collective-permute-start.3 = (bf16[816,128]{1,0:T(8,128)(2,1)S(1)}, bf16[816,128]{1,0:T(8,128)(2,1)S(1)}, u32[]{:S(2)}, u32[]{:S(2)}) collective-permute-start(bf16[816,128]{1,0:T(8,128)(2,1)S(1)} %get-tuple-element.21), channel_id=1, source_target_pairs={{1,2},{2,1},{5,6},{6,5},{9,10},{10,9},{13,14},{14,13},{17,18},{18,... | collective-permute-start | bytes 626696 | tf_op jit(solution)/shard_map/ppermute | solution.py:29
  11.5 18.3 %copy-start.7 = (f32[32]{0:T(128)S(1)}, f32[32]{0:T(128)}, u32[]{:S(2)}) copy-start(f32[32]{0:T(128)} %param.12) | copy-start | bytes 388
  15.0 21.9 %all-to-all-start = ((f32[32,1,128]{2,1,0:T(1,128)}), f32[32,1,128]{2,1,0:T(1,128)S(1)}, u32[]{:S(2)}, u32[]{:S(2)}) async-start(f32[32,1,128]{2,1,0:T(1,128)} %bitcast.6), calls=%async_computation | async-start | bytes 32768 | tf_op jit(solution)/shard_map/all_to_all | solution.py:357
  29.8 0.7 %copy-start.4 = (f32[32]{0:T(128)S(1)}, f32[32]{0:T(128)}, u32[]{:S(2)}) copy-start(f32[32]{0:T(128)} %param.15) | copy-start | bytes 388
  29.8 0.7 %copy-start.5 = (f32[32]{0:T(128)S(1)}, f32[32]{0:T(128)}, u32[]{:S(2)}) copy-start(f32[32]{0:T(128)} %param.14) | copy-start | bytes 388
  29.8 0.7 %copy-start.6 = (f32[32]{0:T(128)S(1)}, f32[32]{0:T(128)}, u32[]{:S(2)}) copy-start(f32[32]{0:T(128)} %param.13) | copy-start | bytes 388

commit v4 on v3

v4 whole, which is shorter than its diff:
```python
import functools

import jax
import jax.numpy as jnp
from jax import lax
from jax.experimental import pallas as pl
from jax.experimental.pallas import tpu as pltpu
from jax.sharding import PartitionSpec as P

BRICK = 8
EPSILON = 1e-05
HALO = 2
AXES = ("region", "strip")
F32 = jnp.float32
BF16 = jnp.bfloat16


def even_pairs(count):
    return [(i, i ^ 1) for i in range(count) if (i ^ 1) < count]


def odd_pairs(count):
    pairs = [(i, i + 1) for i in range(1, count - 1, 2)]
    return pairs + [(b, a) for a, b in pairs]


def swap(even, odd, axis):
    count = lax.axis_size(axis)
    return lax.ppermute(even, axis, even_pairs(count)), lax.ppermute(odd, axis, odd_pairs(count))


def whole(*_):
    return pl.BlockSpec(memory_space=pltpu.VMEM)


def call(body, outs, ins, scratch=(), flops=0, smem=0, aliases=None):
    in_specs = [pl.BlockSpec(memory_space=pltpu.SMEM)] * smem + [whole()] * (len(ins) - smem)
    return pl.pallas_call(
        body,
        out_shape=outs,
        in_specs=in_specs,
        out_specs=jax.tree.map(whole, outs),
        scratch_shapes=list(scratch),
        input_output_aliases=aliases or {},
        compiler_params=pltpu.CompilerParams(vmem_limit_bytes=16 << 20),
        cost_estimate=pl.CostEstimate(
            flops=flops,
            transcendentals=0,
            bytes_accessed=sum(a.size * a.dtype.itemsize for a in ins),
        ),
    )(*ins)


def brick_rows(bricks, depth):
    count = bricks.shape[1]
    at = lax.broadcasted_iota(jnp.int32, (count, depth), 0)
    voxel = lax.broadcasted_iota(jnp.int32, (count, depth), 1)
    spread = (voxel // BRICK == at).astype(F32)
    return jnp.dot(bricks, spread, preferred_element_type=F32, precision=lax.Precision.HIGHEST)


def sides(place, even, odd):
    first = place == 0
    return ((even, jnp.where(first, 0, 1)), (odd, jnp.where(first, 1, 0)))


def gather_kernel(
    dims, place, features, bricks, own, masks, x_even, x_odd, y_even, y_odd, turned
):
    channels, extent_x, extent_y, depth, bx, by = dims
    rows = brick_rows(bricks[...].astype(F32), depth)
    for i in range(bx * by):
        masks[i] = jnp.broadcast_to(rows[i : i + 1], (16, depth))
    for x in range(extent_x):
        for j in range(by):
            part = features[:, x, j * BRICK : (j + 1) * BRICK, :].astype(F32)
            part = part * masks[x // BRICK * by + j][None, :BRICK, :]
            turned[...] = part.reshape(channels * BRICK, depth)
            for y in range(BRICK):
                own[x, j * BRICK + y] = turned[pl.ds(y, channels, stride=BRICK), :].astype(BF16)
    for out, low in sides(place[0], x_even, x_odd):
        start = jnp.where(low == 1, 0, extent_x - HALO)
        for i in range(HALO):
            for y in range(extent_y):
                at = (i * extent_y + y) * channels
                out[at : at + channels, :] = own[start + i, y]
        base = HALO * extent_y * channels
        for j in range(by):
            tile = masks[jnp.where(low == 1, 0, bx - 1) * by + j]
            out[base + 16 * j : base + 16 * (j + 1), :] = tile.astype(BF16)
    for out, low in sides(place[1], y_even, y_odd):
        start = jnp.where(low == 1, 0, extent_y - HALO)
        for x in range(extent_x):
            for j in range(HALO):
                at = (x * HALO + j) * channels
                out[at : at + channels, :] = own[x, start + j]
        base = extent_x * HALO * channels
        for i in range(bx):
            tile = masks[i * by + jnp.where(low == 1, 0, by - 1)]
            out[base + 16 * i : base + 16 * (i + 1), :] = tile.astype(BF16)


def corner_kernel(dims, place, x_even, x_odd, even, odd):
    channels, extent_x, extent_y, depth, bx, by = dims
    first_x = place[0] == 0
    base = HALO * extent_y * channels
    for out, low in sides(place[1], even, odd):
        start = jnp.where(low == 1, 0, extent_y - HALO)
        brick = jnp.where(low == 1, 0, by - 1)
        half = HALO * HALO * channels
        for i in range(HALO):
            for j in range(HALO):
                at = pl.multiple_of((i * extent_y + start + j) * channels, channels)
                a = x_even[pl.ds(at, channels), :]
                b = x_odd[pl.ds(at, channels), :]
                to = (i * HALO + j) * channels
                out[to : to + channels, :] = jnp.where(first_x, b, a)
                out[half + to : half + to + channels, :] = jnp.where(first_x, a, b)
        at = pl.multiple_of(base + brick * 16, 16)
        a = x_even[pl.ds(at, 16), :]
        b = x_odd[pl.ds(at, 16), :]
        out[2 * half : 2 * half + 16, :] = jnp.where(first_x, b, a)
        out[2 * half + 16 : 2 * half + 32, :] = jnp.where(first_x, a, b)


def put_shifted(field, x, y, value):
    channels, depth = value.shape
    lane = lax.broadcasted_iota(jnp.int32, value.shape, 1)
    before = jnp.where(lane == 0, 0.0, pltpu.roll(value, 1, 1))
    after = jnp.where(lane == depth - 1, 0.0, pltpu.roll(value, depth - 1, 1))
    for k, part in enumerate((before, value, after)):
        at = (3 * y + k) * channels
        field[at : at + channels, x * depth : (x + 1) * depth] = part.astype(BF16)


def send_stats(out, channels, sums, squares, counts):
    depth = sums.shape[1]
    rest = jnp.zeros((128 - 2 * channels - counts.shape[0], depth), F32)
    table = jnp.concatenate([sums, squares, counts, rest], axis=0)
    row = jnp.sum(jnp.transpose(table), axis=0, keepdims=True)
    out[...] = jnp.broadcast_to(row, out.shape)


def affine(stats, gain, channels, depth):
    row = jnp.sum(stats[...], axis=0, keepdims=True)
    table = jnp.transpose(jnp.broadcast_to(row, (128, 128)))
    total = jnp.sum(table[2 * channels : 2 * channels + BRICK], axis=0, keepdims=True)
    average = table[:channels] / total
    variance = table[channels : 2 * channels] / total - average * average
    return average, lax.rsqrt(variance + EPSILON) * gain


def fill_kernel(dims, own, field):
    extent_x, extent_y = dims[1:3]
    for x in range(extent_x):
        for y in range(extent_y):
            put_shifted(field, HALO + x, HALO + y, own[x, y].astype(F32))


def fill_halo(dims, place, edges, field):
    channels, extent_x, extent_y = dims[:3]
    first_x = place[0] == 0
    first_y = place[1] == 0
    x_even, x_odd, y_even, y_odd, c_even, c_odd = edges

    def put_pair(first, even, odd, at, low_to, high_to):
        a = even[at : at + channels, :].astype(F32)
        b = odd[at : at + channels, :].astype(F32)
        put_shifted(field, *low_to, jnp.where(first, b, a))
        put_shifted(field, *high_to, jnp.where(first, a, b))

    far_x, far_y = HALO + extent_x, HALO + extent_y
    for i in range(HALO):
        for y in range(extent_y):
            at = (i * extent_y + y) * channels
            put_pair(first_x, x_even, x_odd, at, (i, HALO + y), (far_x + i, HALO + y))
    for x in range(extent_x):
        for j in range(HALO):
            at = (x * HALO + j) * channels
            put_pair(first_y, y_even, y_odd, at, (HALO + x, j), (HALO + x, far_y + j))
    for side in range(2):
        for i in range(HALO):
            for j in range(HALO):
                at = ((side * HALO + i) * HALO + j) * channels
                x = side * far_x + i
                put_pair(first_y, c_even, c_odd, at, (x, j), (x, far_y + j))


def fill_masks(dims, place, masks, edges, wide_masks):
    channels, extent_x, extent_y, depth, bx, by = dims
    first_x = place[0] == 0
    first_y = place[1] == 0
    x_even, x_odd, y_even, y_odd, c_even, c_odd = edges

    def mask_pair(first, even, odd, at, low_to, high_to):
        a = even[at : at + 16, :].astype(F32)[:BRICK]
        b = odd[at : at + 16, :].astype(F32)[:BRICK]
        wide_masks[low_to] = jnp.where(first, b, a)
        wide_masks[high_to] = jnp.where(first, a, b)

    for i in range(bx):
        for j in range(by):
            wide_masks[1 + i, 1 + j] = masks[i * by + j][:BRICK]
    base = HALO * extent_y * channels
    for j in range(by):
        mask_pair(first_x, x_even, x_odd, base + 16 * j, (0, 1 + j), (1 + bx, 1 + j))
    base = extent_x * HALO * channels
    for i in range(bx):
        mask_pair(first_y, y_even, y_odd, base + 16 * i, (1 + i, 0), (1 + i, 1 + by))
    base = 2 * HALO * HALO * channels
    for side in range(2):
        x = side * (1 + bx)
        mask_pair(first_y, c_even, c_odd, base + 16 * side, (x, 0), (x, 1 + by))


def band_dot(band, field, x, y, rows, reach, depth):
    total = jnp.zeros((rows, 2 * depth), F32)
    channels = reach[1]
    for step in range(3):
        parts = [
            field[
                y * 3 * channels : y * 3 * channels + reach[0],
                (i + step) * depth : (i + step + 1) * depth,
            ]
            for i in x
        ]
        window = jnp.concatenate(parts, axis=1)
        total = total + jnp.dot(band[step, :rows, : reach[0]], window, preferred_element_type=F32)
    return total


def first_kernel(dims, place, filled, masks, *refs):
    edges, band, field, first_out, wide_masks, stats = refs[:6], *refs[6:]
    fill_halo(dims, place, edges, field)
    fill_masks(dims, place, masks, edges, wide_masks)
    own_outputs(dims, band, field, 1, wide_masks, first_out, stats)


def own_outputs(dims, band, field, shift, wide_masks, out, stats):
    channels, extent_x, extent_y, depth, bx, by = dims
    sums = jnp.zeros((channels, depth), F32)
    squares = jnp.zeros((channels, depth), F32)
    block = band.shape[1] // channels
    reach = (band.shape[2], channels)
    for x in range(0, extent_x, 2):
        for start in range(0, extent_y, block):
            total = band_dot(
                band,
                field,
                (x + shift, x + shift + 1),
                start + shift,
                block * channels,
                reach,
                depth,
            )
            for i in range(2):
                for j in range(block):
                    mask = wide_masks[(x + i) // BRICK + 1, (start + j) // BRICK + 1][:1]
                    part = total[j * channels : (j + 1) * channels, i * depth : (i + 1) * depth]
                    value = (part * mask).astype(BF16)
                    out[
                        (start + j) * channels : (start + j + 1) * channels,
                        (x + i) * depth : (x + i + 1) * depth,
                    ] = value
                    value = value.astype(F32)
                    sums = sums + value
                    squares = squares + value * value
    count_mask(stats, channels, sums, squares, wide_masks, dims)


def ring_kernel(dims, place, own, *refs):
    channels, extent_x, extent_y, depth, bx, by = dims
    edges, band, wide_masks, ring_y, ring_x, field = refs[:6], *refs[6:]
    fill_halo(dims, place, edges, field)
    for x in range(extent_x):
        for y in range(extent_y):
            if x == 0 or y == 0 or x == extent_x - 1 or y == extent_y - 1:
                put_shifted(field, HALO + x, HALO + y, own[x, y].astype(F32))
    for side in range(2):
        y = side * (extent_y + 1)
        for x in range(0, extent_x + 2, 2):
            total = band_dot(band, field, (x, x + 1), y, channels, (9 * channels, channels), depth)
            for i in range(2):
                mask = wide_masks[(x + i - 1) // BRICK + 1, side * (by + 1)][:1]
                part = total[:, i * depth : (i + 1) * depth] * mask
                ring_y[
                    side * channels : (side + 1) * channels, (x + i) * depth : (x + i + 1) * depth
                ] = part.astype(BF16)
    block = band.shape[1] // channels
    for start in range(0, extent_y, block):
        total = band_dot(
            band,
            field,
            (0, extent_x + 1),
            start + 1,
            block * channels,
            (band.shape[2], channels),
            depth,
        )
        for i in range(2):
            for j in range(block):
                mask = wide_masks[i * (bx + 1), (start + j) // BRICK + 1][:1]
                part = total[j * channels : (j + 1) * channels, i * depth : (i + 1) * depth]
                ring_x[
                    (start + j) * channels : (start + j + 1) * channels,
                    i * depth : (i + 1) * depth,
                ] = (part * mask).astype(BF16)


def count_mask(stats, channels, sums, squares, wide_masks, dims):
    bx, by = dims[4:]
    counts = jnp.zeros(wide_masks.shape[2:], F32)
    for i in range(bx):
        for j in range(by):
            counts = counts + wide_masks[1 + i, 1 + j] * float(BRICK)
    send_stats(stats, channels, sums, squares, counts)


def second_kernel(
    dims, first_out, ring_y, ring_x, wide_masks, received, params, band, second_out, stats, field
):
    channels, extent_x, extent_y, depth, bx, by = dims
    average, scale = affine(received, params[0], channels, depth)
    shift = params[1]

    def tile(ref, row, column):
        return ref[row * channels : (row + 1) * channels, column * depth : (column + 1) * depth]

    for x in range(extent_x + 2):
        for y in range(extent_y + 2):
            if y in (0, extent_y + 1):
                part = tile(ring_y, int(y > 0), x)
            elif x in (0, extent_x + 1):
                part = tile(ring_x, y - 1, int(x > 0))
            else:
                part = tile(first_out, y - 1, x - 1)
            mask = wide_masks[(x - 1) // BRICK + 1, (y - 1) // BRICK + 1][:1]
            part = jnp.maximum((part.astype(F32) - average) * scale + shift, 0.0) * mask
            put_shifted(field, x, y, part)
    own_outputs(dims, band, field, 0, wide_masks, second_out, stats)


def last_kernel(dims, second_out, wide_masks, received, params, own, result, turned):
    channels, extent_x, extent_y, depth, bx, by = dims
    average, scale = affine(received, params[2], channels, depth)
    shift = params[3]
    for x in range(extent_x):
        for j in range(by):
            mask = wide_masks[x // BRICK + 1, j + 1][:1]
            for y in range(BRICK):
                at = j * BRICK + y
                part = second_out[
                    at * channels : (at + 1) * channels, x * depth : (x + 1) * depth
                ].astype(F32)
                part = (part - average) * scale + shift + own[x, at].astype(F32)
                turned[pl.ds(y, channels, stride=BRICK), :] = jnp.maximum(part, 0.0) * mask
            result[:, x, j * BRICK : (j + 1) * BRICK, :] = (
                turned[...].reshape(channels, BRICK, depth).astype(BF16)
            )


def prepare_kernel(block, weights_first, weights_second, rows, first_band, second_band, params):
    for weights, band in ((weights_first, first_band), (weights_second, second_band)):
        fan_in, fan_out = weights.shape[3:]
        tall = 9 * fan_in
        wide = -(-band.shape[2] // 128) * 128
        for step in range(3):
            part = weights[step].astype(F32).reshape(tall, fan_out)
            part = jnp.concatenate([part, jnp.zeros((tall, 128 - fan_out), F32)], axis=1)
            part = jnp.concatenate([part, jnp.zeros((wide - tall, 128), F32)], axis=0)
            part = jnp.transpose(part)[:fan_out]
            for y in range(block):
                moved = part if y == 0 else pltpu.roll(part, 3 * fan_in * y, 1)
                band[step, y * fan_out : (y + 1) * fan_out, :] = moved[:, : band.shape[2]].astype(BF16)
    channels = rows.shape[1]
    for i in range(4):
        row = jnp.concatenate([rows[i : i + 1, :], jnp.zeros((1, 128 - channels), F32)], axis=1)
        params[i] = jnp.transpose(jnp.broadcast_to(row, (128, 128)))[:channels]


def per_device(
    features,
    brick_mask,
    conv_first,
    conv_second,
    gain_first,
    shift_first,
    gain_second,
    shift_second,
):
    channels, extent_x, extent_y, depth = features.shape
    bx, by, bz = brick_mask.shape
    dims = (channels, extent_x, extent_y, depth, bx, by)
    devices = lax.axis_size(AXES)
    place = jnp.stack([lax.axis_index("region") % 2, lax.axis_index("strip") % 2]).astype(jnp.int32)
    wide_x = extent_x + 2 * HALO
    shape = jax.ShapeDtypeStruct

    x_rows = HALO * extent_y * channels + 16 * by
    y_rows = HALO * extent_x * channels + 16 * bx
    c_rows = 2 * HALO * HALO * channels + 32
    own, masks, x_even, x_odd, y_even, y_odd = call(
        functools.partial(gather_kernel, dims),
        (
            shape((extent_x, extent_y, channels, depth), BF16),
            shape((bx * by, 16, depth), F32),
            shape((x_rows, depth), BF16),
            shape((x_rows, depth), BF16),
            shape((y_rows, depth), BF16),
            shape((y_rows, depth), BF16),
        ),
        (place, features, brick_mask.reshape(bx * by, bz)),
        scratch=[pltpu.VMEM((channels * BRICK, depth), F32)],
        smem=1,
    )
    x_even, x_odd = swap(x_even, x_odd, "region")
    y_even, y_odd = swap(y_even, y_odd, "strip")
    c_even, c_odd = call(
        functools.partial(corner_kernel, dims),
        (shape((c_rows, depth), BF16), shape((c_rows, depth), BF16)),
        (place, x_even, x_odd),
        smem=1,
    )
    c_even, c_odd = swap(c_even, c_odd, "strip")

    block = extent_y // 2
    band_shape = shape((3, block * channels, (block + 2) * 3 * channels), BF16)
    first_band, second_band, params = call(
        functools.partial(prepare_kernel, block),
        (band_shape, band_shape, shape((4, channels, depth), F32)),
        (
            conv_first,
            conv_second,
            jnp.stack([gain_first, shift_first, gain_second, shift_second]),
        ),
    )
    field_shape = shape(((extent_y + 2 * HALO) * 3 * channels, wide_x * depth), BF16)
    filled = call(functools.partial(fill_kernel, dims), field_shape, (own,))
    edges = (x_even, x_odd, y_even, y_odd, c_even, c_odd)
    field, first_out, wide_masks, sent = call(
        functools.partial(first_kernel, dims),
        (
            field_shape,
            shape((extent_y * channels, extent_x * depth), BF16),
            shape((bx + 2, by + 2, BRICK, depth), F32),
            shape((devices, 128), F32),
        ),
        (place, filled, masks, *edges, first_band),
        smem=1,
        aliases={1: 0},
    )
    del field
    received = lax.all_to_all(sent, AXES, 0, 0, tiled=True)
    ring_y, ring_x = call(
        functools.partial(ring_kernel, dims),
        (
            shape((2 * channels, (extent_x + 2) * depth), BF16),
            shape((extent_y * channels, 2 * depth), BF16),
        ),
        (place, own, *edges, first_band, wide_masks),
        scratch=[pltpu.VMEM(field_shape.shape, BF16)],
        smem=1,
    )
    second_out, sent = call(
        functools.partial(second_kernel, dims),
        (
            shape((extent_y * channels, extent_x * depth), BF16),
            shape((devices, 128), F32),
        ),
        (first_out, ring_y, ring_x, wide_masks, received, params, second_band),
        scratch=[pltpu.VMEM(((extent_y + 2) * 3 * channels, (extent_x + 2) * depth), BF16)],
    )
    received = lax.all_to_all(sent, AXES, 0, 0, tiled=True)
    return call(
        functools.partial(last_kernel, dims),
        shape(features.shape, BF16),
        (second_out, wide_masks, received, params, own),
        scratch=[pltpu.VMEM((channels * BRICK, depth), F32)],
    )


def solution(mesh):
    in_specs = (
        P(None, "region", "strip", None),
        P("region", "strip", None),
        P(),
        P(),
        P(),
        P(),
        P(),
        P(),
    )
    out_specs = P(None, "region", "strip", None)
    return jax.shard_map(
        per_device, mesh=mesh, in_specs=in_specs, out_specs=out_specs, check_vma=False
    )
```

time: 49.5 us -> 47.3 us (0.956)
  Pallas kernels: 8.36 us -> 10.5 us
  local copies, waits for them, and re-layouts: 3.79 us -> 1.72 us
  waiting for transfers between devices: 8.51 us -> 6.96 us
  starting transfers between devices: 19.3 us -> 18.8 us
    all_to_all x1, starting transfers between devices: 14.8 us -> 12.5 us  [per_device(): received = lax.all_to_all(sent, AXES, 0, 0, tiled=True)]
    pallas_call x5 -> x8, Pallas kernels: 8.36 us -> 10.5 us  [call(): pl.pallas_call(body, out_shape=outs, in_specs=in_specs, out_specs=jax.tre...]
    unnamed x20 -> x16, local copies, waits for them, and re-layouts: 3.38 us -> 1.72 us
    all_to_all x1, waiting for transfers between devices: 6.4 us -> 5.13 us  [per_device(): received = lax.all_to_all(sent, AXES, 0, 0, tiled=True)]
    ppermute x2 -> x3, starting transfers between devices: 3.13 us -> 4.27 us  [swap(): lax.ppermute(even, axis, even_pairs(count))]
    ppermute x2 -> x3, starting transfers between devices: 1.33 us -> 1.98 us  [swap(): lax.ppermute(odd, axis, odd_pairs(count))]
    ppermute x2 -> x3, waiting for transfers between devices: 2.11 us -> 1.82 us  [swap(): lax.ppermute(even, axis, even_pairs(count))]
  transfers between devices with their start and end apart: 5 -> 7, of which waited for: 3 -> 2; matrix products, arithmetic and copies ran while one was open for 2% -> 0% of each run, Pallas kernels for 0% -> 7%
where the time goes in v4:
time: 47.3 us; the launch traced here: 47.1 us
  starting transfers between devices  18.8 us (40%)
  Pallas kernels  10.5 us (22%)
  blocking collectives  8.87 us (19%)
  waiting for transfers between devices  6.96 us (15%)
  local copies, waits for them, and re-layouts  1.72 us (4%)
    all_to_all x1, starting transfers between devices, per_device(): received = lax.all_to_all(sent, AXES, 0, 0, tiled=True)  12.5 us
    pallas_call x8, Pallas kernels, call(): pl.pallas_call(body, out_shape=outs, in_specs=in_specs, out_specs=jax.tre...  10.5 us
    all_to_all x1, blocking collectives, per_device(): received = lax.all_to_all(sent, AXES, 0, 0, tiled=True)  8.87 us
    all_to_all x1, waiting for transfers between devices, per_device(): received = lax.all_to_all(sent, AXES, 0, 0, tiled=True)  5.13 us
    ppermute x3, starting transfers between devices, swap(): lax.ppermute(even, axis, even_pairs(count))  4.27 us
    ppermute x3, starting transfers between devices, swap(): lax.ppermute(odd, axis, odd_pairs(count))  1.98 us
    ppermute x3, waiting for transfers between devices, swap(): lax.ppermute(even, axis, even_pairs(count))  1.82 us
    unnamed x16, local copies, waits for them, and re-layouts  1.72 us
  transfers between devices with their start and end apart: 7, of which 2 were waited for; matrix products, arithmetic and copies ran while one was open for 0% of the time, Pallas kernels for 7%

profile of v4, /device:TPU:0, one launch (start us, length us, event | category | flops | bytes accessed | tf_op | source)
XLA Modules:
  0.0 47.1 jit_solution(14337077341793841452)
XLA Ops:
  0.0 0.1 pad_add_fusion.place
  0.1 1.0 %copy-done = bf16[32,8,8,128]{3,2,1,0:T(8,128)(2,1)S(1)} copy-done((bf16[32,8,8,128]{3,2,1,0:T(8,128)(2,1)S(1)}, bf16[32,8,8,128]{3,2,1,0:T(8,128)(2,1)}, u32[]{:S(2)}) %copy-start) | copy-done | bytes 524312
  1.1 0.7 %copy-done.3 = s32[1,1,16]{2,1,0:T(1,128)S(1)} copy-done((s32[1,1,16]{2,1,0:T(1,128)S(1)}, s32[1,1,16]{2,1,0:T(1,128)}, u32[]{:S(2)}) %copy-start.3) | copy-done | bytes 88
  1.8 1.0 %shard_map.82 = (bf16[8,8,32,128]{3,2,1,0:T(8,128)(2,1)S(1)}, f32[1,16,128]{2,1,0:T(8,128)S(1)}, bf16[528,128]{1,0:T(8,128)(2,1)S(1)}, bf16[528,128]{1,0:T(8,128...) custom-call(s32[2]{0:T(128)S(1)} %pad_add_fusion.place, bf16[32,8,8,128]{3,2,1,0:T(8,128)(2,1)S(1)} %copy-done, ...), custom_call_target="tpu_custom_call" | custom-call | bytes 524360 | tf_op jit(solution)/shard_map/pallas_call | solution.py:38
  2.8 3.1 %collective-permute-start = (bf16[528,128]{1,0:T(8,128)(2,1)S(1)}, bf16[528,128]{1,0:T(8,128)(2,1)S(1)}, u32[]{:S(2)}, u32[]{:S(2)}) collective-permute-start(bf16[528,128]{1,0:T(8,128)(2,1)S(1)} %get-tuple-element.25), channel_id=1, source_target_pairs={{0,4},{4,0},{8,12},{12,8},{16,20},{20,16},{24,28},{28,24},{1,5},{5... | collective-permute-start | bytes 405512 | tf_op jit(solution)/shard_map/ppermute | solution.py:29
  5.9 0.7 %collective-permute-start.1 = (bf16[528,128]{1,0:T(8,128)(2,1)S(1)}, bf16[528,128]{1,0:T(8,128)(2,1)S(1)}, u32[]{:S(2)}, u32[]{:S(2)}) collective-permute-start(bf16[528,128]{1,0:T(8,128)(2,1)S(1)} %get-tuple-element.26), channel_id=1, source_target_pairs={{4,8},{12,16},{20,24},{8,4},{16,12},{24,20},{5,9},{13,17},{21,25},... | collective-permute-start | bytes 405512 | tf_op jit(solution)/shard_map/ppermute | solution.py:29
  6.6 0.1 collective-permute-start.2
  6.6 0.7 %collective-permute-start.3 = (bf16[528,128]{1,0:T(8,128)(2,1)S(1)}, bf16[528,128]{1,0:T(8,128)(2,1)S(1)}, u32[]{:S(2)}, u32[]{:S(2)}) collective-permute-start(bf16[528,128]{1,0:T(8,128)(2,1)S(1)} %get-tuple-element.28), channel_id=1, source_target_pairs={{1,2},{2,1},{5,6},{6,5},{9,10},{10,9},{13,14},{14,13},{17,18},{18,... | collective-permute-start | bytes 405512 | tf_op jit(solution)/shard_map/ppermute | solution.py:29
  7.3 0.3 shard_map.83.filled
  7.7 1.8 %collective-permute-done.x_even.refs_0_ = bf16[528,128]{1,0:T(8,128)(2,1)S(1)} collective-permute-done((bf16[528,128]{1,0:T(8,128)(2,1)S(1)}, bf16[528,128]{1,0:T(8,128)(2,1)S(1)}, u32[]{:S(2)}, u32[]{:S(2)}) %collective-permute-start) | collective-permute-done | bytes 135200 | tf_op jit(solution)/shard_map/ppermute | solution.py:29
  9.5 0.0 collective-permute-done.1.x_odd.refs_1_
  9.5 0.6 %shard_map.84 = (bf16[288,128]{1,0:T(8,128)(2,1)S(1)}, bf16[288,128]{1,0:T(8,128)(2,1)S(1)}) custom-call(s32[2]{0:T(128)S(1)} %pad_add_fusion.place, bf16[528,128]{1,0:T(8,128)(2,1)S(1)} %collective-permute-done.x_even.refs_0_, bf16[528,128]{1,0:T(8,128)(2,1)S(1)} %collective-permute-done.1.x_odd.refs_1_), custom_call_target="tpu_custom_call" | custom-call | bytes 270344 | tf_op jit(solution)/shard_map/pallas_call | solution.py:38
  10.1 1.1 %collective-permute-start.4 = (bf16[288,128]{1,0:T(8,128)(2,1)S(1)}, bf16[288,128]{1,0:T(8,128)(2,1)S(1)}, u32[]{:S(2)}, u32[]{:S(2)}) collective-permute-start(bf16[288,128]{1,0:T(8,128)(2,1)S(1)} %get-tuple-element.29), channel_id=1, source_target_pairs={{0,1},{1,0},{2,3},{3,2},{4,5},{5,4},{6,7},{7,6},{8,9},{9,8},{10,11... | collective-permute-start | bytes 221192 | tf_op jit(solution)/shard_map/ppermute | solution.py:29
  11.2 0.7 %collective-permute-start.5 = (bf16[288,128]{1,0:T(8,128)(2,1)S(1)}, bf16[288,128]{1,0:T(8,128)(2,1)S(1)}, u32[]{:S(2)}, u32[]{:S(2)}) collective-permute-start(bf16[288,128]{1,0:T(8,128)(2,1)S(1)} %get-tuple-element.30), channel_id=1, source_target_pairs={{1,2},{2,1},{5,6},{6,5},{9,10},{10,9},{13,14},{14,13},{17,18},{18,... | collective-permute-start | bytes 221192 | tf_op jit(solution)/shard_map/ppermute | solution.py:29
  11.9 0.5 shard_map.85
  12.4 0.0 collective-permute-done.3.refs_3_
  12.4 0.0 collective-permute-done.5.refs_5_
  12.4 2.8 %shard_map.86 = (bf16[1152,1536]{1,0:T(8,128)(2,1)S(1)}, bf16[256,1024]{1,0:T(8,128)(2,1)S(1)}, f32[3,3,8,128]{3,2,1,0:T(8,128)S(1)}, f32[32,128]{1,0:T(8,128)}) custom-call(s32[2]{0:T(128)S(1)} %pad_add_fusion.place, bf16[1152,1536]{1,0:T(8,128)(2,1)S(1)} %shard_map.83.filled, ...), custom_call_target="tpu_custom_call", output_to_operand_aliasing={{0}: (1, {})} | custom-call | bytes 4677640 | tf_op jit(solution)/shard_map/pallas_call | solution.py:38
  15.2 12.5 %all-to-all-start = ((f32[32,1,128]{2,1,0:T(1,128)}), f32[32,1,128]{2,1,0:T(1,128)S(1)}, u32[]{:S(2)}, u32[]{:S(2)}) async-start(f32[32,1,128]{2,1,0:T(1,128)} %bitcast.8), calls=%async_computation | async-start | bytes 32768 | tf_op jit(solution)/shard_map/all_to_all | solution.py:453
  27.7 2.0 %shard_map.87 = (bf16[64,1280]{1,0:T(8,128)(2,1)S(1)}, bf16[256,256]{1,0:T(8,128)(2,1)S(1)}) custom-call(s32[2]{0:T(128)S(1)} %pad_add_fusion.place, bf16[8,8,32,128]{3,2,1,0:T(8,128)(2,1)S(1)} %get-tuple-element.23.own, bf16[528,128]{1,0:T(8,128)(2,1)S(1)} %collective-permute-done.x_even.refs_0_, bf16[528,128]{1,0:T(8,128)(2,1)S(1)} %collective-permute-done.1.x_odd.refs_1_, ...), custom_call_target="tpu_custom_call" | custom-call | bytes 1691656 | tf_op jit(solution)/shard_map/pallas_call | solution.py:38
  29.7 5.1 %all-to-all-done = f32[32,1,128]{2,1,0:T(1,128)S(1)} async-done(((f32[32,1,128]{2,1,0:T(1,128)}), f32[32,1,128]{2,1,0:T(1,128)S(1)}, u32[]{:S(2)}, u32[]{:S(2)}) %all-to-all-start) | async-done | bytes 16416 | tf_op jit(solution)/shard_map/all_to_all | solution.py:453
  34.8 2.0 %shard_map.88 = (bf16[256,1024]{1,0:T(8,128)(2,1)S(1)}, f32[32,128]{1,0:T(8,128)S(1)}) custom-call(bf16[256,1024]{1,0:T(8,128)(2,1)S(1)} %get-tuple-element.32.first_out, bf16[64,1280]{1,0:T(8,128)(2,1)S(1)} %get-tuple-element.34.ring_y, bf16[256,256]{1,0:T(8,128)(2,1)S(1)} %get-tuple-element.35.ring_x, ...), custom_call_target="tpu_custom_call" | custom-call | bytes 1380352 | tf_op jit(solution)/shard_map/pallas_call | solution.py:38
  36.8 8.9 %all_to_all.22 = f32[32,1,128]{2,1,0:T(1,128)S(1)} all-to-all(f32[32,1,128]{2,1,0:T(1,128)S(1)} %bitcast.17), channel_id=1, replica_groups=mesh['region'=8,'strip'=4] {'region','strip'}, dimensions={0} | all-to-all | bytes 32768 | tf_op jit(solution)/shard_map/all_to_all | solution.py:473
  45.7 1.4 %shard_map.89 = bf16[32,8,8,128]{3,2,1,0:T(8,128)(2,1)} custom-call(bf16[256,1024]{1,0:T(8,128)(2,1)S(1)} %get-tuple-element.39.second_out, f32[3,3,8,128]{3,2,1,0:T(8,128)S(1)} %get-tuple-element.33.refs_7_.wide_masks, f32[32,128]{1,0:T(8,128)S(1)} %bitcast.16, f32[4,32,128]{2,1,0:T(8,128)S(1)} %get-tuple-element.37.params, ...), custom_call_target="tpu_custom_call" | custom-call | bytes 1167360 | tf_op jit(solution)/shard_map/pallas_call | solution.py:38
  (17 shorter events, 0.0 us)
Async XLA Ops:
  0.0 11.8 %copy-start.4 = (f32[32]{0:T(128)S(1)}, f32[32]{0:T(128)}, u32[]{:S(2)}) copy-start(f32[32]{0:T(128)} %param.15) | copy-start | bytes 388
  0.0 11.8 %copy-start.5 = (f32[32]{0:T(128)S(1)}, f32[32]{0:T(128)}, u32[]{:S(2)}) copy-start(f32[32]{0:T(128)} %param.14) | copy-start | bytes 388
  0.0 11.8 %copy-start.6 = (f32[32]{0:T(128)S(1)}, f32[32]{0:T(128)}, u32[]{:S(2)}) copy-start(f32[32]{0:T(128)} %param.13) | copy-start | bytes 388
  0.0 11.9 %copy-start.7 = (f32[32]{0:T(128)S(1)}, f32[32]{0:T(128)}, u32[]{:S(2)}) copy-start(f32[32]{0:T(128)} %param.12) | copy-start | bytes 388
  0.1 1.0 %copy-start = (bf16[32,8,8,128]{3,2,1,0:T(8,128)(2,1)S(1)}, bf16[32,8,8,128]{3,2,1,0:T(8,128)(2,1)}, u32[]{:S(2)}) copy-start(bf16[32,8,8,128]{3,2,1,0:T(8,128)(2,1)} %features.1) | copy-start | bytes 1572868
  1.1 0.7 %copy-start.3 = (s32[1,1,16]{2,1,0:T(1,128)S(1)}, s32[1,1,16]{2,1,0:T(1,128)}, u32[]{:S(2)}) copy-start(s32[1,1,16]{2,1,0:T(1,128)} %param.9) | copy-start | bytes 196
  1.8 10.1 %copy-start.1 = (bf16[3,3,3,32,32]{4,3,2,1,0:T(8,128)(2,1)S(1)}, bf16[3,3,3,32,32]{4,3,2,1,0:T(8,128)(2,1)}, u32[]{:S(2)}) copy-start(bf16[3,3,3,32,32]{4,3,2,1,0:T(8,128)(2,1)} %weights_first.1) | copy-start | bytes 165892
  1.8 10.1 %copy-start.2 = (bf16[3,3,3,32,32]{4,3,2,1,0:T(8,128)(2,1)S(1)}, bf16[3,3,3,32,32]{4,3,2,1,0:T(8,128)(2,1)}, u32[]{:S(2)}) copy-start(bf16[3,3,3,32,32]{4,3,2,1,0:T(8,128)(2,1)} %weights_second.1) | copy-start | bytes 165892
  2.8 6.7 %collective-permute-start = (bf16[528,128]{1,0:T(8,128)(2,1)S(1)}, bf16[528,128]{1,0:T(8,128)(2,1)S(1)}, u32[]{:S(2)}, u32[]{:S(2)}) collective-permute-start(bf16[528,128]{1,0:T(8,128)(2,1)S(1)} %get-tuple-element.25), channel_id=1, source_target_pairs={{0,4},{4,0},{8,12},{12,8},{16,20},{20,16},{24,28},{28,24},{1,5},{5... | collective-permute-start | bytes 405512 | tf_op jit(solution)/shard_map/ppermute | solution.py:29
  5.9 3.6 %collective-permute-start.1 = (bf16[528,128]{1,0:T(8,128)(2,1)S(1)}, bf16[528,128]{1,0:T(8,128)(2,1)S(1)}, u32[]{:S(2)}, u32[]{:S(2)}) collective-permute-start(bf16[528,128]{1,0:T(8,128)(2,1)S(1)} %get-tuple-element.26), channel_id=1, source_target_pairs={{4,8},{12,16},{20,24},{8,4},{16,12},{24,20},{5,9},{13,17},{21,25},... | collective-permute-start | bytes 405512 | tf_op jit(solution)/shard_map/ppermute | solution.py:29
  6.6 5.8 %collective-permute-start.2 = (bf16[528,128]{1,0:T(8,128)(2,1)S(1)}, bf16[528,128]{1,0:T(8,128)(2,1)S(1)}, u32[]{:S(2)}, u32[]{:S(2)}) collective-permute-start(bf16[528,128]{1,0:T(8,128)(2,1)S(1)} %get-tuple-element.27), channel_id=1, source_target_pairs={{0,1},{1,0},{2,3},{3,2},{4,5},{5,4},{6,7},{7,6},{8,9},{9,8},{10,11... | collective-permute-start | bytes 405512 | tf_op jit(solution)/shard_map/ppermute | solution.py:29
  6.6 5.8 %collective-permute-start.3 = (bf16[528,128]{1,0:T(8,128)(2,1)S(1)}, bf16[528,128]{1,0:T(8,128)(2,1)S(1)}, u32[]{:S(2)}, u32[]{:S(2)}) collective-permute-start(bf16[528,128]{1,0:T(8,128)(2,1)S(1)} %get-tuple-element.28), channel_id=1, source_target_pairs={{1,2},{2,1},{5,6},{6,5},{9,10},{10,9},{13,14},{14,13},{17,18},{18,... | collective-permute-start | bytes 405512 | tf_op jit(solution)/shard_map/ppermute | solution.py:29
  10.1 2.3 %collective-permute-start.4 = (bf16[288,128]{1,0:T(8,128)(2,1)S(1)}, bf16[288,128]{1,0:T(8,128)(2,1)S(1)}, u32[]{:S(2)}, u32[]{:S(2)}) collective-permute-start(bf16[288,128]{1,0:T(8,128)(2,1)S(1)} %get-tuple-element.29), channel_id=1, source_target_pairs={{0,1},{1,0},{2,3},{3,2},{4,5},{5,4},{6,7},{7,6},{8,9},{9,8},{10,11... | collective-permute-start | bytes 221192 | tf_op jit(solution)/shard_map/ppermute | solution.py:29
  11.2 1.2 %collective-permute-start.5 = (bf16[288,128]{1,0:T(8,128)(2,1)S(1)}, bf16[288,128]{1,0:T(8,128)(2,1)S(1)}, u32[]{:S(2)}, u32[]{:S(2)}) collective-permute-start(bf16[288,128]{1,0:T(8,128)(2,1)S(1)} %get-tuple-element.30), channel_id=1, source_target_pairs={{1,2},{2,1},{5,6},{6,5},{9,10},{10,9},{13,14},{14,13},{17,18},{18,... | collective-permute-start | bytes 221192 | tf_op jit(solution)/shard_map/ppermute | solution.py:29
  15.2 19.6 %all-to-all-start = ((f32[32,1,128]{2,1,0:T(1,128)}), f32[32,1,128]{2,1,0:T(1,128)S(1)}, u32[]{:S(2)}, u32[]{:S(2)}) async-start(f32[32,1,128]{2,1,0:T(1,128)} %bitcast.8), calls=%async_computation | async-start | bytes 32768 | tf_op jit(solution)/shard_map/all_to_all | solution.py:453

commit v5 on v3

v5 whole, which is shorter than its diff:
```python
import functools

import jax
import jax.numpy as jnp
from jax import lax
from jax.experimental import pallas as pl
from jax.experimental.pallas import tpu as pltpu
from jax.sharding import PartitionSpec as P

BRICK = 8
EPSILON = 1e-05
HALO = 2
AXES = ("region", "strip")
F32 = jnp.float32
BF16 = jnp.bfloat16


def even_pairs(count):
    return [(i, i ^ 1) for i in range(count) if (i ^ 1) < count]


def odd_pairs(count):
    pairs = [(i, i + 1) for i in range(1, count - 1, 2)]
    return pairs + [(b, a) for a, b in pairs]


def swap(even, odd, axis):
    count = lax.axis_size(axis)
    return lax.ppermute(even, axis, even_pairs(count)), lax.ppermute(odd, axis, odd_pairs(count))


def call(body, outs, ins, scratch=(), far=(), far_out=False):
    def space(is_far):
        return pl.BlockSpec(memory_space=pltpu.HBM if is_far else pltpu.VMEM)

    return pl.pallas_call(
        body,
        out_shape=outs,
        in_specs=[space(i in far) for i in range(len(ins))],
        out_specs=jax.tree.map(lambda _: space(far_out), outs),
        scratch_shapes=list(scratch),
        compiler_params=pltpu.CompilerParams(vmem_limit_bytes=16 << 20),
        cost_estimate=pl.CostEstimate(
            flops=0,
            transcendentals=0,
            bytes_accessed=sum(a.size * a.dtype.itemsize for a in ins),
        ),
    )(*ins)


def is_even(axis):
    return lax.rem(lax.axis_index(axis), 2) == 0


def brick_rows(bricks, depth):
    count = bricks.shape[1]
    at = lax.broadcasted_iota(jnp.int32, (count, depth), 0)
    voxel = lax.broadcasted_iota(jnp.int32, (count, depth), 1)
    spread = (voxel // BRICK == at).astype(F32)
    return jnp.dot(bricks, spread, preferred_element_type=F32)


def sides(even_place, even, odd):
    return ((even, jnp.where(even_place, 0, 1)), (odd, jnp.where(even_place, 1, 0)))


def gather_kernel(dims, features, bricks, *refs):
    own, masks, x_even, x_odd, y_even, y_odd, raw, flags, turned, arrived, flags_arrived = refs
    channels, extent_x, extent_y, depth, bx, by = dims
    flag_copy = pltpu.make_async_copy(bricks, flags, flags_arrived)
    flag_copy.start()
    copies = []
    for x in range(0, extent_x, 2):
        copy = pltpu.make_async_copy(
            features.at[:, x : x + 2], raw.at[:, x : x + 2], arrived.at[x // 2]
        )
        copy.start()
        copies.append(copy)
    flag_copy.wait()
    rows = brick_rows(flags[...].astype(F32), depth)
    for i in range(bx * by):
        masks[i] = jnp.broadcast_to(rows[i : i + 1], (16, depth))
    for x in range(extent_x):
        if x % 2 == 0:
            copies[x // 2].wait()
        for j in range(by):
            part = raw[:, x, j * BRICK : (j + 1) * BRICK, :].astype(F32)
            part = part * masks[x // BRICK * by + j][None, :BRICK, :]
            turned[x % 2] = part.reshape(channels * BRICK, depth)
            for y in range(BRICK):
                own[x, j * BRICK + y] = turned[x % 2, pl.ds(y, channels, stride=BRICK), :].astype(
                    BF16
                )
    for out, low in sides(is_even("region"), x_even, x_odd):
        start = jnp.where(low == 1, 0, extent_x - HALO)
        for i in range(HALO):
            for y in range(extent_y):
                at = (i * extent_y + y) * channels
                out[at : at + channels, :] = own[start + i, y]
        base = HALO * extent_y * channels
        for j in range(by):
            tile = masks[jnp.where(low == 1, 0, bx - 1) * by + j]
            out[base + 16 * j : base + 16 * (j + 1), :] = tile.astype(BF16)
    for out, low in sides(is_even("strip"), y_even, y_odd):
        start = jnp.where(low == 1, 0, extent_y - HALO)
        for x in range(extent_x):
            for j in range(HALO):
                at = (x * HALO + j) * channels
                out[at : at + channels, :] = own[x, start + j]
        base = extent_x * HALO * channels
        for i in range(bx):
            tile = masks[i * by + jnp.where(low == 1, 0, by - 1)]
            out[base + 16 * i : base + 16 * (i + 1), :] = tile.astype(BF16)


def corner_kernel(dims, x_even, x_odd, even, odd):
    channels, extent_x, extent_y, depth, bx, by = dims
    first_x = is_even("region")
    base = HALO * extent_y * channels
    for out, low in sides(is_even("strip"), even, odd):
        start = jnp.where(low == 1, 0, extent_y - HALO)
        brick = jnp.where(low == 1, 0, by - 1)
        half = HALO * HALO * channels
        for i in range(HALO):
            for j in range(HALO):
                at = pl.multiple_of((i * extent_y + start + j) * channels, channels)
                a = x_even[pl.ds(at, channels), :]
                b = x_odd[pl.ds(at, channels), :]
                to = (i * HALO + j) * channels
                out[to : to + channels, :] = jnp.where(first_x, b, a)
                out[half + to : half + to + channels, :] = jnp.where(first_x, a, b)
        at = pl.multiple_of(base + brick * 16, 16)
        a = x_even[pl.ds(at, 16), :]
        b = x_odd[pl.ds(at, 16), :]
        out[2 * half : 2 * half + 16, :] = jnp.where(first_x, b, a)
        out[2 * half + 16 : 2 * half + 32, :] = jnp.where(first_x, a, b)


def prepare_kernel(weights_first, weights_second, rows, first_band, second_band, params):
    for weights, band in ((weights_first, first_band), (weights_second, second_band)):
        fan_in, fan_out = weights.shape[3:]
        wide = 4 * fan_in
        blank = jnp.zeros((fan_out, wide), BF16)
        for dz in range(3):
            pieces = []
            for dx in range(3):
                part = jnp.concatenate([weights[dx, dy, dz].astype(F32) for dy in range(3)], axis=0)
                part = jnp.concatenate([part, jnp.zeros((fan_in, fan_out), F32)], axis=0)
                part = jnp.concatenate([part, jnp.zeros((wide, 128 - fan_out), F32)], axis=1)
                part = jnp.transpose(part)[:fan_out]
                pieces.append((part.astype(BF16), pltpu.roll(part, fan_in, 1).astype(BF16)))
            for x in range(2):
                for y in range(2):
                    at = ((dz * 2 + x) * 2 + y) * fan_out
                    for i in range(4):
                        piece = pieces[i - x][y] if 0 <= i - x < 3 else blank
                        band[at : at + fan_out, i * wide : (i + 1) * wide] = piece
    channels = rows.shape[1]
    for i in range(4):
        row = jnp.concatenate([rows[i : i + 1, :], jnp.zeros((1, 128 - channels), F32)], axis=1)
        params[i] = jnp.transpose(jnp.broadcast_to(row, (128, 128)))[:channels]


def convolve_groups(groups, column, band, channels, depth, emit):
    lane = lax.broadcasted_iota(jnp.int32, (channels, depth), 1)
    at_start, at_end = lane == 0, lane == depth - 1
    for i in range(0, len(groups), 2):
        pair = groups[i : i + 2]
        windows = []
        for x, y in pair:
            parts = [column(x + a - 1, y + b - 1) for a in range(4) for b in range(4)]
            windows.append(jnp.concatenate(parts, axis=0))
        window = jnp.concatenate(windows, axis=1) if len(windows) > 1 else windows[0]
        total = jnp.dot(band[...], window, preferred_element_type=F32)
        for n, (x, y) in enumerate(pair):
            for a in range(2):
                for b in range(2):
                    before, here, after = (
                        total[
                            ((dz * 2 + a) * 2 + b) * channels : ((dz * 2 + a) * 2 + b + 1)
                            * channels,
                            n * depth : (n + 1) * depth,
                        ]
                        for dz in range(3)
                    )
                    before = jnp.where(at_start, 0.0, pltpu.roll(before, 1, 1))
                    after = jnp.where(at_end, 0.0, pltpu.roll(after, depth - 1, 1))
                    emit(x + a, y + b, here + before + after)


def send_stats(out, channels, sums, squares, counts):
    depth = sums.shape[1]
    rest = jnp.zeros((128 - 2 * channels - counts.shape[0], depth), F32)
    table = jnp.concatenate([sums, squares, counts, rest], axis=0)
    row = jnp.sum(jnp.transpose(table), axis=0, keepdims=True)
    out[...] = jnp.broadcast_to(row, out.shape)


def affine(stats, gain, channels, depth):
    row = jnp.sum(stats[...], axis=0, keepdims=True)
    table = jnp.transpose(jnp.broadcast_to(row, (128, 128)))
    total = jnp.sum(table[2 * channels : 2 * channels + BRICK], axis=0, keepdims=True)
    average = table[:channels] / total
    variance = table[channels : 2 * channels] / total - average * average
    return average, lax.rsqrt(variance + EPSILON) * gain


class Edges:
    def __init__(self, dims, own, masks, x_pair, y_pair, corner_pair=None):
        self.dims = dims
        self.own, self.masks = own, masks
        self.x_pair, self.y_pair, self.corner_pair = x_pair, y_pair, corner_pair
        self.first_x, self.first_y = is_even("region"), is_even("strip")

    def pick(self, pair, first, low, at, rows):
        even, odd = (ref[at : at + rows, :] for ref in pair)
        return jnp.where(first, odd, even) if low else jnp.where(first, even, odd)

    def column(self, x, y):
        channels, extent_x, extent_y = self.dims[:3]
        inside_x, inside_y = 0 <= x < extent_x, 0 <= y < extent_y
        if inside_x and inside_y:
            return self.own[x, y]
        i = x + HALO if x < 0 else x - extent_x
        j = y + HALO if y < 0 else y - extent_y
        if inside_y:
            at = (i * extent_y + y) * channels
            return self.pick(self.x_pair, self.first_x, x < 0, at, channels)
        if inside_x:
            at = (x * HALO + j) * channels
            return self.pick(self.y_pair, self.first_y, y < 0, at, channels)
        at = ((int(x > 0) * HALO + i) * HALO + j) * channels
        return self.pick(self.corner_pair, self.first_y, y < 0, at, channels)

    def mask(self, i, j):
        channels, extent_x, extent_y, depth, bx, by = self.dims
        inside_x, inside_y = 0 <= i < bx, 0 <= j < by
        if inside_x and inside_y:
            return self.masks[i * by + j][:BRICK]
        if inside_y:
            at = HALO * extent_y * channels + 16 * j
            tile = self.pick(self.x_pair, self.first_x, i < 0, at, 16)
        elif inside_x:
            at = HALO * extent_x * channels + 16 * i
            tile = self.pick(self.y_pair, self.first_y, j < 0, at, 16)
        else:
            at = 2 * HALO * HALO * channels + 16 * int(i > 0)
            tile = self.pick(self.corner_pair, self.first_y, j < 0, at, 16)
        return tile.astype(F32)[:BRICK]


class Sums:
    def __init__(self, sums, squares):
        self.sums, self.squares = sums, squares

    def add(self, value):
        value = value.astype(F32)
        self.sums = self.sums + value
        self.squares = self.squares + value * value


def ring_groups(extent_x, extent_y):
    far = (extent_x - 1, extent_y - 1)
    groups = [(x, y) for x in range(-1, extent_x, 2) for y in range(-1, extent_y, 2)]
    corners = [g for g in groups if g[0] in (-1, far[0]) and g[1] in (-1, far[1])]
    return [g for g in groups if g not in corners], corners


def first_kernel(dims, own, masks, x_even, x_odd, y_even, y_odd, band, first_out, partial):
    channels, extent_x, extent_y, depth, bx, by = dims
    edges = Edges(dims, own, masks, (x_even, x_odd), (y_even, y_odd))
    found = {}
    zero = jnp.zeros((channels, depth), F32)
    sums = Sums(zero, zero)

    def emit(x, y, value):
        brick = (x // BRICK, y // BRICK)
        if brick not in found:
            found[brick] = edges.mask(*brick)[:1]
        value = (value * found[brick]).astype(BF16)
        first_out[x + 1, y + 1] = value
        if 0 <= x < extent_x and 0 <= y < extent_y:
            sums.add(value)

    groups = ring_groups(extent_x, extent_y)[0]
    convolve_groups(groups, edges.column, band, channels, depth, emit)
    partial[0] = sums.sums
    partial[1] = sums.squares


def finish_kernel(dims, own, masks, *refs):
    x_even, x_odd, y_even, y_odd, c_even, c_odd, band, partial, corner_out, wide_masks, stats = refs
    channels, extent_x, extent_y, depth, bx, by = dims
    edges = Edges(dims, own, masks, (x_even, x_odd), (y_even, y_odd), (c_even, c_odd))
    counts = jnp.zeros((BRICK, depth), F32)
    for i in range(-1, bx + 1):
        for j in range(-1, by + 1):
            tile = edges.mask(i, j)
            wide_masks[i + 1, j + 1] = tile
            if 0 <= i < bx and 0 <= j < by:
                counts = counts + tile * float(BRICK)
    sums = Sums(partial[0], partial[1])

    def emit(x, y, value):
        value = (value * edges.mask(x // BRICK, y // BRICK)[:1]).astype(BF16)
        side_x, side_y = int(x > 0 and x >= extent_x - 1), int(y > 0 and y >= extent_y - 1)
        i = x - (extent_x - 1 if side_x else -1)
        j = y - (extent_y - 1 if side_y else -1)
        corner_out[2 * side_x + i, 2 * side_y + j] = value
        if 0 <= x < extent_x and 0 <= y < extent_y:
            sums.add(value)

    groups = ring_groups(extent_x, extent_y)[1]
    convolve_groups(groups, edges.column, band, channels, depth, emit)
    send_stats(stats, channels, sums.sums, sums.squares, counts)


def second_kernel(dims, *refs):
    first_out, corner_out, wide_masks, received, params, band, second_out, stats, field = refs
    channels, extent_x, extent_y, depth, bx, by = dims
    average, scale = affine(received, params[0], channels, depth)
    shift = params[1]
    edge_x, edge_y = (0, 1, extent_x, extent_x + 1), (0, 1, extent_y, extent_y + 1)
    for x in range(extent_x + 2):
        for y in range(extent_y + 2):
            if x in edge_x and y in edge_y:
                part = corner_out[edge_x.index(x), edge_y.index(y)]
            else:
                part = first_out[x, y]
            mask = wide_masks[(x - 1) // BRICK + 1, (y - 1) // BRICK + 1][:1]
            part = jnp.maximum((part.astype(F32) - average) * scale + shift, 0.0) * mask
            field[x, y] = part.astype(BF16)
    zero = jnp.zeros((channels, depth), F32)
    sums = Sums(zero, zero)

    def emit(x, y, value):
        value = (value * wide_masks[x // BRICK + 1, y // BRICK + 1][:1]).astype(BF16)
        second_out[x, y] = value
        sums.add(value)

    groups = [(x, y) for x in range(0, extent_x, 2) for y in range(0, extent_y, 2)]
    convolve_groups(
        groups, lambda x, y: field[x + 1, y + 1], band, channels, depth, emit
    )
    counts = jnp.zeros((BRICK, depth), F32)
    for i in range(bx):
        for j in range(by):
            counts = counts + wide_masks[1 + i, 1 + j] * float(BRICK)
    send_stats(stats, channels, sums.sums, sums.squares, counts)


def last_kernel(dims, second_out, wide_masks, received, params, own, result, turned, ready, sent):
    channels, extent_x, extent_y, depth, bx, by = dims
    average, scale = affine(received, params[2], channels, depth)
    shift = params[3]
    copies = []
    for x in range(extent_x):
        for j in range(by):
            mask = wide_masks[x // BRICK + 1, j + 1][:1]
            for y in range(BRICK):
                at = j * BRICK + y
                part = second_out[x, at].astype(F32)
                part = (part - average) * scale + shift + own[x, at].astype(F32)
                part = jnp.maximum(part, 0.0) * mask
                turned[x % 2, pl.ds(y, channels, stride=BRICK), :] = part
            ready[:, x, j * BRICK : (j + 1) * BRICK, :] = (
                turned[x % 2].reshape(channels, BRICK, depth).astype(BF16)
            )
        if x % 2 == 1:
            copy = pltpu.make_async_copy(
                ready.at[:, x - 1 : x + 1], result.at[:, x - 1 : x + 1], sent.at[x // 2]
            )
            copy.start()
            copies.append(copy)
    for copy in copies:
        copy.wait()


def per_device(
    features,
    brick_mask,
    conv_first,
    conv_second,
    gain_first,
    shift_first,
    gain_second,
    shift_second,
):
    channels, extent_x, extent_y, depth = features.shape
    bx, by, bz = brick_mask.shape
    dims = (channels, extent_x, extent_y, depth, bx, by)
    devices = lax.axis_size(AXES)
    shape = jax.ShapeDtypeStruct

    x_rows = HALO * extent_y * channels + 16 * by
    y_rows = HALO * extent_x * channels + 16 * bx
    c_rows = 2 * HALO * HALO * channels + 32
    own, masks, x_even, x_odd, y_even, y_odd = call(
        functools.partial(gather_kernel, dims),
        (
            shape((extent_x, extent_y, channels, depth), BF16),
            shape((bx * by, 16, depth), F32),
            shape((x_rows, depth), BF16),
            shape((x_rows, depth), BF16),
            shape((y_rows, depth), BF16),
            shape((y_rows, depth), BF16),
        ),
        (
            pltpu.with_memory_space_constraint(features, pltpu.HBM),
            pltpu.with_memory_space_constraint(brick_mask.reshape(bx * by, bz), pltpu.HBM),
        ),
        scratch=[
            pltpu.VMEM(features.shape, BF16),
            pltpu.VMEM((bx * by, bz), jnp.int32),
            pltpu.VMEM((2, channels * BRICK, depth), F32),
            pltpu.SemaphoreType.DMA((extent_x // 2,)),
            pltpu.SemaphoreType.DMA,
        ],
        far=(0, 1),
    )
    x_pair = swap(x_even, x_odd, "region")
    y_pair = swap(y_even, y_odd, "strip")
    corners = call(
        functools.partial(corner_kernel, dims),
        (shape((c_rows, depth), BF16), shape((c_rows, depth), BF16)),
        x_pair,
    )
    c_pair = swap(*corners, "strip")

    band_shape = shape((12 * channels, 16 * channels), BF16)
    first_band, second_band, params = call(
        prepare_kernel,
        (band_shape, band_shape, shape((4, channels, depth), F32)),
        (
            conv_first,
            conv_second,
            jnp.stack([gain_first, shift_first, gain_second, shift_second]),
        ),
    )
    wide_shape = (extent_x + 2, extent_y + 2, channels, depth)
    first_out, partial = call(
        functools.partial(first_kernel, dims),
        (shape(wide_shape, BF16), shape((2, channels, depth), F32)),
        (own, masks, *x_pair, *y_pair, first_band),
    )
    corner_out, wide_masks, sent = call(
        functools.partial(finish_kernel, dims),
        (
            shape((4, 4, channels, depth), BF16),
            shape((bx + 2, by + 2, BRICK, depth), F32),
            shape((devices, 128), F32),
        ),
        (own, masks, *x_pair, *y_pair, *c_pair, first_band, partial),
    )
    received = lax.all_to_all(sent, AXES, 0, 0, tiled=True)
    second_out, sent = call(
        functools.partial(second_kernel, dims),
        (
            shape((extent_x, extent_y, channels, depth), BF16),
            shape((devices, 128), F32),
        ),
        (first_out, corner_out, wide_masks, received, params, second_band),
        scratch=[pltpu.VMEM(wide_shape, BF16)],
    )
    received = lax.all_to_all(sent, AXES, 0, 0, tiled=True)
    return call(
        functools.partial(last_kernel, dims),
        shape(features.shape, BF16),
        (second_out, wide_masks, received, params, own),
        scratch=[
            pltpu.VMEM((2, channels * BRICK, depth), F32),
            pltpu.VMEM(features.shape, BF16),
            pltpu.SemaphoreType.DMA((extent_x // 2,)),
        ],
        far_out=True,
    )


def solution(mesh):
    in_specs = (
        P(None, "region", "strip", None),
        P("region", "strip", None),
        P(),
        P(),
        P(),
        P(),
        P(),
        P(),
    )
    out_specs = P(None, "region", "strip", None)
    return jax.shard_map(
        per_device, mesh=mesh, in_specs=in_specs, out_specs=out_specs, check_vma=False
    )
```

time: 49.5 us -> 42.3 us (0.85)
  blocking collectives: 8.87 us -> 26.7 us
  starting transfers between devices: 19.3 us -> 5.89 us
  waiting for transfers between devices: 8.51 us -> 2.19 us
  local copies, waits for them, and re-layouts: 3.79 us -> 0.67 us
  Pallas kernels: 8.36 us -> 6.44 us
    all_to_all x1 -> x2, blocking collectives: 8.87 us -> 26.7 us  [per_device(): received = lax.all_to_all(sent, AXES, 0, 0, tiled=True)]
    all_to_all x1 -> x0, starting transfers between devices: 14.8 us -> none  [per_device(): received = lax.all_to_all(sent, AXES, 0, 0, tiled=True)]
    all_to_all x1 -> x0, waiting for transfers between devices: 6.4 us -> none  [per_device(): received = lax.all_to_all(sent, AXES, 0, 0, tiled=True)]
    unnamed x20 -> x12, local copies, waits for them, and re-layouts: 3.38 us -> 0.67 us
    pallas_call x5 -> x7, Pallas kernels: 8.36 us -> 6.44 us  [call(): pl.pallas_call(body, out_shape=outs, in_specs=[space(i in far) for i in r...]
    ppermute x2 -> x3, starting transfers between devices: 3.13 us -> 3.91 us  [swap(): lax.ppermute(even, axis, even_pairs(count))]
    ppermute x2 -> x3, starting transfers between devices: 1.33 us -> 1.98 us  [swap(): lax.ppermute(odd, axis, odd_pairs(count))]
    ppermute x2 -> x3, waiting for transfers between devices: 2.11 us -> 2.17 us  [swap(): lax.ppermute(even, axis, even_pairs(count))]
  transfers between devices with their start and end apart: 5 -> 6, of which waited for: 3 -> 1; matrix products, arithmetic and copies ran while one was open for 2% -> 0% of each run, Pallas kernels for 0% -> 4%
where the time goes in v5:
time: 42.3 us; the launch traced here: 42.1 us
  blocking collectives  26.7 us (63%)
  Pallas kernels  6.44 us (15%)
  starting transfers between devices  5.89 us (14%)
  waiting for transfers between devices  2.19 us (5%)
  local copies, waits for them, and re-layouts  0.67 us (2%)
    all_to_all x2, blocking collectives, per_device(): received = lax.all_to_all(sent, AXES, 0, 0, tiled=True)  26.7 us
    pallas_call x7, Pallas kernels, call(): pl.pallas_call(body, out_shape=outs, in_specs=[space(i in far) for i in r...  6.44 us
    ppermute x3, starting transfers between devices, swap(): lax.ppermute(even, axis, even_pairs(count))  3.91 us
    ppermute x3, waiting for transfers between devices, swap(): lax.ppermute(even, axis, even_pairs(count))  2.17 us
    ppermute x3, starting transfers between devices, swap(): lax.ppermute(odd, axis, odd_pairs(count))  1.98 us
  transfers between devices with their start and end apart: 6, of which 1 were waited for; matrix products, arithmetic and copies ran while one was open for 0% of the time, Pallas kernels for 4%

profile of v5, /device:TPU:0, one launch (start us, length us, event | category | flops | bytes accessed | tf_op | source)
XLA Modules:
  0.0 42.1 jit_solution(6621619463699184173)
XLA Ops:
  0.0 1.4 %shard_map.82 = (bf16[8,8,32,128]{3,2,1,0:T(8,128)(2,1)S(1)}, f32[1,16,128]{2,1,0:T(8,128)S(1)}, bf16[528,128]{1,0:T(8,128)(2,1)S(1)}, bf16[528,128]{1,0:T(8,128...) custom-call(bf16[32,8,8,128]{3,2,1,0:T(8,128)(2,1)} %features.1, s32[1,16]{1,0:T(1,128)} %bitcast.17), custom_call_target="tpu_custom_call" | custom-call | bytes 524352 | tf_op jit(solution)/shard_map/pallas_call | solution.py:36
  1.4 0.0 copy-start
  1.4 3.1 %collective-permute-start = (bf16[528,128]{1,0:T(8,128)(2,1)S(1)}, bf16[528,128]{1,0:T(8,128)(2,1)S(1)}, u32[]{:S(2)}, u32[]{:S(2)}) collective-permute-start(bf16[528,128]{1,0:T(8,128)(2,1)S(1)} %get-tuple-element.25), channel_id=1, source_target_pairs={{0,4},{4,0},{8,12},{12,8},{16,20},{20,16},{24,28},{28,24},{1,5},{5... | collective-permute-start | bytes 405512 | tf_op jit(solution)/shard_map/ppermute | solution.py:29
  4.5 0.7 %collective-permute-start.1 = (bf16[528,128]{1,0:T(8,128)(2,1)S(1)}, bf16[528,128]{1,0:T(8,128)(2,1)S(1)}, u32[]{:S(2)}, u32[]{:S(2)}) collective-permute-start(bf16[528,128]{1,0:T(8,128)(2,1)S(1)} %get-tuple-element.26), channel_id=1, source_target_pairs={{4,8},{12,16},{20,24},{8,4},{16,12},{24,20},{5,9},{13,17},{21,25},... | collective-permute-start | bytes 405512 | tf_op jit(solution)/shard_map/ppermute | solution.py:29
  5.1 0.1 collective-permute-start.2
  5.2 0.7 %collective-permute-start.3 = (bf16[528,128]{1,0:T(8,128)(2,1)S(1)}, bf16[528,128]{1,0:T(8,128)(2,1)S(1)}, u32[]{:S(2)}, u32[]{:S(2)}) collective-permute-start(bf16[528,128]{1,0:T(8,128)(2,1)S(1)} %get-tuple-element.28), channel_id=1, source_target_pairs={{1,2},{2,1},{5,6},{6,5},{9,10},{10,9},{13,14},{14,13},{17,18},{18,... | collective-permute-start | bytes 405512 | tf_op jit(solution)/shard_map/ppermute | solution.py:29
  5.9 2.2 %collective-permute-done.x_even.refs_0_ = bf16[528,128]{1,0:T(8,128)(2,1)S(1)} collective-permute-done((bf16[528,128]{1,0:T(8,128)(2,1)S(1)}, bf16[528,128]{1,0:T(8,128)(2,1)S(1)}, u32[]{:S(2)}, u32[]{:S(2)}) %collective-permute-start) | collective-permute-done | bytes 135200 | tf_op jit(solution)/shard_map/ppermute | solution.py:29
  8.1 0.0 copy-start.5
  8.1 0.8 %collective-permute-start.4 = (bf16[288,128]{1,0:T(8,128)(2,1)S(1)}, bf16[288,128]{1,0:T(8,128)(2,1)S(1)}, u32[]{:S(2)}, u32[]{:S(2)}) collective-permute-start(bf16[288,128]{1,0:T(8,128)(2,1)S(1)} %get-tuple-element.31), channel_id=1, source_target_pairs={{0,1},{1,0},{2,3},{3,2},{4,5},{5,4},{6,7},{7,6},{8,9},{9,8},{10,11... | collective-permute-start | bytes 221192 | tf_op jit(solution)/shard_map/ppermute | solution.py:29
  8.9 0.7 %collective-permute-start.5 = (bf16[288,128]{1,0:T(8,128)(2,1)S(1)}, bf16[288,128]{1,0:T(8,128)(2,1)S(1)}, u32[]{:S(2)}, u32[]{:S(2)}) collective-permute-start(bf16[288,128]{1,0:T(8,128)(2,1)S(1)} %get-tuple-element.32), channel_id=1, source_target_pairs={{1,2},{2,1},{5,6},{6,5},{9,10},{10,9},{13,14},{14,13},{17,18},{18,... | collective-permute-start | bytes 221192 | tf_op jit(solution)/shard_map/ppermute | solution.py:29
  9.6 0.0 copy-start.2
  9.6 0.0 copy-start.3
  9.6 0.0 copy-start.4
  9.6 0.6 %copy-done.2 = f32[32]{0:T(128)S(1)} copy-done((f32[32]{0:T(128)S(1)}, f32[32]{0:T(128)}, u32[]{:S(2)}) %copy-start.2) | copy-done | bytes 152
  10.2 0.0 copy-done.3
  10.2 0.0 copy-done.4
  10.3 0.4 shard_map.83
  10.7 0.0 collective-permute-done.3.y_odd.refs_3_
  10.7 1.4 %shard_map.84 = (bf16[10,10,32,128]{3,2,1,0:T(8,128)(2,1)S(1)}, f32[2,32,128]{2,1,0:T(8,128)S(1)}) custom-call(bf16[8,8,32,128]{3,2,1,0:T(8,128)(2,1)S(1)} %get-tuple-element.23.own, f32[1,16,128]{2,1,0:T(8,128)S(1)} %get-tuple-element.24.masks, bf16[528,128]{1,0:T(8,128)(2,1)S(1)} %collective-permute-done.x_even.refs_0_, ...), custom_call_target="tpu_custom_call" | custom-call | bytes 1466368 | tf_op jit(solution)/shard_map/pallas_call | solution.py:36
  12.1 0.6 %shard_map.86 = (bf16[4,4,32,128]{3,2,1,0:T(8,128)(2,1)S(1)}, f32[3,3,8,128]{3,2,1,0:T(8,128)S(1)}, f32[32,128]{1,0:T(8,128)S(1)}) custom-call(bf16[8,8,32,128]{3,2,1,0:T(8,128)(2,1)S(1)} %get-tuple-element.23.own, f32[1,16,128]{2,1,0:T(8,128)S(1)} %get-tuple-element.24.masks, bf16[528,128]{1,0:T(8,128)(2,1)S(1)} %collective-permute-done.x_even.refs_0_, ...), custom_call_target="tpu_custom_call" | custom-call | bytes 1646592 | tf_op jit(solution)/shard_map/pallas_call | solution.py:36
  12.7 17.9 %all_to_all.22 = f32[32,1,128]{2,1,0:T(1,128)S(1)} all-to-all(f32[32,1,128]{2,1,0:T(1,128)S(1)} %bitcast.15), channel_id=1, replica_groups=mesh['region'=8,'strip'=4] {'region','strip'}, dimensions={0} | all-to-all | bytes 32768 | tf_op jit(solution)/shard_map/all_to_all | solution.py:455
  30.6 1.4 %shard_map.87 = (bf16[8,8,32,128]{3,2,1,0:T(8,128)(2,1)S(1)}, f32[32,128]{1,0:T(8,128)S(1)}) custom-call(bf16[10,10,32,128]{3,2,1,0:T(8,128)(2,1)S(1)} %get-tuple-element.30.refs_0_, bf16[4,4,32,128]{3,2,1,0:T(8,128)(2,1)S(1)} %get-tuple-element.34.refs_1_, f32[3,3,8,128]{3,2,1,0:T(8,128)S(1)} %get-tuple-element.35.refs_2_.wide_masks, ...), custom_call_target="tpu_custom_call" | custom-call | bytes 1462272 | tf_op jit(solution)/shard_map/pallas_call | solution.py:36
  32.0 8.9 %all_to_all.23 = f32[32,1,128]{2,1,0:T(1,128)S(1)} all-to-all(f32[32,1,128]{2,1,0:T(1,128)S(1)} %bitcast.16), channel_id=1, replica_groups=mesh['region'=8,'strip'=4] {'region','strip'}, dimensions={0} | all-to-all | bytes 32768 | tf_op jit(solution)/shard_map/all_to_all | solution.py:465
  40.9 1.2 %shard_map.88 = bf16[32,8,8,128]{3,2,1,0:T(8,128)(2,1)} custom-call(bf16[8,8,32,128]{3,2,1,0:T(8,128)(2,1)S(1)} %get-tuple-element.39.second_out, f32[3,3,8,128]{3,2,1,0:T(8,128)S(1)} %get-tuple-element.35.refs_2_.wide_masks, f32[32,128]{1,0:T(8,128)S(1)} %bitcast.14, f32[4,32,128]{2,1,0:T(8,128)S(1)} %get-tuple-element.37.refs_4_.params, ...), custom_call_target="tpu_custom_call" | custom-call | bytes 1167360 | tf_op jit(solution)/shard_map/pallas_call | solution.py:36
  (10 shorter events, 0.1 us)
Async XLA Ops:
  0.0 10.3 %copy-start.1 = (bf16[3,3,3,32,32]{4,3,2,1,0:T(8,128)(2,1)S(1)}, bf16[3,3,3,32,32]{4,3,2,1,0:T(8,128)(2,1)}, u32[]{:S(2)}) copy-start(bf16[3,3,3,32,32]{4,3,2,1,0:T(8,128)(2,1)} %weights_second.1) | copy-start | bytes 165892
  1.4 8.9 %copy-start = (bf16[3,3,3,32,32]{4,3,2,1,0:T(8,128)(2,1)S(1)}, bf16[3,3,3,32,32]{4,3,2,1,0:T(8,128)(2,1)}, u32[]{:S(2)}) copy-start(bf16[3,3,3,32,32]{4,3,2,1,0:T(8,128)(2,1)} %weights_first.1) | copy-start | bytes 165892
  1.4 6.6 %collective-permute-start = (bf16[528,128]{1,0:T(8,128)(2,1)S(1)}, bf16[528,128]{1,0:T(8,128)(2,1)S(1)}, u32[]{:S(2)}, u32[]{:S(2)}) collective-permute-start(bf16[528,128]{1,0:T(8,128)(2,1)S(1)} %get-tuple-element.25), channel_id=1, source_target_pairs={{0,4},{4,0},{8,12},{12,8},{16,20},{20,16},{24,28},{28,24},{1,5},{5... | collective-permute-start | bytes 405512 | tf_op jit(solution)/shard_map/ppermute | solution.py:29
  4.5 3.6 %collective-permute-start.1 = (bf16[528,128]{1,0:T(8,128)(2,1)S(1)}, bf16[528,128]{1,0:T(8,128)(2,1)S(1)}, u32[]{:S(2)}, u32[]{:S(2)}) collective-permute-start(bf16[528,128]{1,0:T(8,128)(2,1)S(1)} %get-tuple-element.26), channel_id=1, source_target_pairs={{4,8},{12,16},{20,24},{8,4},{16,12},{24,20},{5,9},{13,17},{21,25},... | collective-permute-start | bytes 405512 | tf_op jit(solution)/shard_map/ppermute | solution.py:29
  5.1 5.5 %collective-permute-start.2 = (bf16[528,128]{1,0:T(8,128)(2,1)S(1)}, bf16[528,128]{1,0:T(8,128)(2,1)S(1)}, u32[]{:S(2)}, u32[]{:S(2)}) collective-permute-start(bf16[528,128]{1,0:T(8,128)(2,1)S(1)} %get-tuple-element.27), channel_id=1, source_target_pairs={{0,1},{1,0},{2,3},{3,2},{4,5},{5,4},{6,7},{7,6},{8,9},{9,8},{10,11... | collective-permute-start | bytes 405512 | tf_op jit(solution)/shard_map/ppermute | solution.py:29
  5.2 5.4 %collective-permute-start.3 = (bf16[528,128]{1,0:T(8,128)(2,1)S(1)}, bf16[528,128]{1,0:T(8,128)(2,1)S(1)}, u32[]{:S(2)}, u32[]{:S(2)}) collective-permute-start(bf16[528,128]{1,0:T(8,128)(2,1)S(1)} %get-tuple-element.28), channel_id=1, source_target_pairs={{1,2},{2,1},{5,6},{6,5},{9,10},{10,9},{13,14},{14,13},{17,18},{18,... | collective-permute-start | bytes 405512 | tf_op jit(solution)/shard_map/ppermute | solution.py:29
  8.1 1.5 %copy-start.5 = (f32[32]{0:T(128)S(1)}, f32[32]{0:T(128)}, u32[]{:S(2)}) copy-start(f32[32]{0:T(128)} %param.12) | copy-start | bytes 388
  8.1 4.0 %collective-permute-start.4 = (bf16[288,128]{1,0:T(8,128)(2,1)S(1)}, bf16[288,128]{1,0:T(8,128)(2,1)S(1)}, u32[]{:S(2)}, u32[]{:S(2)}) collective-permute-start(bf16[288,128]{1,0:T(8,128)(2,1)S(1)} %get-tuple-element.31), channel_id=1, source_target_pairs={{0,1},{1,0},{2,3},{3,2},{4,5},{5,4},{6,7},{7,6},{8,9},{9,8},{10,11... | collective-permute-start | bytes 221192 | tf_op jit(solution)/shard_map/ppermute | solution.py:29
  8.9 3.2 %collective-permute-start.5 = (bf16[288,128]{1,0:T(8,128)(2,1)S(1)}, bf16[288,128]{1,0:T(8,128)(2,1)S(1)}, u32[]{:S(2)}, u32[]{:S(2)}) collective-permute-start(bf16[288,128]{1,0:T(8,128)(2,1)S(1)} %get-tuple-element.32), channel_id=1, source_target_pairs={{1,2},{2,1},{5,6},{6,5},{9,10},{10,9},{13,14},{14,13},{17,18},{18,... | collective-permute-start | bytes 221192 | tf_op jit(solution)/shard_map/ppermute | solution.py:29
  9.6 0.7 %copy-start.2 = (f32[32]{0:T(128)S(1)}, f32[32]{0:T(128)}, u32[]{:S(2)}) copy-start(f32[32]{0:T(128)} %param.15) | copy-start | bytes 388
  9.6 0.7 %copy-start.3 = (f32[32]{0:T(128)S(1)}, f32[32]{0:T(128)}, u32[]{:S(2)}) copy-start(f32[32]{0:T(128)} %param.14) | copy-start | bytes 388
  9.6 0.7 %copy-start.4 = (f32[32]{0:T(128)S(1)}, f32[32]{0:T(128)}, u32[]{:S(2)}) copy-start(f32[32]{0:T(128)} %param.13) | copy-start | bytes 388

commit v6 on v5

--- a/solution.py
+++ b/solution.py
@@ -26,7 +26,8 @@
 
 def swap(even, odd, axis):
     count = lax.axis_size(axis)
-    return lax.ppermute(even, axis, even_pairs(count)), lax.ppermute(odd, axis, odd_pairs(count))
+    odd = lax.ppermute(odd, axis, odd_pairs(count))
+    return lax.ppermute(even, axis, even_pairs(count)), odd
 
 
 def call(body, outs, ins, scratch=(), far=(), far_out=False):
@@ -64,44 +65,60 @@
     return ((even, jnp.where(even_place, 0, 1)), (odd, jnp.where(even_place, 1, 0)))
 
 
-def gather_kernel(dims, features, bricks, *refs):
-    own, masks, x_even, x_odd, y_even, y_odd, raw, flags, turned, arrived, flags_arrived = refs
+def turn(dims, raw, x, raw_x, masks, turned, keep):
+    channels, extent_x, extent_y, depth, bx, by = dims
+    for j in range(by):
+        part = raw[:, raw_x, j * BRICK : (j + 1) * BRICK, :].astype(F32)
+        part = part * masks[x // BRICK * by + j][None]
+        turned[x % 2] = part.reshape(channels * BRICK, depth)
+        for y in range(BRICK):
+            value = turned[x % 2, pl.ds(y, channels, stride=BRICK), :]
+            keep(j * BRICK + y, value.astype(BF16))
+
+
+def edge_kernel(dims, features, bricks, *refs):
+    masks, even, odd, raw, flags, turned, edge, arrived, flags_arrived = refs
     channels, extent_x, extent_y, depth, bx, by = dims
     flag_copy = pltpu.make_async_copy(bricks, flags, flags_arrived)
     flag_copy.start()
     copies = []
-    for x in range(0, extent_x, 2):
+    for side in range(2):
+        start = side * (extent_x - HALO)
         copy = pltpu.make_async_copy(
-            features.at[:, x : x + 2], raw.at[:, x : x + 2], arrived.at[x // 2]
+            features.at[:, start : start + HALO], raw.at[side], arrived.at[side]
         )
         copy.start()
         copies.append(copy)
     flag_copy.wait()
     rows = brick_rows(flags[...].astype(F32), depth)
     for i in range(bx * by):
-        masks[i] = jnp.broadcast_to(rows[i : i + 1], (16, depth))
-    for x in range(extent_x):
-        if x % 2 == 0:
-            copies[x // 2].wait()
-        for j in range(by):
-            part = raw[:, x, j * BRICK : (j + 1) * BRICK, :].astype(F32)
-            part = part * masks[x // BRICK * by + j][None, :BRICK, :]
-            turned[x % 2] = part.reshape(channels * BRICK, depth)
-            for y in range(BRICK):
-                own[x, j * BRICK + y] = turned[x % 2, pl.ds(y, channels, stride=BRICK), :].astype(
-                    BF16
-                )
-    for out, low in sides(is_even("region"), x_even, x_odd):
-        start = jnp.where(low == 1, 0, extent_x - HALO)
+        masks[i] = jnp.broadcast_to(rows[i : i + 1], (BRICK, depth))
+    for side in range(2):
+        copies[side].wait()
         for i in range(HALO):
-            for y in range(extent_y):
+
+            def keep(y, value):
                 at = (i * extent_y + y) * channels
-                out[at : at + channels, :] = own[start + i, y]
-        base = HALO * extent_y * channels
+                edge[1 - side, at : at + channels, :] = value
+
+            turn(dims, raw.at[side], side * (extent_x - HALO) + i, i, masks, turned, keep)
+    rows = HALO * extent_y * channels
+    for out, low in sides(is_even("region"), even, odd):
+        out[:rows, :] = edge[low]
         for j in range(by):
             tile = masks[jnp.where(low == 1, 0, bx - 1) * by + j]
-            out[base + 16 * j : base + 16 * (j + 1), :] = tile.astype(BF16)
-    for out, low in sides(is_even("strip"), y_even, y_odd):
+            out[rows + BRICK * j : rows + BRICK * (j + 1), :] = tile.astype(BF16)
+
+
+def gather_kernel(dims, features, masks, own, even, odd, turned):
+    channels, extent_x, extent_y, depth, bx, by = dims
+    for x in range(extent_x):
+
+        def keep(y, value):
+            own[x, y] = value
+
+        turn(dims, features, x, x, masks, turned, keep)
+    for out, low in sides(is_even("strip"), even, odd):
         start = jnp.where(low == 1, 0, extent_y - HALO)
         for x in range(extent_x):
             for j in range(HALO):
@@ -110,7 +127,7 @@
         base = extent_x * HALO * channels
         for i in range(bx):
             tile = masks[i * by + jnp.where(low == 1, 0, by - 1)]
-            out[base + 16 * i : base + 16 * (i + 1), :] = tile.astype(BF16)
+            out[base + BRICK * i : base + BRICK * (i + 1), :] = tile.astype(BF16)
 
 
 def corner_kernel(dims, x_even, x_odd, even, odd):
@@ -129,11 +146,11 @@
                 to = (i * HALO + j) * channels
                 out[to : to + channels, :] = jnp.where(first_x, b, a)
                 out[half + to : half + to + channels, :] = jnp.where(first_x, a, b)
-        at = pl.multiple_of(base + brick * 16, 16)
-        a = x_even[pl.ds(at, 16), :]
-        b = x_odd[pl.ds(at, 16), :]
-        out[2 * half : 2 * half + 16, :] = jnp.where(first_x, b, a)
-        out[2 * half + 16 : 2 * half + 32, :] = jnp.where(first_x, a, b)
+        at = pl.multiple_of(base + brick * BRICK, BRICK)
+        a = x_even[pl.ds(at, BRICK), :].astype(F32)
+        b = x_odd[pl.ds(at, BRICK), :].astype(F32)
+        tiles = (jnp.where(first_x, b, a), jnp.where(first_x, a, b))
+        out[2 * half : 2 * half + 2 * BRICK, :] = jnp.concatenate(tiles, axis=0).astype(BF16)
 
 
 def prepare_kernel(weights_first, weights_second, rows, first_band, second_band, params):
@@ -161,17 +178,27 @@
         params[i] = jnp.transpose(jnp.broadcast_to(row, (128, 128)))[:channels]
 
 
-def convolve_groups(groups, column, band, channels, depth, emit):
+def window_of(group):
+    return [(group[0] + a - 1, group[1] + b - 1) for a in range(4) for b in range(4)]
+
+
+def convolve_groups(groups, column, band, channels, depth, emit, ready=None):
+    pairs = [groups[i : i + 2] for i in range(0, len(groups), 2)]
+
+    def prepare(i):
+        if ready is not None and i < len(pairs):
+            for group in pairs[i]:
+                for x, y in window_of(group):
+                    ready(x, y)
+
+    prepare(0)
     lane = lax.broadcasted_iota(jnp.int32, (channels, depth), 1)
     at_start, at_end = lane == 0, lane == depth - 1
-    for i in range(0, len(groups), 2):
-        pair = groups[i : i + 2]
-        windows = []
-        for x, y in pair:
-            parts = [column(x + a - 1, y + b - 1) for a in range(4) for b in range(4)]
-            windows.append(jnp.concatenate(parts, axis=0))
+    for i, pair in enumerate(pairs):
+        windows = [jnp.concatenate([column(*at) for at in window_of(g)], axis=0) for g in pair]
         window = jnp.concatenate(windows, axis=1) if len(windows) > 1 else windows[0]
         total = jnp.dot(band[...], window, preferred_element_type=F32)
+        prepare(i + 1)
         for n, (x, y) in enumerate(pair):
             for a in range(2):
                 for b in range(2):
@@ -214,6 +241,8 @@
 
     def pick(self, pair, first, low, at, rows):
         even, odd = (ref[at : at + rows, :] for ref in pair)
+        if rows == BRICK:
+            even, odd = even.astype(F32), odd.astype(F32)
         return jnp.where(first, odd, even) if low else jnp.where(first, even, odd)
 
     def column(self, x, y):
@@ -236,17 +265,17 @@
         channels, extent_x, extent_y, depth, bx, by = self.dims
         inside_x, inside_y = 0 <= i < bx, 0 <= j < by
         if inside_x and inside_y:
-            return self.masks[i * by + j][:BRICK]
+            return self.masks[i * by + j]
         if inside_y:
-            at = HALO * extent_y * channels + 16 * j
-            tile = self.pick(self.x_pair, self.first_x, i < 0, at, 16)
+            at = HALO * extent_y * channels + BRICK * j
+            tile = self.pick(self.x_pair, self.first_x, i < 0, at, BRICK)
         elif inside_x:
-            at = HALO * extent_x * channels + 16 * i
-            tile = self.pick(self.y_pair, self.first_y, j < 0, at, 16)
+            at = HALO * extent_x * channels + BRICK * i
+            tile = self.pick(self.y_pair, self.first_y, j < 0, at, BRICK)
         else:
-            at = 2 * HALO * HALO * channels + 16 * int(i > 0)
-            tile = self.pick(self.corner_pair, self.first_y, j < 0, at, 16)
-        return tile.astype(F32)[:BRICK]
+            at = 2 * HALO * HALO * channels + BRICK * int(i > 0)
+            tile = self.pick(self.corner_pair, self.first_y, j < 0, at, BRICK)
+        return tile
 
 
 class Sums:
@@ -321,15 +350,20 @@
     average, scale = affine(received, params[0], channels, depth)
     shift = params[1]
     edge_x, edge_y = (0, 1, extent_x, extent_x + 1), (0, 1, extent_y, extent_y + 1)
-    for x in range(extent_x + 2):
-        for y in range(extent_y + 2):
-            if x in edge_x and y in edge_y:
-                part = corner_out[edge_x.index(x), edge_y.index(y)]
-            else:
-                part = first_out[x, y]
-            mask = wide_masks[(x - 1) // BRICK + 1, (y - 1) // BRICK + 1][:1]
-            part = jnp.maximum((part.astype(F32) - average) * scale + shift, 0.0) * mask
-            field[x, y] = part.astype(BF16)
+    done = set()
+
+    def activate(x, y):
+        if (x, y) in done:
+            return
+        done.add((x, y))
+        if x + 1 in edge_x and y + 1 in edge_y:
+            part = corner_out[edge_x.index(x + 1), edge_y.index(y + 1)]
+        else:
+            part = first_out[x + 1, y + 1]
+        mask = wide_masks[x // BRICK + 1, y // BRICK + 1][:1]
+        part = jnp.maximum((part.astype(F32) - average) * scale + shift, 0.0) * mask
+        field[x + 1, y + 1] = part.astype(BF16)
+
     zero = jnp.zeros((channels, depth), F32)
     sums = Sums(zero, zero)
 
@@ -340,7 +374,7 @@
 
     groups = [(x, y) for x in range(0, extent_x, 2) for y in range(0, extent_y, 2)]
     convolve_groups(
-        groups, lambda x, y: field[x + 1, y + 1], band, channels, depth, emit
+        groups, lambda x, y: field[x + 1, y + 1], band, channels, depth, emit, activate
     )
     counts = jnp.zeros((BRICK, depth), F32)
     for i in range(bx):
@@ -392,33 +426,42 @@
     devices = lax.axis_size(AXES)
     shape = jax.ShapeDtypeStruct
 
-    x_rows = HALO * extent_y * channels + 16 * by
-    y_rows = HALO * extent_x * channels + 16 * bx
-    c_rows = 2 * HALO * HALO * channels + 32
-    own, masks, x_even, x_odd, y_even, y_odd = call(
+    x_rows = HALO * extent_y * channels + BRICK * by
+    y_rows = HALO * extent_x * channels + BRICK * bx
+    c_rows = 2 * HALO * HALO * channels + 2 * BRICK
+    turned = pltpu.VMEM((2, channels * BRICK, depth), F32)
+    masks, x_even, x_odd = call(
+        functools.partial(edge_kernel, dims),
+        (
+            shape((bx * by, BRICK, depth), F32),
+            shape((x_rows, depth), BF16),
+            shape((x_rows, depth), BF16),
+        ),
+        (
+            pltpu.with_memory_space_constraint(features, pltpu.HBM),
+            pltpu.with_memory_space_constraint(brick_mask.reshape(bx * by, bz), pltpu.HBM),
+        ),
+        scratch=[
+            pltpu.VMEM((2, channels, HALO, extent_y, depth), BF16),
+            pltpu.VMEM((bx * by, bz), jnp.int32),
+            turned,
+            pltpu.VMEM((2, HALO * extent_y * channels, depth), BF16),
+            pltpu.SemaphoreType.DMA((2,)),
+            pltpu.SemaphoreType.DMA,
+        ],
+        far=(0, 1),
+    )
+    x_pair = swap(x_even, x_odd, "region")
+    own, y_even, y_odd = call(
         functools.partial(gather_kernel, dims),
         (
             shape((extent_x, extent_y, channels, depth), BF16),
-            shape((bx * by, 16, depth), F32),
-            shape((x_rows, depth), BF16),
-            shape((x_rows, depth), BF16),
             shape((y_rows, depth), BF16),
             shape((y_rows, depth), BF16),
         ),
-        (
-            pltpu.with_memory_space_constraint(features, pltpu.HBM),
-            pltpu.with_memory_space_constraint(brick_mask.reshape(bx * by, bz), pltpu.HBM),
-        ),
-        scratch=[
-            pltpu.VMEM(features.shape, BF16),
-            pltpu.VMEM((bx * by, bz), jnp.int32),
-            pltpu.VMEM((2, channels * BRICK, depth), F32),
-            pltpu.SemaphoreType.DMA((extent_x // 2,)),
-            pltpu.SemaphoreType.DMA,
-        ],
-        far=(0, 1),
-    )
-    x_pair = swap(x_even, x_odd, "region")
+        (features, masks),
+        scratch=[turned],
+    )
     y_pair = swap(y_even, y_odd, "strip")
     corners = call(
         functools.partial(corner_kernel, dims),
@@ -468,7 +511,7 @@
         shape(features.shape, BF16),
         (second_out, wide_masks, received, params, own),
         scratch=[
-            pltpu.VMEM((2, channels * BRICK, depth), F32),
+            turned,
             pltpu.VMEM(features.shape, BF16),
             pltpu.SemaphoreType.DMA((extent_x // 2,)),
         ],

time: 42.3 us -> 42 us (level)
  starting transfers between devices: 5.89 us -> 6.54 us
  waiting for transfers between devices: 2.19 us -> 1.68 us
  blocking collectives: 26.7 us -> 26.2 us
    ppermute x6, starting transfers between devices: 5.89 us -> 6.54 us  [the longest x3 4.43 us: swap(): return (lax.ppermute(even, axis, even_pairs(count)), odd)]
    all_to_all x2, blocking collectives: 26.7 us -> 26.2 us  [per_device(): received = lax.all_to_all(sent, AXES, 0, 0, tiled=True)]
    ppermute x6, waiting for transfers between devices: 2.19 us -> 1.68 us  [the longest x3 1.66 us: swap(): return (lax.ppermute(even, axis, even_pairs(count)), odd)]
    pallas_call x7 -> x8, Pallas kernels: 6.44 us -> 6.52 us  [call(): pl.pallas_call(body, out_shape=outs, in_specs=[space(i in far) for i in r...]
  transfers between devices with their start and end apart: 6 -> 6, of which waited for: 1 -> 1; matrix products, arithmetic and copies ran while one was open for 0% -> 0% of each run, Pallas kernels for 4% -> 5%
where the time goes in v6:
time: 42 us; the launch traced here: 41.8 us
  blocking collectives  26.2 us (62%)
  starting transfers between devices  6.54 us (16%)
  Pallas kernels  6.52 us (16%)
  waiting for transfers between devices  1.68 us (4%)
  local copies, waits for them, and re-layouts  0.68 us (2%)
    all_to_all x2, blocking collectives, per_device(): received = lax.all_to_all(sent, AXES, 0, 0, tiled=True)  26.2 us
    pallas_call x8, Pallas kernels, call(): pl.pallas_call(body, out_shape=outs, in_specs=[space(i in far) for i in r...  6.52 us
    ppermute x3, starting transfers between devices, swap(): return (lax.ppermute(even, axis, even_pairs(count)), odd)  4.43 us
    ppermute x3, starting transfers between devices, swap(): odd = lax.ppermute(odd, axis, odd_pairs(count))  2.11 us
    ppermute x3, waiting for transfers between devices, swap(): return (lax.ppermute(even, axis, even_pairs(count)), odd)  1.66 us
  transfers between devices with their start and end apart: 6, of which 1 were waited for; matrix products, arithmetic and copies ran while one was open for 0% of the time, Pallas kernels for 5%

profile of v6, /device:TPU:0, one launch (start us, length us, event | category | flops | bytes accessed | tf_op | source)
XLA Modules:
  0.0 41.8 jit_solution(16616160333880529942)
XLA Ops:
  0.0 1.2 %shard_map.82 = (f32[1,8,128]{2,1,0:T(8,128)S(1)}, bf16[520,128]{1,0:T(8,128)(2,1)S(1)}, bf16[520,128]{1,0:T(8,128)(2,1)S(1)}) custom-call(bf16[32,8,8,128]{3,2,1,0:T(8,128)(2,1)} %features.3, s32[1,16]{1,0:T(1,128)} %bitcast.17), custom_call_target="tpu_custom_call" | custom-call | bytes 524352 | tf_op jit(solution)/shard_map/pallas_call | solution.py:37
  1.2 3.1 %collective-permute-start = (bf16[520,128]{1,0:T(8,128)(2,1)S(1)}, bf16[520,128]{1,0:T(8,128)(2,1)S(1)}, u32[]{:S(2)}, u32[]{:S(2)}) collective-permute-start(bf16[520,128]{1,0:T(8,128)(2,1)S(1)} %get-tuple-element.25), channel_id=1, source_target_pairs={{0,4},{4,0},{8,12},{12,8},{16,20},{20,16},{24,28},{28,24},{1,5},{5... | collective-permute-start | bytes 399368 | tf_op jit(solution)/shard_map/ppermute | solution.py:30
  4.2 0.7 %collective-permute-start.1 = (bf16[520,128]{1,0:T(8,128)(2,1)S(1)}, bf16[520,128]{1,0:T(8,128)(2,1)S(1)}, u32[]{:S(2)}, u32[]{:S(2)}) collective-permute-start(bf16[520,128]{1,0:T(8,128)(2,1)S(1)} %get-tuple-element.26), channel_id=1, source_target_pairs={{4,8},{12,16},{20,24},{8,4},{16,12},{24,20},{5,9},{13,17},{21,25},... | collective-permute-start | bytes 399368 | tf_op jit(solution)/shard_map/ppermute | solution.py:29
  4.9 0.0 copy-start.2
  4.9 0.3 shard_map.83
  5.2 0.0 copy-start.1
  5.2 0.1 collective-permute-start.2
  5.3 0.8 %collective-permute-start.3 = (bf16[520,128]{1,0:T(8,128)(2,1)S(1)}, bf16[520,128]{1,0:T(8,128)(2,1)S(1)}, u32[]{:S(2)}, u32[]{:S(2)}) collective-permute-start(bf16[520,128]{1,0:T(8,128)(2,1)S(1)} %get-tuple-element.28), channel_id=1, source_target_pairs={{1,2},{2,1},{5,6},{6,5},{9,10},{10,9},{13,14},{14,13},{17,18},{18,... | collective-permute-start | bytes 399368 | tf_op jit(solution)/shard_map/ppermute | solution.py:29
  6.1 1.7 %collective-permute-done.x_even.refs_0_ = bf16[520,128]{1,0:T(8,128)(2,1)S(1)} collective-permute-done((bf16[520,128]{1,0:T(8,128)(2,1)S(1)}, bf16[520,128]{1,0:T(8,128)(2,1)S(1)}, u32[]{:S(2)}, u32[]{:S(2)}) %collective-permute-start) | collective-permute-done | bytes 133152 | tf_op jit(solution)/shard_map/ppermute | solution.py:30
  7.8 1.3 %collective-permute-start.4 = (bf16[272,128]{1,0:T(8,128)(2,1)S(1)}, bf16[272,128]{1,0:T(8,128)(2,1)S(1)}, u32[]{:S(2)}, u32[]{:S(2)}) collective-permute-start(bf16[272,128]{1,0:T(8,128)(2,1)S(1)} %get-tuple-element.31), channel_id=1, source_target_pairs={{0,1},{1,0},{2,3},{3,2},{4,5},{5,4},{6,7},{7,6},{8,9},{9,8},{10,11... | collective-permute-start | bytes 208904 | tf_op jit(solution)/shard_map/ppermute | solution.py:30
  9.1 0.7 %collective-permute-start.5 = (bf16[272,128]{1,0:T(8,128)(2,1)S(1)}, bf16[272,128]{1,0:T(8,128)(2,1)S(1)}, u32[]{:S(2)}, u32[]{:S(2)}) collective-permute-start(bf16[272,128]{1,0:T(8,128)(2,1)S(1)} %get-tuple-element.32), channel_id=1, source_target_pairs={{1,2},{2,1},{5,6},{6,5},{9,10},{10,9},{13,14},{14,13},{17,18},{18,... | collective-permute-start | bytes 208904 | tf_op jit(solution)/shard_map/ppermute | solution.py:29
  9.8 0.0 copy-start.3
  9.8 0.0 copy-start.4
  9.8 0.6 %copy-done.3 = f32[32]{0:T(128)S(1)} copy-done((f32[32]{0:T(128)S(1)}, f32[32]{0:T(128)}, u32[]{:S(2)}) %copy-start.3) | copy-done | bytes 152
  10.4 0.0 copy-done.4
  10.4 0.0 copy-done.5
  10.5 0.4 shard_map.84
  10.9 0.0 collective-permute-done.3.y_odd.refs_3_
  10.9 1.4 %shard_map.85 = (bf16[10,10,32,128]{3,2,1,0:T(8,128)(2,1)S(1)}, f32[2,32,128]{2,1,0:T(8,128)S(1)}) custom-call(bf16[8,8,32,128]{3,2,1,0:T(8,128)(2,1)S(1)} %get-tuple-element.24.own, f32[1,8,128]{2,1,0:T(8,128)S(1)} %get-tuple-element.23.masks, bf16[520,128]{1,0:T(8,128)(2,1)S(1)} %collective-permute-done.x_even.refs_0_, ...), custom_call_target="tpu_custom_call" | custom-call | bytes 1454080 | tf_op jit(solution)/shard_map/pallas_call | solution.py:37
  12.3 0.6 %shard_map.87 = (bf16[4,4,32,128]{3,2,1,0:T(8,128)(2,1)S(1)}, f32[3,3,8,128]{3,2,1,0:T(8,128)S(1)}, f32[32,128]{1,0:T(8,128)S(1)}) custom-call(bf16[8,8,32,128]{3,2,1,0:T(8,128)(2,1)S(1)} %get-tuple-element.24.own, f32[1,8,128]{2,1,0:T(8,128)S(1)} %get-tuple-element.23.masks, bf16[520,128]{1,0:T(8,128)(2,1)S(1)} %collective-permute-done.x_even.refs_0_, ...), custom_call_target="tpu_custom_call" | custom-call | bytes 1626112 | tf_op jit(solution)/shard_map/pallas_call | solution.py:37
  12.9 17.3 %all_to_all.22 = f32[32,1,128]{2,1,0:T(1,128)S(1)} all-to-all(f32[32,1,128]{2,1,0:T(1,128)S(1)} %bitcast.15), channel_id=1, replica_groups=mesh['region'=8,'strip'=4] {'region','strip'}, dimensions={0} | all-to-all | bytes 32768 | tf_op jit(solution)/shard_map/all_to_all | solution.py:498
  30.2 1.4 %shard_map.88 = (bf16[8,8,32,128]{3,2,1,0:T(8,128)(2,1)S(1)}, f32[32,128]{1,0:T(8,128)S(1)}) custom-call(bf16[10,10,32,128]{3,2,1,0:T(8,128)(2,1)S(1)} %get-tuple-element.30.refs_0_, bf16[4,4,32,128]{3,2,1,0:T(8,128)(2,1)S(1)} %get-tuple-element.34.refs_1_, f32[3,3,8,128]{3,2,1,0:T(8,128)S(1)} %get-tuple-element.35.refs_2_.wide_masks, ...), custom_call_target="tpu_custom_call" | custom-call | bytes 1462272 | tf_op jit(solution)/shard_map/pallas_call | solution.py:37
  31.6 8.9 %all_to_all.23 = f32[32,1,128]{2,1,0:T(1,128)S(1)} all-to-all(f32[32,1,128]{2,1,0:T(1,128)S(1)} %bitcast.16), channel_id=1, replica_groups=mesh['region'=8,'strip'=4] {'region','strip'}, dimensions={0} | all-to-all | bytes 32768 | tf_op jit(solution)/shard_map/all_to_all | solution.py:508
  40.5 1.2 %shard_map.89 = bf16[32,8,8,128]{3,2,1,0:T(8,128)(2,1)} custom-call(bf16[8,8,32,128]{3,2,1,0:T(8,128)(2,1)S(1)} %get-tuple-element.39.second_out, f32[3,3,8,128]{3,2,1,0:T(8,128)S(1)} %get-tuple-element.35.refs_2_.wide_masks, f32[32,128]{1,0:T(8,128)S(1)} %bitcast.14, f32[4,32,128]{2,1,0:T(8,128)S(1)} %get-tuple-element.37.refs_4_.params, ...), custom_call_target="tpu_custom_call" | custom-call | bytes 1167360 | tf_op jit(solution)/shard_map/pallas_call | solution.py:37
  (13 shorter events, 0.1 us)
Async XLA Ops:
  0.0 4.9 %copy-start = (bf16[32,8,8,128]{3,2,1,0:T(8,128)(2,1)S(1)}, bf16[32,8,8,128]{3,2,1,0:T(8,128)(2,1)}, u32[]{:S(2)}) copy-start(bf16[32,8,8,128]{3,2,1,0:T(8,128)(2,1)} %features.3) | copy-start | bytes 1572868
  1.2 6.6 %collective-permute-start = (bf16[520,128]{1,0:T(8,128)(2,1)S(1)}, bf16[520,128]{1,0:T(8,128)(2,1)S(1)}, u32[]{:S(2)}, u32[]{:S(2)}) collective-permute-start(bf16[520,128]{1,0:T(8,128)(2,1)S(1)} %get-tuple-element.25), channel_id=1, source_target_pairs={{0,4},{4,0},{8,12},{12,8},{16,20},{20,16},{24,28},{28,24},{1,5},{5... | collective-permute-start | bytes 399368 | tf_op jit(solution)/shard_map/ppermute | solution.py:30
  4.2 3.5 %collective-permute-start.1 = (bf16[520,128]{1,0:T(8,128)(2,1)S(1)}, bf16[520,128]{1,0:T(8,128)(2,1)S(1)}, u32[]{:S(2)}, u32[]{:S(2)}) collective-permute-start(bf16[520,128]{1,0:T(8,128)(2,1)S(1)} %get-tuple-element.26), channel_id=1, source_target_pairs={{4,8},{12,16},{20,24},{8,4},{16,12},{24,20},{5,9},{13,17},{21,25},... | collective-permute-start | bytes 399368 | tf_op jit(solution)/shard_map/ppermute | solution.py:29
  4.9 5.6 %copy-start.2 = (bf16[3,3,3,32,32]{4,3,2,1,0:T(8,128)(2,1)S(1)}, bf16[3,3,3,32,32]{4,3,2,1,0:T(8,128)(2,1)}, u32[]{:S(2)}) copy-start(bf16[3,3,3,32,32]{4,3,2,1,0:T(8,128)(2,1)} %weights_second.1) | copy-start | bytes 165892
  5.2 5.3 %copy-start.1 = (bf16[3,3,3,32,32]{4,3,2,1,0:T(8,128)(2,1)S(1)}, bf16[3,3,3,32,32]{4,3,2,1,0:T(8,128)(2,1)}, u32[]{:S(2)}) copy-start(bf16[3,3,3,32,32]{4,3,2,1,0:T(8,128)(2,1)} %weights_first.1) | copy-start | bytes 165892
  5.2 5.6 %collective-permute-start.2 = (bf16[520,128]{1,0:T(8,128)(2,1)S(1)}, bf16[520,128]{1,0:T(8,128)(2,1)S(1)}, u32[]{:S(2)}, u32[]{:S(2)}) collective-permute-start(bf16[520,128]{1,0:T(8,128)(2,1)S(1)} %get-tuple-element.27), channel_id=1, source_target_pairs={{0,1},{1,0},{2,3},{3,2},{4,5},{5,4},{6,7},{7,6},{8,9},{9,8},{10,11... | collective-permute-start | bytes 399368 | tf_op jit(solution)/shard_map/ppermute | solution.py:30
  5.3 5.6 %collective-permute-start.3 = (bf16[520,128]{1,0:T(8,128)(2,1)S(1)}, bf16[520,128]{1,0:T(8,128)(2,1)S(1)}, u32[]{:S(2)}, u32[]{:S(2)}) collective-permute-start(bf16[520,128]{1,0:T(8,128)(2,1)S(1)} %get-tuple-element.28), channel_id=1, source_target_pairs={{1,2},{2,1},{5,6},{6,5},{9,10},{10,9},{13,14},{14,13},{17,18},{18,... | collective-permute-start | bytes 399368 | tf_op jit(solution)/shard_map/ppermute | solution.py:29
  7.8 2.0 %copy-start.6 = (f32[32]{0:T(128)S(1)}, f32[32]{0:T(128)}, u32[]{:S(2)}) copy-start(f32[32]{0:T(128)} %param.12) | copy-start | bytes 388
  7.8 4.5 %collective-permute-start.4 = (bf16[272,128]{1,0:T(8,128)(2,1)S(1)}, bf16[272,128]{1,0:T(8,128)(2,1)S(1)}, u32[]{:S(2)}, u32[]{:S(2)}) collective-permute-start(bf16[272,128]{1,0:T(8,128)(2,1)S(1)} %get-tuple-element.31), channel_id=1, source_target_pairs={{0,1},{1,0},{2,3},{3,2},{4,5},{5,4},{6,7},{7,6},{8,9},{9,8},{10,11... | collective-permute-start | bytes 208904 | tf_op jit(solution)/shard_map/ppermute | solution.py:30
  9.1 3.2 %collective-permute-start.5 = (bf16[272,128]{1,0:T(8,128)(2,1)S(1)}, bf16[272,128]{1,0:T(8,128)(2,1)S(1)}, u32[]{:S(2)}, u32[]{:S(2)}) collective-permute-start(bf16[272,128]{1,0:T(8,128)(2,1)S(1)} %get-tuple-element.32), channel_id=1, source_target_pairs={{1,2},{2,1},{5,6},{6,5},{9,10},{10,9},{13,14},{14,13},{17,18},{18,... | collective-permute-start | bytes 208904 | tf_op jit(solution)/shard_map/ppermute | solution.py:29
  9.8 0.7 %copy-start.3 = (f32[32]{0:T(128)S(1)}, f32[32]{0:T(128)}, u32[]{:S(2)}) copy-start(f32[32]{0:T(128)} %param.15) | copy-start | bytes 388
  9.8 0.7 %copy-start.4 = (f32[32]{0:T(128)S(1)}, f32[32]{0:T(128)}, u32[]{:S(2)}) copy-start(f32[32]{0:T(128)} %param.14) | copy-start | bytes 388
  9.8 0.7 %copy-start.5 = (f32[32]{0:T(128)S(1)}, f32[32]{0:T(128)}, u32[]{:S(2)}) copy-start(f32[32]{0:T(128)} %param.13) | copy-start | bytes 388

commit v7 on v6

--- a/solution.py
+++ b/solution.py
@@ -7,9 +7,11 @@
 from jax.experimental.pallas import tpu as pltpu
 from jax.sharding import PartitionSpec as P
 
+
 BRICK = 8
 EPSILON = 1e-05
 HALO = 2
+PART = 16
 AXES = ("region", "strip")
 F32 = jnp.float32
 BF16 = jnp.bfloat16
@@ -26,8 +28,9 @@
 
 def swap(even, odd, axis):
     count = lax.axis_size(axis)
+    even = lax.ppermute(even, axis, even_pairs(count))
     odd = lax.ppermute(odd, axis, odd_pairs(count))
-    return lax.ppermute(even, axis, even_pairs(count)), odd
+    return even, odd
 
 
 def call(body, outs, ins, scratch=(), far=(), far_out=False):
@@ -66,7 +69,7 @@
 
 
 def turn(dims, raw, x, raw_x, masks, turned, keep):
-    channels, extent_x, extent_y, depth, bx, by = dims
+    channels, _, _, depth, _, by = dims
     for j in range(by):
         part = raw[:, raw_x, j * BRICK : (j + 1) * BRICK, :].astype(F32)
         part = part * masks[x // BRICK * by + j][None]
@@ -111,7 +114,7 @@
 
 
 def gather_kernel(dims, features, masks, own, even, odd, turned):
-    channels, extent_x, extent_y, depth, bx, by = dims
+    channels, extent_x, extent_y, _, bx, by = dims
     for x in range(extent_x):
 
         def keep(y, value):
@@ -131,7 +134,7 @@
 
 
 def corner_kernel(dims, x_even, x_odd, even, odd):
-    channels, extent_x, extent_y, depth, bx, by = dims
+    channels, _, extent_y, _, _, by = dims
     first_x = is_even("region")
     base = HALO * extent_y * channels
     for out, low in sides(is_even("strip"), even, odd):
@@ -191,6 +194,18 @@
                 for x, y in window_of(group):
                     ready(x, y)
 
+    def value_of(total, n, a, b):
+        before, here, after = (
+            total[
+                ((dz * 2 + a) * 2 + b) * channels : ((dz * 2 + a) * 2 + b + 1) * channels,
+                n * depth : (n + 1) * depth,
+            ]
+            for dz in range(3)
+        )
+        before = jnp.where(at_start, 0.0, pltpu.roll(before, 1, 1))
+        after = jnp.where(at_end, 0.0, pltpu.roll(after, depth - 1, 1))
+        return here + before + after
+
     prepare(0)
     lane = lax.broadcasted_iota(jnp.int32, (channels, depth), 1)
     at_start, at_end = lane == 0, lane == depth - 1
@@ -202,17 +217,7 @@
         for n, (x, y) in enumerate(pair):
             for a in range(2):
                 for b in range(2):
-                    before, here, after = (
-                        total[
-                            ((dz * 2 + a) * 2 + b) * channels : ((dz * 2 + a) * 2 + b + 1)
-                            * channels,
-                            n * depth : (n + 1) * depth,
-                        ]
-                        for dz in range(3)
-                    )
-                    before = jnp.where(at_start, 0.0, pltpu.roll(before, 1, 1))
-                    after = jnp.where(at_end, 0.0, pltpu.roll(after, depth - 1, 1))
-                    emit(x + a, y + b, here + before + after)
+                    emit(x + a, y + b, functools.partial(value_of, total, n, a, b))
 
 
 def send_stats(out, channels, sums, squares, counts):
@@ -223,13 +228,14 @@
     out[...] = jnp.broadcast_to(row, out.shape)
 
 
-def affine(stats, gain, channels, depth):
+def affine(stats, gain, shift, channels):
     row = jnp.sum(stats[...], axis=0, keepdims=True)
     table = jnp.transpose(jnp.broadcast_to(row, (128, 128)))
     total = jnp.sum(table[2 * channels : 2 * channels + BRICK], axis=0, keepdims=True)
     average = table[:channels] / total
     variance = table[channels : 2 * channels] / total - average * average
-    return average, lax.rsqrt(variance + EPSILON) * gain
+    scale = lax.rsqrt(variance + EPSILON) * gain
+    return scale, shift - average * scale
 
 
 class Edges:
@@ -262,7 +268,7 @@
         return self.pick(self.corner_pair, self.first_y, y < 0, at, channels)
 
     def mask(self, i, j):
-        channels, extent_x, extent_y, depth, bx, by = self.dims
+        channels, extent_x, extent_y, _, bx, by = self.dims
         inside_x, inside_y = 0 <= i < bx, 0 <= j < by
         if inside_x and inside_y:
             return self.masks[i * by + j]
@@ -296,7 +302,7 @@
 
 
 def first_kernel(dims, own, masks, x_even, x_odd, y_even, y_odd, band, first_out, partial):
-    channels, extent_x, extent_y, depth, bx, by = dims
+    channels, extent_x, extent_y, depth, _, _ = dims
     edges = Edges(dims, own, masks, (x_even, x_odd), (y_even, y_odd))
     found = {}
     zero = jnp.zeros((channels, depth), F32)
@@ -306,7 +312,7 @@
         brick = (x // BRICK, y // BRICK)
         if brick not in found:
             found[brick] = edges.mask(*brick)[:1]
-        value = (value * found[brick]).astype(BF16)
+        value = (value() * found[brick]).astype(BF16)
         first_out[x + 1, y + 1] = value
         if 0 <= x < extent_x and 0 <= y < extent_y:
             sums.add(value)
@@ -330,25 +336,34 @@
                 counts = counts + tile * float(BRICK)
     sums = Sums(partial[0], partial[1])
 
-    def emit(x, y, value):
-        value = (value * edges.mask(x // BRICK, y // BRICK)[:1]).astype(BF16)
-        side_x, side_y = int(x > 0 and x >= extent_x - 1), int(y > 0 and y >= extent_y - 1)
+    outputs = []
+    groups = ring_groups(extent_x, extent_y)[1]
+    convolve_groups(groups, edges.column, band, channels, depth, lambda *it: outputs.append(it))
+
+    def put(x, y, value):
+        value = (value() * edges.mask(x // BRICK, y // BRICK)[:1]).astype(BF16)
+        side_x, side_y = int(x >= extent_x - 1), int(y >= extent_y - 1)
         i = x - (extent_x - 1 if side_x else -1)
         j = y - (extent_y - 1 if side_y else -1)
         corner_out[2 * side_x + i, 2 * side_y + j] = value
-        if 0 <= x < extent_x and 0 <= y < extent_y:
-            sums.add(value)
-
-    groups = ring_groups(extent_x, extent_y)[1]
-    convolve_groups(groups, edges.column, band, channels, depth, emit)
+        return value
+
+    def is_own(x, y):
+        return 0 <= x < extent_x and 0 <= y < extent_y
+
+    for x, y, value in outputs:
+        if is_own(x, y):
+            sums.add(put(x, y, value))
     send_stats(stats, channels, sums.sums, sums.squares, counts)
+    for x, y, value in outputs:
+        if not is_own(x, y):
+            put(x, y, value)
 
 
 def second_kernel(dims, *refs):
     first_out, corner_out, wide_masks, received, params, band, second_out, stats, field = refs
     channels, extent_x, extent_y, depth, bx, by = dims
-    average, scale = affine(received, params[0], channels, depth)
-    shift = params[1]
+    scale, offset = affine(received, params[0], params[1], channels)
     edge_x, edge_y = (0, 1, extent_x, extent_x + 1), (0, 1, extent_y, extent_y + 1)
     done = set()
 
@@ -361,14 +376,14 @@
         else:
             part = first_out[x + 1, y + 1]
         mask = wide_masks[x // BRICK + 1, y // BRICK + 1][:1]
-        part = jnp.maximum((part.astype(F32) - average) * scale + shift, 0.0) * mask
+        part = jnp.maximum(part.astype(F32) * scale + offset, 0.0) * mask
         field[x + 1, y + 1] = part.astype(BF16)
 
     zero = jnp.zeros((channels, depth), F32)
     sums = Sums(zero, zero)
 
     def emit(x, y, value):
-        value = (value * wide_masks[x // BRICK + 1, y // BRICK + 1][:1]).astype(BF16)
+        value = (value() * wide_masks[x // BRICK + 1, y // BRICK + 1][:1]).astype(BF16)
         second_out[x, y] = value
         sums.add(value)
 
@@ -384,28 +399,25 @@
 
 
 def last_kernel(dims, second_out, wide_masks, received, params, own, result, turned, ready, sent):
-    channels, extent_x, extent_y, depth, bx, by = dims
-    average, scale = affine(received, params[2], channels, depth)
-    shift = params[3]
+    channels, extent_x, _, depth, _, by = dims
+    scale, offset = affine(received, params[2], params[3], channels)
     copies = []
-    for x in range(extent_x):
-        for j in range(by):
-            mask = wide_masks[x // BRICK + 1, j + 1][:1]
-            for y in range(BRICK):
-                at = j * BRICK + y
-                part = second_out[x, at].astype(F32)
-                part = (part - average) * scale + shift + own[x, at].astype(F32)
-                part = jnp.maximum(part, 0.0) * mask
-                turned[x % 2, pl.ds(y, channels, stride=BRICK), :] = part
-            ready[:, x, j * BRICK : (j + 1) * BRICK, :] = (
-                turned[x % 2].reshape(channels, BRICK, depth).astype(BF16)
-            )
-        if x % 2 == 1:
-            copy = pltpu.make_async_copy(
-                ready.at[:, x - 1 : x + 1], result.at[:, x - 1 : x + 1], sent.at[x // 2]
-            )
-            copy.start()
-            copies.append(copy)
+    for start in range(0, channels, PART):
+        rows = slice(start, start + PART)
+        for x in range(extent_x):
+            for j in range(by):
+                mask = wide_masks[x // BRICK + 1, j + 1][:1]
+                for y in range(BRICK):
+                    at = j * BRICK + y
+                    part = second_out[x, at, rows].astype(F32) * scale[rows] + offset[rows]
+                    part = jnp.maximum(part + own[x, at, rows].astype(F32), 0.0) * mask
+                    turned[x % 2, pl.ds(y, PART, stride=BRICK), :] = part
+                ready[rows, x, j * BRICK : (j + 1) * BRICK, :] = (
+                    turned[x % 2, : PART * BRICK].reshape(PART, BRICK, depth).astype(BF16)
+                )
+        copy = pltpu.make_async_copy(ready.at[rows], result.at[rows], sent.at[start // PART])
+        copy.start()
+        copies.append(copy)
     for copy in copies:
         copy.wait()
 
@@ -513,7 +525,7 @@
         scratch=[
             turned,
             pltpu.VMEM(features.shape, BF16),
-            pltpu.SemaphoreType.DMA((extent_x // 2,)),
+            pltpu.SemaphoreType.DMA((channels // PART,)),
         ],
         far_out=True,
     )

time: 42 us -> 41.9 us (level)
  no operation moved by 1% of the time
where the time goes in v7:
time: 41.9 us; the launch traced here: 41.7 us
  blocking collectives  26.2 us (63%)
  starting transfers between devices  6.54 us (16%)
  Pallas kernels  6.49 us (15%)
  waiting for transfers between devices  1.68 us (4%)
  local copies, waits for them, and re-layouts  0.68 us (2%)
    all_to_all x2, blocking collectives, per_device(): received = lax.all_to_all(sent, AXES, 0, 0, tiled=True)  26.2 us
    pallas_call x8, Pallas kernels, call(): pl.pallas_call(body, out_shape=outs, in_specs=[space(i in far) for i in r...  6.49 us
    ppermute x3, starting transfers between devices, swap(): even = lax.ppermute(even, axis, even_pairs(count))  4.43 us
    ppermute x3, starting transfers between devices, swap(): odd = lax.ppermute(odd, axis, odd_pairs(count))  2.11 us
    ppermute x3, waiting for transfers between devices, swap(): even = lax.ppermute(even, axis, even_pairs(count))  1.66 us
  transfers between devices with their start and end apart: 6, of which 1 were waited for; matrix products, arithmetic and copies ran while one was open for 0% of the time, Pallas kernels for 5%

profile of v7, /device:TPU:0, one launch (start us, length us, event | category | flops | bytes accessed | tf_op | source)
XLA Modules:
  0.0 41.7 jit_solution(553603872962696976)
XLA Ops:
  0.0 1.2 %shard_map.82 = (f32[1,8,128]{2,1,0:T(8,128)S(1)}, bf16[520,128]{1,0:T(8,128)(2,1)S(1)}, bf16[520,128]{1,0:T(8,128)(2,1)S(1)}) custom-call(bf16[32,8,8,128]{3,2,1,0:T(8,128)(2,1)} %features.3, s32[1,16]{1,0:T(1,128)} %bitcast.17), custom_call_target="tpu_custom_call" | custom-call | bytes 524352 | tf_op jit(solution)/shard_map/pallas_call | solution.py:40
  1.2 3.1 %collective-permute-start = (bf16[520,128]{1,0:T(8,128)(2,1)S(1)}, bf16[520,128]{1,0:T(8,128)(2,1)S(1)}, u32[]{:S(2)}, u32[]{:S(2)}) collective-permute-start(bf16[520,128]{1,0:T(8,128)(2,1)S(1)} %get-tuple-element.25), channel_id=1, source_target_pairs={{0,4},{4,0},{8,12},{12,8},{16,20},{20,16},{24,28},{28,24},{1,5},{5... | collective-permute-start | bytes 399368 | tf_op jit(solution)/shard_map/ppermute | solution.py:31
  4.2 0.7 %collective-permute-start.1 = (bf16[520,128]{1,0:T(8,128)(2,1)S(1)}, bf16[520,128]{1,0:T(8,128)(2,1)S(1)}, u32[]{:S(2)}, u32[]{:S(2)}) collective-permute-start(bf16[520,128]{1,0:T(8,128)(2,1)S(1)} %get-tuple-element.26), channel_id=1, source_target_pairs={{4,8},{12,16},{20,24},{8,4},{16,12},{24,20},{5,9},{13,17},{21,25},... | collective-permute-start | bytes 399368 | tf_op jit(solution)/shard_map/ppermute | solution.py:32
  4.9 0.0 copy-start.2
  4.9 0.3 shard_map.83
  5.2 0.0 copy-start.1
  5.2 0.1 collective-permute-start.2
  5.3 0.8 %collective-permute-start.3 = (bf16[520,128]{1,0:T(8,128)(2,1)S(1)}, bf16[520,128]{1,0:T(8,128)(2,1)S(1)}, u32[]{:S(2)}, u32[]{:S(2)}) collective-permute-start(bf16[520,128]{1,0:T(8,128)(2,1)S(1)} %get-tuple-element.28), channel_id=1, source_target_pairs={{1,2},{2,1},{5,6},{6,5},{9,10},{10,9},{13,14},{14,13},{17,18},{18,... | collective-permute-start | bytes 399368 | tf_op jit(solution)/shard_map/ppermute | solution.py:32
  6.1 1.7 %collective-permute-done.x_even.refs_0_ = bf16[520,128]{1,0:T(8,128)(2,1)S(1)} collective-permute-done((bf16[520,128]{1,0:T(8,128)(2,1)S(1)}, bf16[520,128]{1,0:T(8,128)(2,1)S(1)}, u32[]{:S(2)}, u32[]{:S(2)}) %collective-permute-start) | collective-permute-done | bytes 133152 | tf_op jit(solution)/shard_map/ppermute | solution.py:31
  7.8 1.3 %collective-permute-start.4 = (bf16[272,128]{1,0:T(8,128)(2,1)S(1)}, bf16[272,128]{1,0:T(8,128)(2,1)S(1)}, u32[]{:S(2)}, u32[]{:S(2)}) collective-permute-start(bf16[272,128]{1,0:T(8,128)(2,1)S(1)} %get-tuple-element.31), channel_id=1, source_target_pairs={{0,1},{1,0},{2,3},{3,2},{4,5},{5,4},{6,7},{7,6},{8,9},{9,8},{10,11... | collective-permute-start | bytes 208904 | tf_op jit(solution)/shard_map/ppermute | solution.py:31
  9.1 0.7 %collective-permute-start.5 = (bf16[272,128]{1,0:T(8,128)(2,1)S(1)}, bf16[272,128]{1,0:T(8,128)(2,1)S(1)}, u32[]{:S(2)}, u32[]{:S(2)}) collective-permute-start(bf16[272,128]{1,0:T(8,128)(2,1)S(1)} %get-tuple-element.32), channel_id=1, source_target_pairs={{1,2},{2,1},{5,6},{6,5},{9,10},{10,9},{13,14},{14,13},{17,18},{18,... | collective-permute-start | bytes 208904 | tf_op jit(solution)/shard_map/ppermute | solution.py:32
  9.8 0.0 copy-start.3
  9.8 0.0 copy-start.4
  9.8 0.6 %copy-done.3 = f32[32]{0:T(128)S(1)} copy-done((f32[32]{0:T(128)S(1)}, f32[32]{0:T(128)}, u32[]{:S(2)}) %copy-start.3) | copy-done | bytes 152
  10.4 0.0 copy-done.4
  10.4 0.0 copy-done.5
  10.5 0.4 shard_map.84
  10.9 0.0 collective-permute-done.3.y_odd.refs_3_
  10.9 1.4 %shard_map.85 = (bf16[10,10,32,128]{3,2,1,0:T(8,128)(2,1)S(1)}, f32[2,32,128]{2,1,0:T(8,128)S(1)}) custom-call(bf16[8,8,32,128]{3,2,1,0:T(8,128)(2,1)S(1)} %get-tuple-element.24.own, f32[1,8,128]{2,1,0:T(8,128)S(1)} %get-tuple-element.23.masks, bf16[520,128]{1,0:T(8,128)(2,1)S(1)} %collective-permute-done.x_even.refs_0_, ...), custom_call_target="tpu_custom_call" | custom-call | bytes 1454080 | tf_op jit(solution)/shard_map/pallas_call | solution.py:40
  12.3 0.6 %shard_map.87 = (bf16[4,4,32,128]{3,2,1,0:T(8,128)(2,1)S(1)}, f32[3,3,8,128]{3,2,1,0:T(8,128)S(1)}, f32[32,128]{1,0:T(8,128)S(1)}) custom-call(bf16[8,8,32,128]{3,2,1,0:T(8,128)(2,1)S(1)} %get-tuple-element.24.own, f32[1,8,128]{2,1,0:T(8,128)S(1)} %get-tuple-element.23.masks, bf16[520,128]{1,0:T(8,128)(2,1)S(1)} %collective-permute-done.x_even.refs_0_, ...), custom_call_target="tpu_custom_call" | custom-call | bytes 1626112 | tf_op jit(solution)/shard_map/pallas_call | solution.py:40
  12.9 17.3 %all_to_all.22 = f32[32,1,128]{2,1,0:T(1,128)S(1)} all-to-all(f32[32,1,128]{2,1,0:T(1,128)S(1)} %bitcast.15), channel_id=1, replica_groups=mesh['region'=8,'strip'=4] {'region','strip'}, dimensions={0} | all-to-all | bytes 32768 | tf_op jit(solution)/shard_map/all_to_all | solution.py:510
  30.2 1.4 %shard_map.88 = (bf16[8,8,32,128]{3,2,1,0:T(8,128)(2,1)S(1)}, f32[32,128]{1,0:T(8,128)S(1)}) custom-call(bf16[10,10,32,128]{3,2,1,0:T(8,128)(2,1)S(1)} %get-tuple-element.30.refs_0_, bf16[4,4,32,128]{3,2,1,0:T(8,128)(2,1)S(1)} %get-tuple-element.34.refs_1_, f32[3,3,8,128]{3,2,1,0:T(8,128)S(1)} %get-tuple-element.35.refs_2_.wide_masks, ...), custom_call_target="tpu_custom_call" | custom-call | bytes 1462272 | tf_op jit(solution)/shard_map/pallas_call | solution.py:40
  31.6 8.9 %all_to_all.23 = f32[32,1,128]{2,1,0:T(1,128)S(1)} all-to-all(f32[32,1,128]{2,1,0:T(1,128)S(1)} %bitcast.16), channel_id=1, replica_groups=mesh['region'=8,'strip'=4] {'region','strip'}, dimensions={0} | all-to-all | bytes 32768 | tf_op jit(solution)/shard_map/all_to_all | solution.py:520
  40.5 1.2 %shard_map.89 = bf16[32,8,8,128]{3,2,1,0:T(8,128)(2,1)} custom-call(bf16[8,8,32,128]{3,2,1,0:T(8,128)(2,1)S(1)} %get-tuple-element.39.second_out, f32[3,3,8,128]{3,2,1,0:T(8,128)S(1)} %get-tuple-element.35.refs_2_.wide_masks, f32[32,128]{1,0:T(8,128)S(1)} %bitcast.14, f32[4,32,128]{2,1,0:T(8,128)S(1)} %get-tuple-element.37.refs_4_.params, ...), custom_call_target="tpu_custom_call" | custom-call | bytes 1167360 | tf_op jit(solution)/shard_map/pallas_call | solution.py:40
  (13 shorter events, 0.1 us)
Async XLA Ops:
  0.0 4.9 %copy-start = (bf16[32,8,8,128]{3,2,1,0:T(8,128)(2,1)S(1)}, bf16[32,8,8,128]{3,2,1,0:T(8,128)(2,1)}, u32[]{:S(2)}) copy-start(bf16[32,8,8,128]{3,2,1,0:T(8,128)(2,1)} %features.3) | copy-start | bytes 1572868
  1.2 6.6 %collective-permute-start = (bf16[520,128]{1,0:T(8,128)(2,1)S(1)}, bf16[520,128]{1,0:T(8,128)(2,1)S(1)}, u32[]{:S(2)}, u32[]{:S(2)}) collective-permute-start(bf16[520,128]{1,0:T(8,128)(2,1)S(1)} %get-tuple-element.25), channel_id=1, source_target_pairs={{0,4},{4,0},{8,12},{12,8},{16,20},{20,16},{24,28},{28,24},{1,5},{5... | collective-permute-start | bytes 399368 | tf_op jit(solution)/shard_map/ppermute | solution.py:31
  4.2 3.5 %collective-permute-start.1 = (bf16[520,128]{1,0:T(8,128)(2,1)S(1)}, bf16[520,128]{1,0:T(8,128)(2,1)S(1)}, u32[]{:S(2)}, u32[]{:S(2)}) collective-permute-start(bf16[520,128]{1,0:T(8,128)(2,1)S(1)} %get-tuple-element.26), channel_id=1, source_target_pairs={{4,8},{12,16},{20,24},{8,4},{16,12},{24,20},{5,9},{13,17},{21,25},... | collective-permute-start | bytes 399368 | tf_op jit(solution)/shard_map/ppermute | solution.py:32
  4.9 5.6 %copy-start.2 = (bf16[3,3,3,32,32]{4,3,2,1,0:T(8,128)(2,1)S(1)}, bf16[3,3,3,32,32]{4,3,2,1,0:T(8,128)(2,1)}, u32[]{:S(2)}) copy-start(bf16[3,3,3,32,32]{4,3,2,1,0:T(8,128)(2,1)} %weights_second.1) | copy-start | bytes 165892
  5.2 5.3 %copy-start.1 = (bf16[3,3,3,32,32]{4,3,2,1,0:T(8,128)(2,1)S(1)}, bf16[3,3,3,32,32]{4,3,2,1,0:T(8,128)(2,1)}, u32[]{:S(2)}) copy-start(bf16[3,3,3,32,32]{4,3,2,1,0:T(8,128)(2,1)} %weights_first.1) | copy-start | bytes 165892
  5.2 5.6 %collective-permute-start.2 = (bf16[520,128]{1,0:T(8,128)(2,1)S(1)}, bf16[520,128]{1,0:T(8,128)(2,1)S(1)}, u32[]{:S(2)}, u32[]{:S(2)}) collective-permute-start(bf16[520,128]{1,0:T(8,128)(2,1)S(1)} %get-tuple-element.27), channel_id=1, source_target_pairs={{0,1},{1,0},{2,3},{3,2},{4,5},{5,4},{6,7},{7,6},{8,9},{9,8},{10,11... | collective-permute-start | bytes 399368 | tf_op jit(solution)/shard_map/ppermute | solution.py:31
  5.3 5.6 %collective-permute-start.3 = (bf16[520,128]{1,0:T(8,128)(2,1)S(1)}, bf16[520,128]{1,0:T(8,128)(2,1)S(1)}, u32[]{:S(2)}, u32[]{:S(2)}) collective-permute-start(bf16[520,128]{1,0:T(8,128)(2,1)S(1)} %get-tuple-element.28), channel_id=1, source_target_pairs={{1,2},{2,1},{5,6},{6,5},{9,10},{10,9},{13,14},{14,13},{17,18},{18,... | collective-permute-start | bytes 399368 | tf_op jit(solution)/shard_map/ppermute | solution.py:32
  7.8 2.0 %copy-start.6 = (f32[32]{0:T(128)S(1)}, f32[32]{0:T(128)}, u32[]{:S(2)}) copy-start(f32[32]{0:T(128)} %param.12) | copy-start | bytes 388
  7.8 4.5 %collective-permute-start.4 = (bf16[272,128]{1,0:T(8,128)(2,1)S(1)}, bf16[272,128]{1,0:T(8,128)(2,1)S(1)}, u32[]{:S(2)}, u32[]{:S(2)}) collective-permute-start(bf16[272,128]{1,0:T(8,128)(2,1)S(1)} %get-tuple-element.31), channel_id=1, source_target_pairs={{0,1},{1,0},{2,3},{3,2},{4,5},{5,4},{6,7},{7,6},{8,9},{9,8},{10,11... | collective-permute-start | bytes 208904 | tf_op jit(solution)/shard_map/ppermute | solution.py:31
  9.1 3.2 %collective-permute-start.5 = (bf16[272,128]{1,0:T(8,128)(2,1)S(1)}, bf16[272,128]{1,0:T(8,128)(2,1)S(1)}, u32[]{:S(2)}, u32[]{:S(2)}) collective-permute-start(bf16[272,128]{1,0:T(8,128)(2,1)S(1)} %get-tuple-element.32), channel_id=1, source_target_pairs={{1,2},{2,1},{5,6},{6,5},{9,10},{10,9},{13,14},{14,13},{17,18},{18,... | collective-permute-start | bytes 208904 | tf_op jit(solution)/shard_map/ppermute | solution.py:32
  9.8 0.7 %copy-start.3 = (f32[32]{0:T(128)S(1)}, f32[32]{0:T(128)}, u32[]{:S(2)}) copy-start(f32[32]{0:T(128)} %param.15) | copy-start | bytes 388
  9.8 0.7 %copy-start.4 = (f32[32]{0:T(128)S(1)}, f32[32]{0:T(128)}, u32[]{:S(2)}) copy-start(f32[32]{0:T(128)} %param.14) | copy-start | bytes 388
  9.8 0.7 %copy-start.5 = (f32[32]{0:T(128)S(1)}, f32[32]{0:T(128)}, u32[]{:S(2)}) copy-start(f32[32]{0:T(128)} %param.13) | copy-start | bytes 388

commit v8 on v7

--- a/solution.py
+++ b/solution.py
@@ -194,30 +194,32 @@
                 for x, y in window_of(group):
                     ready(x, y)
 
-    def value_of(total, n, a, b):
+    def rows_of(a):
+        wide = 2 * channels
+        parts = [band[(dz * 2 + a) * wide : (dz * 2 + a + 1) * wide, :] for dz in range(3)]
+        return jnp.concatenate(parts, axis=0)
+
+    def value_of(total, n, b):
         before, here, after = (
-            total[
-                ((dz * 2 + a) * 2 + b) * channels : ((dz * 2 + a) * 2 + b + 1) * channels,
-                n * depth : (n + 1) * depth,
-            ]
+            total[(2 * dz + b) * channels : (2 * dz + b + 1) * channels, n * depth : (n + 1) * depth]
             for dz in range(3)
         )
         before = jnp.where(at_start, 0.0, pltpu.roll(before, 1, 1))
         after = jnp.where(at_end, 0.0, pltpu.roll(after, depth - 1, 1))
         return here + before + after
 
-    prepare(0)
     lane = lax.broadcasted_iota(jnp.int32, (channels, depth), 1)
     at_start, at_end = lane == 0, lane == depth - 1
+    prepare(0)
     for i, pair in enumerate(pairs):
         windows = [jnp.concatenate([column(*at) for at in window_of(g)], axis=0) for g in pair]
         window = jnp.concatenate(windows, axis=1) if len(windows) > 1 else windows[0]
-        total = jnp.dot(band[...], window, preferred_element_type=F32)
         prepare(i + 1)
-        for n, (x, y) in enumerate(pair):
-            for a in range(2):
+        for a in range(2):
+            total = jnp.dot(rows_of(a), window, preferred_element_type=F32)
+            for n, (x, y) in enumerate(pair):
                 for b in range(2):
-                    emit(x + a, y + b, functools.partial(value_of, total, n, a, b))
+                    emit(x + a, y + b, functools.partial(value_of, total, n, b))
 
 
 def send_stats(out, channels, sums, squares, counts):

time: 41.9 us -> 41.9 us (level)
  no operation moved by 1% of the time
where the time goes in v8:
time: 41.9 us; the launch traced here: 41.7 us
  blocking collectives  26.2 us (63%)
  starting transfers between devices  6.54 us (16%)
  Pallas kernels  6.49 us (15%)
  waiting for transfers between devices  1.68 us (4%)
  local copies, waits for them, and re-layouts  0.68 us (2%)
    all_to_all x2, blocking collectives, per_device(): received = lax.all_to_all(sent, AXES, 0, 0, tiled=True)  26.2 us
    pallas_call x8, Pallas kernels, call(): pl.pallas_call(body, out_shape=outs, in_specs=[space(i in far) for i in r...  6.49 us
    ppermute x3, starting transfers between devices, swap(): even = lax.ppermute(even, axis, even_pairs(count))  4.43 us
    ppermute x3, starting transfers between devices, swap(): odd = lax.ppermute(odd, axis, odd_pairs(count))  2.11 us
    ppermute x3, waiting for transfers between devices, swap(): even = lax.ppermute(even, axis, even_pairs(count))  1.66 us
  transfers between devices with their start and end apart: 6, of which 1 were waited for; matrix products, arithmetic and copies ran while one was open for 0% of the time, Pallas kernels for 5%

profile of v8, /device:TPU:0, one launch (start us, length us, event | category | flops | bytes accessed | tf_op | source)
XLA Modules:
  0.0 41.7 jit_solution(3111678936789381463)
XLA Ops:
  0.0 1.2 %shard_map.82 = (f32[1,8,128]{2,1,0:T(8,128)S(1)}, bf16[520,128]{1,0:T(8,128)(2,1)S(1)}, bf16[520,128]{1,0:T(8,128)(2,1)S(1)}) custom-call(bf16[32,8,8,128]{3,2,1,0:T(8,128)(2,1)} %features.3, s32[1,16]{1,0:T(1,128)} %bitcast.17), custom_call_target="tpu_custom_call" | custom-call | bytes 524352 | tf_op jit(solution)/shard_map/pallas_call | solution.py:40
  1.2 3.1 %collective-permute-start = (bf16[520,128]{1,0:T(8,128)(2,1)S(1)}, bf16[520,128]{1,0:T(8,128)(2,1)S(1)}, u32[]{:S(2)}, u32[]{:S(2)}) collective-permute-start(bf16[520,128]{1,0:T(8,128)(2,1)S(1)} %get-tuple-element.25), channel_id=1, source_target_pairs={{0,4},{4,0},{8,12},{12,8},{16,20},{20,16},{24,28},{28,24},{1,5},{5... | collective-permute-start | bytes 399368 | tf_op jit(solution)/shard_map/ppermute | solution.py:31
  4.2 0.7 %collective-permute-start.1 = (bf16[520,128]{1,0:T(8,128)(2,1)S(1)}, bf16[520,128]{1,0:T(8,128)(2,1)S(1)}, u32[]{:S(2)}, u32[]{:S(2)}) collective-permute-start(bf16[520,128]{1,0:T(8,128)(2,1)S(1)} %get-tuple-element.26), channel_id=1, source_target_pairs={{4,8},{12,16},{20,24},{8,4},{16,12},{24,20},{5,9},{13,17},{21,25},... | collective-permute-start | bytes 399368 | tf_op jit(solution)/shard_map/ppermute | solution.py:32
  4.9 0.0 copy-start.2
  4.9 0.3 shard_map.83
  5.2 0.0 copy-start.1
  5.2 0.1 collective-permute-start.2
  5.3 0.8 %collective-permute-start.3 = (bf16[520,128]{1,0:T(8,128)(2,1)S(1)}, bf16[520,128]{1,0:T(8,128)(2,1)S(1)}, u32[]{:S(2)}, u32[]{:S(2)}) collective-permute-start(bf16[520,128]{1,0:T(8,128)(2,1)S(1)} %get-tuple-element.28), channel_id=1, source_target_pairs={{1,2},{2,1},{5,6},{6,5},{9,10},{10,9},{13,14},{14,13},{17,18},{18,... | collective-permute-start | bytes 399368 | tf_op jit(solution)/shard_map/ppermute | solution.py:32
  6.1 1.7 %collective-permute-done.x_even.refs_0_ = bf16[520,128]{1,0:T(8,128)(2,1)S(1)} collective-permute-done((bf16[520,128]{1,0:T(8,128)(2,1)S(1)}, bf16[520,128]{1,0:T(8,128)(2,1)S(1)}, u32[]{:S(2)}, u32[]{:S(2)}) %collective-permute-start) | collective-permute-done | bytes 133152 | tf_op jit(solution)/shard_map/ppermute | solution.py:31
  7.8 1.3 %collective-permute-start.4 = (bf16[272,128]{1,0:T(8,128)(2,1)S(1)}, bf16[272,128]{1,0:T(8,128)(2,1)S(1)}, u32[]{:S(2)}, u32[]{:S(2)}) collective-permute-start(bf16[272,128]{1,0:T(8,128)(2,1)S(1)} %get-tuple-element.31), channel_id=1, source_target_pairs={{0,1},{1,0},{2,3},{3,2},{4,5},{5,4},{6,7},{7,6},{8,9},{9,8},{10,11... | collective-permute-start | bytes 208904 | tf_op jit(solution)/shard_map/ppermute | solution.py:31
  9.1 0.7 %collective-permute-start.5 = (bf16[272,128]{1,0:T(8,128)(2,1)S(1)}, bf16[272,128]{1,0:T(8,128)(2,1)S(1)}, u32[]{:S(2)}, u32[]{:S(2)}) collective-permute-start(bf16[272,128]{1,0:T(8,128)(2,1)S(1)} %get-tuple-element.32), channel_id=1, source_target_pairs={{1,2},{2,1},{5,6},{6,5},{9,10},{10,9},{13,14},{14,13},{17,18},{18,... | collective-permute-start | bytes 208904 | tf_op jit(solution)/shard_map/ppermute | solution.py:32
  9.8 0.0 copy-start.3
  9.8 0.0 copy-start.4
  9.8 0.6 %copy-done.3 = f32[32]{0:T(128)S(1)} copy-done((f32[32]{0:T(128)S(1)}, f32[32]{0:T(128)}, u32[]{:S(2)}) %copy-start.3) | copy-done | bytes 152
  10.4 0.0 copy-done.4
  10.4 0.0 copy-done.5
  10.5 0.4 shard_map.84
  10.9 0.0 collective-permute-done.3.y_odd.refs_3_
  10.9 1.4 %shard_map.85 = (bf16[10,10,32,128]{3,2,1,0:T(8,128)(2,1)S(1)}, f32[2,32,128]{2,1,0:T(8,128)S(1)}) custom-call(bf16[8,8,32,128]{3,2,1,0:T(8,128)(2,1)S(1)} %get-tuple-element.24.own, f32[1,8,128]{2,1,0:T(8,128)S(1)} %get-tuple-element.23.masks, bf16[520,128]{1,0:T(8,128)(2,1)S(1)} %collective-permute-done.x_even.refs_0_, ...), custom_call_target="tpu_custom_call" | custom-call | bytes 1454080 | tf_op jit(solution)/shard_map/pallas_call | solution.py:40
  12.3 0.6 %shard_map.87 = (bf16[4,4,32,128]{3,2,1,0:T(8,128)(2,1)S(1)}, f32[3,3,8,128]{3,2,1,0:T(8,128)S(1)}, f32[32,128]{1,0:T(8,128)S(1)}) custom-call(bf16[8,8,32,128]{3,2,1,0:T(8,128)(2,1)S(1)} %get-tuple-element.24.own, f32[1,8,128]{2,1,0:T(8,128)S(1)} %get-tuple-element.23.masks, bf16[520,128]{1,0:T(8,128)(2,1)S(1)} %collective-permute-done.x_even.refs_0_, ...), custom_call_target="tpu_custom_call" | custom-call | bytes 1626112 | tf_op jit(solution)/shard_map/pallas_call | solution.py:40
  13.0 17.3 %all_to_all.22 = f32[32,1,128]{2,1,0:T(1,128)S(1)} all-to-all(f32[32,1,128]{2,1,0:T(1,128)S(1)} %bitcast.15), channel_id=1, replica_groups=mesh['region'=8,'strip'=4] {'region','strip'}, dimensions={0} | all-to-all | bytes 32768 | tf_op jit(solution)/shard_map/all_to_all | solution.py:512
  30.2 1.4 %shard_map.88 = (bf16[8,8,32,128]{3,2,1,0:T(8,128)(2,1)S(1)}, f32[32,128]{1,0:T(8,128)S(1)}) custom-call(bf16[10,10,32,128]{3,2,1,0:T(8,128)(2,1)S(1)} %get-tuple-element.30.refs_0_, bf16[4,4,32,128]{3,2,1,0:T(8,128)(2,1)S(1)} %get-tuple-element.34.refs_1_, f32[3,3,8,128]{3,2,1,0:T(8,128)S(1)} %get-tuple-element.35.refs_2_.wide_masks, ...), custom_call_target="tpu_custom_call" | custom-call | bytes 1462272 | tf_op jit(solution)/shard_map/pallas_call | solution.py:40
  31.6 8.9 %all_to_all.23 = f32[32,1,128]{2,1,0:T(1,128)S(1)} all-to-all(f32[32,1,128]{2,1,0:T(1,128)S(1)} %bitcast.16), channel_id=1, replica_groups=mesh['region'=8,'strip'=4] {'region','strip'}, dimensions={0} | all-to-all | bytes 32768 | tf_op jit(solution)/shard_map/all_to_all | solution.py:522
  40.5 1.2 %shard_map.89 = bf16[32,8,8,128]{3,2,1,0:T(8,128)(2,1)} custom-call(bf16[8,8,32,128]{3,2,1,0:T(8,128)(2,1)S(1)} %get-tuple-element.39.second_out, f32[3,3,8,128]{3,2,1,0:T(8,128)S(1)} %get-tuple-element.35.refs_2_.wide_masks, f32[32,128]{1,0:T(8,128)S(1)} %bitcast.14, f32[4,32,128]{2,1,0:T(8,128)S(1)} %get-tuple-element.37.refs_4_.params, ...), custom_call_target="tpu_custom_call" | custom-call | bytes 1167360 | tf_op jit(solution)/shard_map/pallas_call | solution.py:40
  (13 shorter events, 0.1 us)
Async XLA Ops:
  0.0 4.9 %copy-start = (bf16[32,8,8,128]{3,2,1,0:T(8,128)(2,1)S(1)}, bf16[32,8,8,128]{3,2,1,0:T(8,128)(2,1)}, u32[]{:S(2)}) copy-start(bf16[32,8,8,128]{3,2,1,0:T(8,128)(2,1)} %features.3) | copy-start | bytes 1572868
  1.2 6.6 %collective-permute-start = (bf16[520,128]{1,0:T(8,128)(2,1)S(1)}, bf16[520,128]{1,0:T(8,128)(2,1)S(1)}, u32[]{:S(2)}, u32[]{:S(2)}) collective-permute-start(bf16[520,128]{1,0:T(8,128)(2,1)S(1)} %get-tuple-element.25), channel_id=1, source_target_pairs={{0,4},{4,0},{8,12},{12,8},{16,20},{20,16},{24,28},{28,24},{1,5},{5... | collective-permute-start | bytes 399368 | tf_op jit(solution)/shard_map/ppermute | solution.py:31
  4.2 3.5 %collective-permute-start.1 = (bf16[520,128]{1,0:T(8,128)(2,1)S(1)}, bf16[520,128]{1,0:T(8,128)(2,1)S(1)}, u32[]{:S(2)}, u32[]{:S(2)}) collective-permute-start(bf16[520,128]{1,0:T(8,128)(2,1)S(1)} %get-tuple-element.26), channel_id=1, source_target_pairs={{4,8},{12,16},{20,24},{8,4},{16,12},{24,20},{5,9},{13,17},{21,25},... | collective-permute-start | bytes 399368 | tf_op jit(solution)/shard_map/ppermute | solution.py:32
  4.9 5.6 %copy-start.2 = (bf16[3,3,3,32,32]{4,3,2,1,0:T(8,128)(2,1)S(1)}, bf16[3,3,3,32,32]{4,3,2,1,0:T(8,128)(2,1)}, u32[]{:S(2)}) copy-start(bf16[3,3,3,32,32]{4,3,2,1,0:T(8,128)(2,1)} %weights_second.1) | copy-start | bytes 165892
  5.2 5.3 %copy-start.1 = (bf16[3,3,3,32,32]{4,3,2,1,0:T(8,128)(2,1)S(1)}, bf16[3,3,3,32,32]{4,3,2,1,0:T(8,128)(2,1)}, u32[]{:S(2)}) copy-start(bf16[3,3,3,32,32]{4,3,2,1,0:T(8,128)(2,1)} %weights_first.1) | copy-start | bytes 165892
  5.2 5.6 %collective-permute-start.2 = (bf16[520,128]{1,0:T(8,128)(2,1)S(1)}, bf16[520,128]{1,0:T(8,128)(2,1)S(1)}, u32[]{:S(2)}, u32[]{:S(2)}) collective-permute-start(bf16[520,128]{1,0:T(8,128)(2,1)S(1)} %get-tuple-element.27), channel_id=1, source_target_pairs={{0,1},{1,0},{2,3},{3,2},{4,5},{5,4},{6,7},{7,6},{8,9},{9,8},{10,11... | collective-permute-start | bytes 399368 | tf_op jit(solution)/shard_map/ppermute | solution.py:31
  5.3 5.6 %collective-permute-start.3 = (bf16[520,128]{1,0:T(8,128)(2,1)S(1)}, bf16[520,128]{1,0:T(8,128)(2,1)S(1)}, u32[]{:S(2)}, u32[]{:S(2)}) collective-permute-start(bf16[520,128]{1,0:T(8,128)(2,1)S(1)} %get-tuple-element.28), channel_id=1, source_target_pairs={{1,2},{2,1},{5,6},{6,5},{9,10},{10,9},{13,14},{14,13},{17,18},{18,... | collective-permute-start | bytes 399368 | tf_op jit(solution)/shard_map/ppermute | solution.py:32
  7.8 2.0 %copy-start.6 = (f32[32]{0:T(128)S(1)}, f32[32]{0:T(128)}, u32[]{:S(2)}) copy-start(f32[32]{0:T(128)} %param.12) | copy-start | bytes 388
  7.8 4.5 %collective-permute-start.4 = (bf16[272,128]{1,0:T(8,128)(2,1)S(1)}, bf16[272,128]{1,0:T(8,128)(2,1)S(1)}, u32[]{:S(2)}, u32[]{:S(2)}) collective-permute-start(bf16[272,128]{1,0:T(8,128)(2,1)S(1)} %get-tuple-element.31), channel_id=1, source_target_pairs={{0,1},{1,0},{2,3},{3,2},{4,5},{5,4},{6,7},{7,6},{8,9},{9,8},{10,11... | collective-permute-start | bytes 208904 | tf_op jit(solution)/shard_map/ppermute | solution.py:31
  9.1 3.2 %collective-permute-start.5 = (bf16[272,128]{1,0:T(8,128)(2,1)S(1)}, bf16[272,128]{1,0:T(8,128)(2,1)S(1)}, u32[]{:S(2)}, u32[]{:S(2)}) collective-permute-start(bf16[272,128]{1,0:T(8,128)(2,1)S(1)} %get-tuple-element.32), channel_id=1, source_target_pairs={{1,2},{2,1},{5,6},{6,5},{9,10},{10,9},{13,14},{14,13},{17,18},{18,... | collective-permute-start | bytes 208904 | tf_op jit(solution)/shard_map/ppermute | solution.py:32
  9.8 0.7 %copy-start.3 = (f32[32]{0:T(128)S(1)}, f32[32]{0:T(128)}, u32[]{:S(2)}) copy-start(f32[32]{0:T(128)} %param.15) | copy-start | bytes 388
  9.8 0.7 %copy-start.4 = (f32[32]{0:T(128)S(1)}, f32[32]{0:T(128)}, u32[]{:S(2)}) copy-start(f32[32]{0:T(128)} %param.14) | copy-start | bytes 388
  9.8 0.7 %copy-start.5 = (f32[32]{0:T(128)S(1)}, f32[32]{0:T(128)}, u32[]{:S(2)}) copy-start(f32[32]{0:T(128)} %param.13) | copy-start | bytes 388
